TPU v7x, 32 devices: a whole 2x2x4 slice. The times are simulated.
32 devices in a mesh: dp: 2 (over y), fsdp: 16 (over z, x, core).
Axes of the slice: x: 2, y: 2, z: 4, core: 2. Of those that a mesh axis runs over, the one named last changes fastest.
Arguments:
- hidden_in: bfloat16 [512, 128, 768], P(('dp', 'fsdp')), may hold values from -6 to 6
- segment_ids: int32 [512, 128], P(('dp', 'fsdp')), may hold values from 0 to 3, never falling along the last dimension, each value on 1 to 64 neighbouring positions
- pooled_grad: float32 [512, 4, 768], P(('dp', 'fsdp')), may hold values from -192 to 192
- qkv_weight: bfloat16 [768, 2304], P('fsdp'), may hold values from -0.21875 to 0.21875
- qv_bias: bfloat16 [1536], P('fsdp'), may hold values from -3 to 3
- out_weight: bfloat16 [768, 768], P('fsdp'), may hold values from -1.25 to 1.25
- out_bias: bfloat16 [768], P('fsdp'), may hold values from -3 to 3
- first_gain: bfloat16 [768], P('fsdp'), may hold values from 0.5 to 1.5
- first_shift: bfloat16 [768], P('fsdp'), may hold values from -3 to 3
- up_weight: bfloat16 [768, 3072], P('fsdp'), may hold values from -0.21875 to 0.21875
- up_bias: bfloat16 [3072], P('fsdp'), may hold values from -3 to 3
- down_weight: bfloat16 [3072, 768], P('fsdp'), may hold values from -0.109375 to 0.109375
- down_bias: bfloat16 [768], P('fsdp'), may hold values from -3 to 3
- second_gain: bfloat16 [768], P('fsdp'), may hold values from 0.5 to 1.5
- second_shift: bfloat16 [768], P('fsdp'), may hold values from -3 to 3
Outputs:
- pooled: float32 [512, 4, 768], P(('dp', 'fsdp'))
- grad_input: float32 [512, 128, 768], P(('dp', 'fsdp'))
- grad_qkv_weight: float32 [768, 2304], P('fsdp')
- grad_qv_bias: float32 [1536], P('fsdp')
- grad_out_weight: float32 [768, 768], P('fsdp')
- grad_out_bias: float32 [768], P('fsdp')
- grad_first_gain: float32 [768], P('fsdp')
- grad_first_shift: float32 [768], P('fsdp')
- grad_up_weight: float32 [768, 3072], P('fsdp')
- grad_up_bias: float32 [3072], P('fsdp')
- grad_down_weight: float32 [3072, 768], P('fsdp')
- grad_down_bias: float32 [768], P('fsdp')
- grad_second_gain: float32 [768], P('fsdp')
- grad_second_shift: float32 [768], P('fsdp')
Inputs may be any that keep to these rules, and one draw needn't show every extreme that they name: `segment_ids`: within each row of 128 positions the ids never fall, every id occurs, and the longest segment has exactly 64 positions.
All inputs are finite; a program needn't handle non-finite values.
Results may differ from a plain program's by a relative error of at most 0.0065.
Values may be sent and summed in bfloat16 or wider, within the bound.
No kernel may reach another device: no remote copies, remote signals or barrier semaphores. Data moves between devices by JAX's collectives and lax.ppermute only.
A program may use at most 256 MiB of HBM per device.

v0:
```python
import math

import jax
import jax.numpy as jnp
from jax import lax
from jax.sharding import PartitionSpec as P

HEAD = 64


EPSILON = 1e-12
HIGHEST = lax.Precision.HIGHEST


def norm_rows(residual, norm_gain, norm_shift):
    average = jnp.mean(residual, axis=-1, keepdims=True)
    centred = residual - average
    variance = jnp.mean(centred * centred, axis=-1, keepdims=True)
    return centred * lax.rsqrt(variance + EPSILON) * norm_gain + norm_shift


def norm_scaled(residual, norm_gain):
    return norm_rows(residual, norm_gain, 0.0)


def gelu_exact(inputs_pre):
    return jax.nn.gelu(inputs_pre, approximate=False)


def product(left_side, right_side):
    return jnp.dot(left_side, right_side, preferred_element_type=jnp.float32)


def times_transpose(left_side, right_side):
    return lax.dot_general(
        left_side, right_side, (((1,), (1,)), ((), ())), preferred_element_type=jnp.float32
    )


def transpose_times(left_side, right_side):
    return lax.dot_general(
        left_side, right_side, (((0,), (0,)), ((), ())), preferred_element_type=jnp.float32
    )


def column_sum(matrix):
    return jnp.sum(matrix.astype(jnp.float32), axis=0)


def masked_scores(queries, key_rows, same_segment, score_scale):
    scores = (
        jnp.einsum("bqhd,bkhd->bhqk", queries, key_rows, preferred_element_type=jnp.float32)
        * score_scale
    )
    return jnp.where(same_segment[:, None], scores, -1e30)


def body(
    hidden_in,
    segment_ids,
    pooled_grad,
    qkv_weight,
    qv_bias,
    out_weight,
    out_bias,
    first_gain,
    first_shift,
    up_weight,
    up_bias,
    down_weight,
    down_bias,
    second_gain,
    second_shift,
):
    row_count, length, model_width = hidden_in.shape
    head_count = model_width // HEAD
    token_count = row_count * length
    score_scale = 1.0 / math.sqrt(HEAD)
    flat_in = hidden_in.reshape(token_count, model_width)
    same_segment = segment_ids[:, :, None] == segment_ids[:, None, :]
    segment_total = pooled_grad.shape[1]
    member = (
        segment_ids[:, :, None] == jnp.arange(segment_total, dtype=jnp.int32)[None, None, :]
    ).astype(jnp.float32)
    population = jnp.sum(member, axis=1)
    attention_set = (
        lax.all_gather(qkv_weight, "fsdp", axis=0, tiled=True),
        lax.all_gather(qv_bias, "fsdp", axis=0, tiled=True),
        lax.all_gather(out_weight, "fsdp", axis=0, tiled=True),
        lax.all_gather(out_bias, "fsdp", axis=0, tiled=True),
        lax.all_gather(first_gain, "fsdp", axis=0, tiled=True),
        lax.all_gather(first_shift, "fsdp", axis=0, tiled=True),
    )
    qkv_matrix, query_value_bias, output_matrix, output_bias, gain_one, shift_one = attention_set
    zero_bias = jnp.zeros((model_width,), jnp.float32)
    joined_bias = jnp.concatenate(
        [
            query_value_bias[:model_width].astype(jnp.float32),
            zero_bias,
            query_value_bias[model_width:].astype(jnp.float32),
        ]
    )
    qkv_low = (product(flat_in, qkv_matrix) + joined_bias).astype(jnp.bfloat16)
    qkv_heads = qkv_low.reshape(row_count, length, 3, head_count, HEAD)
    queries = qkv_heads[:, :, 0]
    key_rows = qkv_heads[:, :, 1]
    value_rows = qkv_heads[:, :, 2]
    masked = masked_scores(queries, key_rows, same_segment, score_scale)
    row_peak = jnp.max(masked, axis=-1, keepdims=True)
    log_total = row_peak + jnp.log(jnp.sum(jnp.exp(masked - row_peak), axis=-1, keepdims=True))
    attention_low = jnp.exp(masked - log_total).astype(jnp.bfloat16)
    context = jnp.einsum(
        "bhqk,bkhd->bqhd", attention_low, value_rows, preferred_element_type=jnp.float32
    )
    context_low = context.astype(jnp.bfloat16).reshape(token_count, model_width)
    first_sum = (
        flat_in.astype(jnp.float32)
        + product(context_low, output_matrix)
        + output_bias.astype(jnp.float32)
    )
    normed_one = norm_rows(first_sum, gain_one.astype(jnp.float32), shift_one.astype(jnp.float32))
    normed_low = normed_one.astype(jnp.bfloat16)
    feedforward_set = (
        lax.all_gather(up_weight, "fsdp", axis=0, tiled=True),
        lax.all_gather(up_bias, "fsdp", axis=0, tiled=True),
        lax.all_gather(down_weight, "fsdp", axis=0, tiled=True),
        lax.all_gather(down_bias, "fsdp", axis=0, tiled=True),
        lax.all_gather(second_gain, "fsdp", axis=0, tiled=True),
        lax.all_gather(second_shift, "fsdp", axis=0, tiled=True),
    )
    up_matrix, up_vector, down_matrix, down_vector, gain_two, shift_two = feedforward_set
    hidden_pre = product(normed_low, up_matrix) + up_vector.astype(jnp.float32)
    active_low = gelu_exact(hidden_pre).astype(jnp.bfloat16)
    second_sum = normed_one + product(active_low, down_matrix) + down_vector.astype(jnp.float32)
    final_rows = norm_rows(second_sum, gain_two.astype(jnp.float32), shift_two.astype(jnp.float32))
    final_rows = final_rows.reshape(row_count, length, model_width)
    pooled = (
        jnp.einsum("bts,btd->bsd", member, final_rows, precision=HIGHEST) / population[:, :, None]
    )
    attention_again = (
        lax.all_gather(qkv_weight, "fsdp", axis=0, tiled=True),
        lax.all_gather(out_weight, "fsdp", axis=0, tiled=True),
        lax.all_gather(first_gain, "fsdp", axis=0, tiled=True),
    )
    feedforward_again = (
        lax.all_gather(up_weight, "fsdp", axis=0, tiled=True),
        lax.all_gather(down_weight, "fsdp", axis=0, tiled=True),
        lax.all_gather(second_gain, "fsdp", axis=0, tiled=True),
    )
    qkv_back, output_back, gain_one_back = attention_again
    up_back, down_back, gain_two_back = feedforward_again
    token_grad = jnp.einsum(
        "bts,bsd->btd", member, pooled_grad / population[:, :, None], precision=HIGHEST
    )
    token_grad = token_grad.reshape(token_count, model_width)
    unused_second, second_back = jax.vjp(norm_scaled, second_sum, gain_two_back.astype(jnp.float32))
    second_grad, grad_gain_two = second_back(token_grad)
    grad_shift_two = jnp.sum(token_grad, axis=0)
    branch_grad = second_grad.astype(jnp.bfloat16)
    grad_down = transpose_times(active_low, branch_grad)
    grad_down_vector = column_sum(branch_grad)
    unused_active, gelu_back = jax.vjp(gelu_exact, hidden_pre)
    (hidden_full,) = gelu_back(times_transpose(branch_grad, down_back))
    hidden_grad = hidden_full.astype(jnp.bfloat16)
    grad_up = transpose_times(normed_low, hidden_grad)
    grad_up_vector = column_sum(hidden_grad)
    normed_grad = second_grad + times_transpose(hidden_grad, up_back)
    unused_first, first_back = jax.vjp(norm_scaled, first_sum, gain_one_back.astype(jnp.float32))
    first_grad, grad_gain_one = first_back(normed_grad)
    grad_shift_one = jnp.sum(normed_grad, axis=0)
    attended_grad = first_grad.astype(jnp.bfloat16)
    grad_output = transpose_times(context_low, attended_grad)
    grad_output_vector = column_sum(attended_grad)
    context_grad = times_transpose(attended_grad, output_back).astype(jnp.bfloat16)
    context_grad = context_grad.reshape(row_count, length, head_count, HEAD)
    again_masked = masked_scores(queries, key_rows, same_segment, score_scale)
    attention_again_rows = jnp.exp(again_masked - log_total)
    attention_again_low = attention_again_rows.astype(jnp.bfloat16)
    probs_grad = jnp.einsum(
        "bqhd,bkhd->bhqk", context_grad, value_rows, preferred_element_type=jnp.float32
    )
    values_grad = jnp.einsum(
        "bhqk,bqhd->bkhd", attention_again_low, context_grad, preferred_element_type=jnp.float32
    )
    inner_total = jnp.sum(attention_again_rows * probs_grad, axis=-1, keepdims=True)
    scores_grad = (attention_again_rows * (probs_grad - inner_total)).astype(jnp.bfloat16)
    queries_grad = (
        jnp.einsum("bhqk,bkhd->bqhd", scores_grad, key_rows, preferred_element_type=jnp.float32)
        * score_scale
    )
    keys_grad = (
        jnp.einsum("bhqk,bqhd->bkhd", scores_grad, queries, preferred_element_type=jnp.float32)
        * score_scale
    )
    qkv_grad = jnp.stack([queries_grad, keys_grad, values_grad], axis=2).astype(jnp.bfloat16)
    qkv_grad = qkv_grad.reshape(token_count, 3 * model_width)
    grad_qkv = transpose_times(flat_in, qkv_grad)
    grad_query_value = jnp.concatenate(
        [column_sum(qkv_grad[:, :model_width]), column_sum(qkv_grad[:, 2 * model_width :])]
    )
    grad_input = first_grad + times_transpose(qkv_grad, qkv_back)
    feedforward_parts = (
        lax.psum_scatter(grad_up, "fsdp", scatter_dimension=0, tiled=True),
        lax.psum_scatter(grad_up_vector, "fsdp", scatter_dimension=0, tiled=True),
        lax.psum_scatter(grad_down, "fsdp", scatter_dimension=0, tiled=True),
        lax.psum_scatter(grad_down_vector, "fsdp", scatter_dimension=0, tiled=True),
        lax.psum_scatter(grad_gain_two, "fsdp", scatter_dimension=0, tiled=True),
        lax.psum_scatter(grad_shift_two, "fsdp", scatter_dimension=0, tiled=True),
    )
    attention_parts = (
        lax.psum_scatter(grad_qkv, "fsdp", scatter_dimension=0, tiled=True),
        lax.psum_scatter(grad_query_value, "fsdp", scatter_dimension=0, tiled=True),
        lax.psum_scatter(grad_output, "fsdp", scatter_dimension=0, tiled=True),
        lax.psum_scatter(grad_output_vector, "fsdp", scatter_dimension=0, tiled=True),
        lax.psum_scatter(grad_gain_one, "fsdp", scatter_dimension=0, tiled=True),
        lax.psum_scatter(grad_shift_one, "fsdp", scatter_dimension=0, tiled=True),
    )
    totals = lax.psum(
        (
            attention_parts[0],
            attention_parts[1],
            attention_parts[2],
            attention_parts[3],
            attention_parts[4],
            attention_parts[5],
            feedforward_parts[0],
            feedforward_parts[1],
            feedforward_parts[2],
            feedforward_parts[3],
            feedforward_parts[4],
            feedforward_parts[5],
        ),
        "dp",
    )
    return (
        pooled,
        grad_input.reshape(row_count, length, model_width),
        totals[0],
        totals[1],
        totals[2],
        totals[3],
        totals[4],
        totals[5],
        totals[6],
        totals[7],
        totals[8],
        totals[9],
        totals[10],
        totals[11],
    )


def solution(mesh):
    in_specs = (
        P(("dp", "fsdp"), None, None),
        P(("dp", "fsdp"), None),
        P(("dp", "fsdp"), None, None),
        P("fsdp", None),
        P("fsdp"),
        P("fsdp", None),
        P("fsdp"),
        P("fsdp"),
        P("fsdp"),
        P("fsdp", None),
        P("fsdp"),
        P("fsdp", None),
        P("fsdp"),
        P("fsdp"),
        P("fsdp"),
    )
    out_specs = (
        P(("dp", "fsdp"), None, None),
        P(("dp", "fsdp"), None, None),
        P("fsdp", None),
        P("fsdp"),
        P("fsdp", None),
        P("fsdp"),
        P("fsdp"),
        P("fsdp"),
        P("fsdp", None),
        P("fsdp"),
        P("fsdp", None),
        P("fsdp"),
        P("fsdp"),
        P("fsdp"),
    )
    return jax.shard_map(body, mesh=mesh, in_specs=in_specs, out_specs=out_specs, check_vma=False)
```

profile of v0, /device:TPU:0, one launch (start us, length us, event | category | flops | bytes accessed | tf_op | source)
XLA Modules:
  0.0 907.2 jit_solution(1191663198079244398)
XLA Ops:
  22.0 64.3 %all-reduce.19 = (bf16[768]{0:T(1024)(128)(2,1)S(1)}, bf16[1536]{0:T(1024)(128)(2,1)S(1)}, bf16[768]{0:T(1024)(128)(2,1)S(1)}, bf16[768]{0:T(1024)(128)(2,1)S(1)...) all-reduce(bf16[768]{0:T(1024)(128)(2,1)S(1)} %dynamic-update-slice, ...), channel_id=1, replica_groups=mesh['dp'=2,'fsdp'=16] {'fsdp'}, use_global_device_ids=true, to_apply=%add.1 | all-reduce | flops 9216 | bytes 36864
  88.1 7.1 fusion.46
  95.2 12.4 %add_convert_fusion.1 = bf16[2048,2304]{1,0:T(8,128)(2,1)} fusion(bf16[2048,768]{1,0:T(8,128)(2,1)} %bitcast.124, bf16[768,2304]{1,0:T(8,128)(2,1)} %all-gather.5.cloned.1.call-done, f32[2304]{0:T(1024)S(1)} %pad_maximum_fusion), kind=kOutput, calls=%fused_computation.19 | convolution fusion | flops 7257194496 | bytes 16131072 | tf_op jit(solution)/shard_map/dot_general | solution.py:31
  107.6 12.7 %copy.53 = bf16[2048,2304]{0,1:T(8,128)(2,1)} copy(bf16[2048,2304]{1,0:T(8,128)(2,1)} %add_convert_fusion.1) | data formatting | bytes 18874368 | tf_op jit(solution)/shard_map/convert_element_type | solution.py:103
  120.3 11.0 %copy.76 = bf16[288,8,16,128]{3,2,1,0:T(8,128)(2,1)} copy(bf16[288,8,16,128]{3,1,2,0:T(8,128)(2,1)} %bitcast.116) | data formatting | bytes 18874368
  131.3 6.2 fusion.42
  137.5 6.3 fusion.6
  143.9 4.0 exponential_reduce_fusion
  148.4 7.1 convert_bitcast_fusion
  155.5 4.3 copy.58
  159.8 7.3 fusion.44
  167.2 2.7 copy-done.2
  171.3 70.3 %multiply_convert_fusion = (bf16[2048,3072]{1,0:T(8,128)(2,1)}, f32[2048,3072]{1,0:T(8,128)}, f32[2048,3072]{1,0:T(8,128)}) fusion(f32[3072]{0:T(1024)S(1)} %convert_element_type.109, bf16[768,3072]{1,0:T(8,128)(2,1)} %all-gather.9.cloned.1.call-done, f32[2048,768]{1,0:T(8,128)} %copy-done.2, f32[768]{0:T(1024)S(1)} %convert_element_type.107, ...), kind=kOutput, calls=%fused_computation.4 | convolution fusion | flops 10086776832 | bytes 73959424 | tf_op jit(solution)/shard_map/dot_general | solution.py:31
  241.7 16.4 %fusion.45 = (f32[2048]{0:T(1024)S(1)}, f32[2048,768]{1,0:T(8,128)S(1)}) fusion(f32[768]{0:T(1024)S(1)} %copy-done.36, bf16[2048,3072]{1,0:T(8,128)(2,1)} %get-tuple-element.99, bf16[3072,768]{1,0:T(8,128)(2,1)} %all-gather.11.cloned.1.call-done, f32[768]{0:T(1024)S(1)} %convert_element_type.107, f32[768]{0:T(1024)S(1)} %convert_element_type.106, ...), kind=kOutput, calls=%fused_computation.104 | convolution fusion | flops 9674684416 | bytes 29918208 | tf_op jit(solution)/shard_map/dot_general | solution.py:31
  259.1 3.2 fusion.8
  262.3 4.7 fusion.40
  267.0 2.6 copy-done.3
  270.8 29.1 %convert_reduce_fusion = (f32[3072]{0:T(1024)}, bf16[2048,3072]{1,0:T(8,128)(2,1)}) fusion(f32[2048,3072]{1,0:T(8,128)} %get-tuple-element.100, bf16[2048,768]{1,0:T(8,128)(2,1)S(1)} %get-tuple-element.92, bf16[3072,768]{1,0:T(8,128)(2,1)} %all-gather.11.cloned.1.call-done, f32[2048,3072]{1,0:T(8,128)} %get-tuple-element.113, f32[3072]{0:T(1024)S(1)} %convert_element_type.109), kind=kOutput, calls=%fused_computation.2 | convolution fusion | flops 9770628096 | bytes 70803456 | tf_op jit(solution)/shard_map/dot_general | solution.py:35
  299.9 19.2 %multiply_reduce_fusion.1 = (f32[768]{0:T(1024)}, f32[2048]{0:T(1024)S(1)}, f32[768]{0:T(1024)}, f32[2048,768]{1,0:T(8,128)S(1)}) fusion(f32[2048,768]{1,0:T(8,128)} %copy-done.2, f32[2048]{0:T(1024)S(1)} %fusion.31, f32[2048]{0:T(1024)S(1)} %broadcast_multiply_fusion.1, f32[768]{0:T(1024)S(1)} %convert_element_type.106, ...), kind=kOutput, calls=%fused_computation.34 | convolution fusion | flops 9679400960 | bytes 36217856 | tf_op jit(solution)/shard_map/dot_general | solution.py:35
  319.1 4.2 fusion.39
  323.4 2.6 copy-done.1
  328.9 4.0 convolution_convert_fusion
  332.9 3.4 copy.59
  339.0 10.6 %fusion.23 = bf16[16,128,1,12,64]{1,4,3,0,2:T(8,128)(2,1)} fusion(bf16[16,128,12,64]{1,0,3,2:T(8,128)(2,1)S(1)} %bitcast.120, f32[16,12,128,128]{2,3,1,0:T(8,128)} %copy-done, f32[16,12,128]{2,1,0:T(8,128)S(1)} %copy-done.17, pred[16,128,128]{1,2,0:T(8,128)(4,1)S(1)} %copy-done.10), kind=kOutput, calls=%fused_computation.72 | convolution fusion | flops 415236096 | bytes 19234816 | tf_op jit(solution)/shard_map/bhqk,bqhd->bkhd/dot_general | solution.py:182
  349.6 10.9 %multiply_reduce_fusion = (f32[16,12,128]{2,1,0:T(8,128)S(1)}, f32[16,12,128,128]{2,3,1,0:T(8,128)}) fusion(f32[16,12,128,128]{2,3,1,0:T(8,128)} %copy-done, f32[16,12,128]{2,1,0:T(8,128)S(1)} %copy-done.17, pred[16,128,128]{1,2,0:T(8,128)(4,1)S(1)} %copy-done.10, bf16[16,128,1,12,64]{1,0,4,3,2:T(8,128)(2,1)S(1)} %copy-done.7, ...), kind=kOutput, calls=%fused_computation.21 | convolution fusion | flops 418357248 | bytes 31916032 | tf_op jit(solution)/shard_map/bqhd,bkhd->bhqk/dot_general | solution.py:179
  360.5 10.6 %multiply_convert_fusion.1 = bf16[16,12,128,128]{2,3,1,0:T(8,128)(2,1)S(1)} fusion(f32[16,12,128,128]{2,3,1,0:T(8,128)} %get-tuple-element.118, f32[16,12,128,128]{2,3,1,0:T(8,128)} %copy-done, f32[16,12,128]{2,1,0:T(8,128)S(1)} %get-tuple-element.117, f32[16,12,128]{2,1,0:T(8,128)S(1)} %copy-done.17, pred[16,128,128]{1,2,0:T(8,128)(4,1)S(1)} %copy-done.10), kind=kLoop, calls=%fused_computation.20 | loop fusion | flops 18874368 | bytes 31916032 | tf_op jit(solution)/shard_map/convert_element_type | solution.py:186
  371.1 5.7 multiply_bitcast_fusion
  376.8 2.2 multiply_bitcast_fusion.1
  379.0 7.3 maximum_convert_fusion
  386.3 26.1 %copy.65 = bf16[16,128,3,12,64]{1,0,4,3,2:T(8,128)(2,1)} copy(bf16[16,128,3,12,64]{1,4,3,0,2:T(8,128)(2,1)} %maximum_convert_fusion) | data formatting | bytes 18874368 | tf_op jit(solution)/shard_map/convert_element_type | solution.py:195
  412.3 13.0 %convolution_bitcast_fusion = f32[768,2304]{0,1:T(8,128)} fusion(bf16[2048,768]{1,0:T(8,128)(2,1)S(1)} %bitcast.126, bf16[288,8,16,128]{3,2,1,0:T(8,128)(2,1)} %bitcast.112), kind=kOutput, calls=%fused_computation.52 | convolution fusion | flops 7247757312 | bytes 19660800 | tf_op jit(solution)/shard_map/dot_general | solution.py:41
  425.3 8.0 copy.71
  435.2 6.3 fusion.10
  441.6 19.2 %fusion.35 = f32[768,3072]{1,0:T(8,128)} fusion(bf16[2048,3072]{1,0:T(8,128)(2,1)} %get-tuple-element.120, f32[2048,768]{1,0:T(8,128)} %copy-done.2, f32[768]{0:T(1024)S(1)} %copy-done.35, f32[768]{0:T(1024)S(1)} %copy-done.32, f32[2048]{0:T(1024)S(1)} %copy-done.25, f32[2048]{0:T(1024)S(1)} %broadcast_multiply_fusion.1), kind=kOutput, calls=%fused_computation.97 | convolution fusion | flops 9671540736 | bytes 28334080 | tf_op jit(solution)/shard_map/dot_general | solution.py:41
  461.3 2.2 copy-done.12
  463.6 15.4 %fusion.47 = f32[3072,768]{1,0:T(8,128)} fusion(bf16[2048,3072]{1,0:T(8,128)(2,1)} %get-tuple-element.99, bf16[2048,768]{1,0:T(8,128)(2,1)S(1)} %copy-done.12), kind=kOutput, calls=%fused_computation.106 | convolution fusion | flops 9663676416 | bytes 25165824 | tf_op jit(solution)/shard_map/dot_general | solution.py:41
  481.0 12.2 %copy.122 = bf16[288,8,16,128]{3,1,2,0:T(8,128)(2,1)} copy(bf16[288,8,16,128]{3,2,1,0:T(8,128)(2,1)} %bitcast.113) | data formatting | bytes 18874368
  493.2 3.8 convert_reduce_fusion.4
  497.1 59.1 %all-reduce.16 = (f32[1536]{0:T(1024)S(1)}, f32[768]{0:T(1024)S(1)}, f32[768]{0:T(1024)S(1)}, f32[768]{0:T(1024)S(1)}, f32[3072]{0:T(1024)S(1)}, /*index=5*/f32[...) all-reduce(f32[1536]{0:T(1024)S(1)} %pad_maximum_fusion.1, ...), channel_id=3, replica_groups=mesh['dp'=2,'fsdp'=16] {'fsdp'}, use_global_device_ids=true, to_apply=%region_16.17.clone | all-reduce | flops 9216 | bytes 73728
  556.8 5.5 all-reduce.17
  562.3 5.7 convolution_divide_fusion
  568.0 2.4 copy.72
  570.4 17.3 %reduce-scatter.7.cloned.1.call-done = f32[48,768]{1,0:T(8,128)} async-done(((f32[768,768]{1,0:T(8,128)}), f32[48,768]{1,0:T(8,128)}) %reduce-scatter.7.cloned.1.call-update) | async-done | bytes 147472 | tf_op jit(solution)/shard_map/reduce_scatter | solution.py:213
  587.7 114.5 %reduce-scatter.9.cloned.1.call-done = f32[48,3072]{1,0:T(8,128)} async-done(((f32[768,3072]{1,0:T(8,128)}), f32[48,3072]{1,0:T(8,128)}) %reduce-scatter.9.cloned.1.call-update) | async-done | bytes 589840 | tf_op jit(solution)/shard_map/reduce_scatter | solution.py:203
  702.2 115.8 %reduce-scatter.11.cloned.1.call-done = f32[192,768]{1,0:T(8,128)} async-done(((f32[3072,768]{1,0:T(8,128)}), f32[192,768]{1,0:T(8,128)}) %reduce-scatter.11.cloned.1.call-update) | async-done | bytes 589840 | tf_op jit(solution)/shard_map/reduce_scatter | solution.py:205
  818.1 14.5 %add_add_fusion.4 = f32[2048,768]{1,0:T(8,128)} fusion(f32[2048,768]{1,0:T(8,128)} %copy-done.1, bf16[768,2304]{1,0:T(8,128)(2,1)} %all-gather.5.cloned.1.call-done, f32[2048]{0:T(1024)S(1)} %negate_multiply_fusion.1, bf16[288,8,16,128]{3,2,1,0:T(8,128)(2,1)} %bitcast.114), kind=kOutput, calls=%fused_computation.48 | convolution fusion | flops 7250903040 | bytes 25567232 | tf_op jit(solution)/shard_map/dot_general | solution.py:35
  832.5 60.1 %all-reduce.22.cloned.1.call-done = (f32[48,2304]{0,1:T(8,128)}, f32[48,768]{1,0:T(8,128)}, f32[48,3072]{1,0:T(8,128)}, f32[192,768]{1,0:T(8,128)}) async-done(((f32[48,2304]{0,1:T(8,128)}, f32[48,768]{1,0:T(8,128)}, f32[48,3072]{1,0:T(8,128)}, f32[192,768]{1,0:T(8,128)}), (f32[48,2304]{0,1:T(8,128)}, f32[48,768]{1,0:T(8,128)}, f32[48,3072]{1,0:T(8,128)}, ...) | async-done | bytes 1769488 | tf_op jit(solution)/shard_map/psum | solution.py:218
  892.7 2.4 copy.66
  (161 shorter events, 32.8 us)
Async XLA Ops:
  7.2 88.0 %all-gather.5.cloned.1.call-start = ((), (), s32[]{:S(2)}) async-start(), calls=%async_computation.4 | async-start | bytes 3760128 | tf_op jit(solution)/shard_map/all_gather | solution.py:87
  7.9 151.9 %all-gather.7.cloned.1.call-start = ((), (), s32[]{:S(2)}) async-start(), calls=%async_computation.5 | async-start | bytes 1253376 | tf_op jit(solution)/shard_map/all_gather | solution.py:89
  8.7 162.6 %all-gather.9.cloned.1.call-start = ((), (), s32[]{:S(2)}) async-start(), calls=%async_computation.6 | async-start | bytes 5013504 | tf_op jit(solution)/shard_map/all_gather | solution.py:124
  9.4 232.2 %all-gather.11.cloned.1.call-start = ((), (), s32[]{:S(2)}) async-start(), calls=%async_computation.7 | async-start | bytes 5013504 | tf_op jit(solution)/shard_map/all_gather | solution.py:126
  10.0 558.0 %reduce-scatter.13.cloned.1.call-start = ((), (), s32[]{:S(2)}) async-start(), calls=%async_computation.11 | async-start | bytes 7520256
  10.8 96.8 %copy-start.19 = (f32[16,4]{1,0:T(8,128)}, f32[16,4]{1,0:T(8,128)S(1)}, u32[]{:S(2)}) copy-start(f32[16,4]{1,0:T(8,128)S(1)} %convert_reduce_fusion.5) | copy-start | bytes 772
  12.0 136.0 %copy-start.9 = (pred[16,128,128]{1,2,0:T(8,128)(4,1)}, pred[16,128,128]{1,2,0:T(8,128)(4,1)S(1)}, u32[]{:S(2)}) copy-start(pred[16,128,128]{1,2,0:T(8,128)(4,1)S(1)} %broadcast_compare_fusion) | copy-start | bytes 786436
  86.9 154.7 %copy-start.34 = (f32[768]{0:T(1024)}, f32[768]{0:T(1024)S(1)}, u32[]{:S(2)}) copy-start(f32[768]{0:T(1024)S(1)} %convert_element_type.107) | copy-start | bytes 9220
  86.9 232.1 %copy-start.31 = (f32[768]{0:T(1024)}, f32[768]{0:T(1024)S(1)}, u32[]{:S(2)}) copy-start(f32[768]{0:T(1024)S(1)} %convert_element_type.106) | copy-start | bytes 9220
  137.5 6.3 copy-start.4
  143.8 4.5 copy-start
  147.9 7.5 copy-start.16
  159.8 7.4 copy-start.15
  167.1 2.7 copy-start.2
  171.3 147.8 %copy-start.24 = (f32[2048]{0:T(1024)}, f32[2048]{0:T(1024)S(1)}, u32[]{:S(2)}) copy-start(f32[2048]{0:T(1024)S(1)} %fusion.31) | copy-start | bytes 24580
  171.3 70.3 %copy-start.36 = (f32[768]{0:T(1024)S(1)}, f32[768]{0:T(1024)}, u32[]{:S(2)}) copy-start(f32[768]{0:T(1024)} %convert_element_type.111) | copy-start | bytes 9220
  241.6 17.4 %slice-start = ((s8[6291456]{0:T(1024)(128)(4,1)}), s8[4194304]{0:T(1024)(128)(4,1)S(1)}, s32[]{:S(2)}) async-start(s8[6291456]{0:T(1024)(128)(4,1)} %bitcast.110), calls=%async_computation.13 | async-start | bytes 8388608
  241.7 17.4 %slice-start.1 = ((s8[6291456]{0:T(1024)(128)(4,1)}), s8[2097152]{0:T(1024)(128)(4,1)S(1)}, s32[]{:S(2)}) async-start(s8[6291456]{0:T(1024)(128)(4,1)} %bitcast.110), calls=%async_computation.14 | async-start | bytes 4194304
  259.1 3.2 copy-start.28
  267.0 2.6 copy-start.3
  270.8 29.1 %copy-start.11 = (bf16[2048,768]{1,0:T(8,128)(2,1)}, bf16[2048,768]{1,0:T(8,128)(2,1)S(1)}, u32[]{:S(2)}) copy-start(bf16[2048,768]{1,0:T(8,128)(2,1)S(1)} %get-tuple-element.92) | copy-start | bytes 9437188
  299.9 19.2 %copy-start.22 = (f32[2048]{0:T(1024)S(1)}, f32[2048]{0:T(1024)}, u32[]{:S(2)}) copy-start(f32[2048]{0:T(1024)} %copy-done.21) | copy-start | bytes 24580
  323.3 2.6 copy-start.1
  323.3 5.5 copy-start.40
  332.9 6.1 copy-start.10
  332.9 6.1 copy-start.17
  339.0 10.6 %copy-start.7 = (bf16[16,128,1,12,64]{1,0,4,3,2:T(8,128)(2,1)S(1)}, bf16[16,128,1,12,64]{1,0,4,3,2:T(8,128)(2,1)}, u32[]{:S(2)}) copy-start(bf16[16,128,1,12,64]{1,0,4,3,2:T(8,128)(2,1)} %get-tuple-element.103) | copy-start | bytes 9437188
  360.5 10.6 %copy-start.6 = (bf16[16,128,1,12,64]{1,0,4,3,2:T(8,128)(2,1)S(1)}, bf16[16,128,1,12,64]{1,0,4,3,2:T(8,128)(2,1)}, u32[]{:S(2)}) copy-start(bf16[16,128,1,12,64]{1,0,4,3,2:T(8,128)(2,1)} %get-tuple-element.102) | copy-start | bytes 9437188
  371.0 5.7 copy-start.5
  386.3 26.1 %copy-start.39 = (bf16[16,128,768]{2,1,0:T(8,128)(2,1)S(1)}, bf16[16,128,768]{2,1,0:T(8,128)(2,1)}, u32[]{:S(2)}) copy-start(bf16[16,128,768]{2,1,0:T(8,128)(2,1)} %param.15) | copy-start | bytes 9437188
  433.3 1.9 copy-start.14
  433.4 8.2 copy-start.25
  433.4 8.2 copy-start.32
  433.4 8.2 copy-start.35
  433.4 154.3 %reduce-scatter.7.cloned.1.call-start = ((), (), s32[]{:S(2)}) async-start(), calls=%async_computation.8 | async-start | bytes 2506752 | tf_op jit(solution)/shard_map/reduce_scatter | solution.py:213
  441.5 260.7 %reduce-scatter.9.cloned.1.call-start = ((), (), s32[]{:S(2)}) async-start(), calls=%async_computation.9 | async-start | bytes 10027008 | tf_op jit(solution)/shard_map/reduce_scatter | solution.py:203
  460.8 2.7 copy-start.12
  460.9 357.2 %reduce-scatter.11.cloned.1.call-start = ((), (), s32[]{:S(2)}) async-start(), calls=%async_computation.10 | async-start | bytes 10027008 | tf_op jit(solution)/shard_map/reduce_scatter | solution.py:205
  479.0 413.7 %all-reduce.22.cloned.1.call-start = ((), (), s32[]{:S(2)}) async-start(), calls=%async_computation.12 | async-start | bytes 5013504 | tf_op jit(solution)/shard_map/psum | solution.py:218
  493.1 3.9 copy-start.26
  493.1 3.9 copy-start.27
  493.1 3.9 copy-start.29
  493.1 3.9 copy-start.30
  493.1 3.9 copy-start.33
  493.1 3.9 copy-start.37
  493.1 3.9 copy-start.38
  493.2 69.2 %copy-start.18 = (s32[16,128]{1,0:T(8,128)S(1)}, s32[16,128]{1,0:T(8,128)}, u32[]{:S(2)}) copy-start(s32[16,128]{1,0:T(8,128)} %param.16) | copy-start | bytes 24580
  493.2 69.2 %copy-start.20 = (f32[16,4]{1,0:T(8,128)S(1)}, f32[16,4]{1,0:T(8,128)}, u32[]{:S(2)}) copy-start(f32[16,4]{1,0:T(8,128)} %copy-done.19) | copy-start | bytes 772
  (4 other events, 4.9 us)
Sparse Core Ops, SparseCore 0:
  10.3 50.0 all-gather.4
  62.7 37.3 all-gather.6
  102.3 52.1 all-gather.8
  156.7 51.7 all-gather.10
  433.5 87.4 reduce-scatter.12
  525.1 62.5 reduce-scatter.6
  591.8 110.3 reduce-scatter.8
  706.9 111.1 reduce-scatter.10
  820.5 72.1 all-reduce.21
where the time goes:
time: 911 us; the launch traced here: 907 us
  waiting for transfers between devices  310 us (34%)
  matrix products  283 us (31%)
  blocking collectives  129 us (14%)
  local copies, waits for them, and re-layouts  120 us (13%)
  other arithmetic  45.7 us (5%)
  between operations  18.6 us (2%)
    unnamed x2, blocking collectives  123 us
    reduce_scatter x1, waiting for transfers between devices, body(): lax.psum_scatter(grad_down, 'fsdp', scatter_dimension=0, tiled=True)  116 us
    reduce_scatter x1, waiting for transfers between devices, body(): lax.psum_scatter(grad_up, 'fsdp', scatter_dimension=0, tiled=True)  115 us
    dot_general x4, matrix products, product(): return jnp.dot(left_side, right_side, preferred_element_type=jnp.float32)  106 us
    unnamed x120, local copies, waits for them, and re-layouts  67.3 us
    dot_general x4, matrix products, times_transpose(): lax.dot_general(left_side, right_side, (((1,), (1,)), ((), ())), preferre...  66.7 us
    psum x1, waiting for transfers between devices, body(): lax.psum((attention_parts[0], attention_parts[1], attention_parts[2], att...  60.1 us
    dot_general x4, matrix products, transpose_times(): lax.dot_general(left_side, right_side, (((0,), (0,)), ((), ())), preferre...  53.8 us
  transfers between devices with their start and end apart: 9, of which 4 were waited for; matrix products, arithmetic and copies ran while one was open for 27% of the time, Pallas kernels for 0%

commit v1 on v0

v1 whole, which is shorter than its diff:
```python
import functools
import math

import jax
import jax.numpy as jnp
from jax import lax
from jax.experimental import pallas as pl
from jax.experimental.pallas import tpu as pltpu
from jax.sharding import PartitionSpec as P

HEAD = 64
PAIR = 2 * HEAD
EPSILON = 1e-12
F32 = jnp.float32
BF16 = jnp.bfloat16
VMEM_LIMIT = 60000 * 1024

ERFC_SLOPE = 0.33
ERFC_TERMS = (
    0.18635788923911423,
    0.18295457713165508,
    0.20123280917878972,
    0.04718951182123742,
    0.408562666534809,
    -0.35122255207376696,
    0.46028245445329624,
    -0.1353573694779288,
)


def product(left, right):
    return jnp.dot(left, right, preferred_element_type=F32)


def times_transpose(left, right):
    return lax.dot_general(left, right, (((1,), (1,)), ((), ())), preferred_element_type=F32)


def transpose_times(left, right):
    return lax.dot_general(left, right, (((0,), (0,)), ((), ())), preferred_element_type=F32)


def normal_parts(u):
    density = jnp.exp(-0.5 * u * u)
    t = 1.0 / (1.0 + (ERFC_SLOPE / math.sqrt(2.0)) * jnp.abs(u))
    poly = jnp.full_like(t, 0.5 * ERFC_TERMS[-1])
    for term in ERFC_TERMS[-2::-1]:
        poly = poly * t + 0.5 * term
    tail = poly * t * density
    cumulative = jnp.where(u >= 0.0, 1.0 - tail, tail)
    return cumulative, u * (density * (1.0 / math.sqrt(2.0 * math.pi)))


def normalise(rows):
    average = jnp.mean(rows, axis=-1, keepdims=True)
    centred = rows - average
    variance = jnp.mean(centred * centred, axis=-1, keepdims=True)
    rstd = lax.rsqrt(variance + EPSILON)
    return centred * rstd, rstd


def normalise_back(grad, gain, xhat, rstd):
    e = grad * gain
    mean_e = jnp.mean(e, axis=-1, keepdims=True)
    mean_ex = jnp.mean(e * xhat, axis=-1, keepdims=True)
    return rstd * (e - mean_e - xhat * mean_ex)


def fold(values):
    rows, width = values.shape
    return jnp.sum(values.reshape(rows // 8, 8, width), axis=0)


def lane_halves():
    lane = lax.broadcasted_iota(jnp.int32, (1, PAIR), 1)
    return (lane < HEAD).astype(BF16), (lane >= HEAD).astype(BF16)


def split_heads(block, low_half, high_half):
    return jnp.concatenate([block * low_half, block * high_half], axis=0)


def segment_grid(seg_ref, row, length):
    ids = seg_ref[pl.ds(row, 1), :].astype(F32)
    along_lanes = jnp.broadcast_to(ids, (length, length))
    return along_lanes, along_lanes.T


def attention_kernel(length, width, x_ref, seg_ref, w_ref, bias_ref, qkv_ref, ctx_ref):
    tokens = x_ref.shape[0]
    step = pl.program_id(0)
    x = x_ref[...]
    for part in range(3):
        cols = pl.ds(part * width, width)
        qkv_ref[:, cols] = (product(x, w_ref[:, cols]) + bias_ref[:, cols]).astype(BF16)
    low_half, high_half = lane_halves()
    ones_low = jnp.broadcast_to(low_half, (length, PAIR))
    ones_high = jnp.broadcast_to(high_half, (length, PAIR))
    scale = HEAD**-0.5
    for local in range(tokens // length):
        rows = pl.ds(local * length, length)
        along_lanes, along_rows = segment_grid(seg_ref, step * (tokens // length) + local, length)
        same = along_lanes == along_rows
        for pair in range(width // PAIR):
            q = qkv_ref[rows, pl.ds(pair * PAIR, PAIR)] * BF16(scale)
            k = qkv_ref[rows, pl.ds(width + pair * PAIR, PAIR)]
            v = qkv_ref[rows, pl.ds(2 * width + pair * PAIR, PAIR)]
            scores = times_transpose(q, split_heads(k, low_half, high_half))
            parts = []
            for half in range(2):
                masked = jnp.where(same, scores[:, half * length : (half + 1) * length], -1e30)
                peak = jnp.max(masked, axis=-1, keepdims=True)
                parts.append(jnp.exp(masked - peak).astype(BF16))
            values = jnp.concatenate(
                [
                    split_heads(v, low_half, high_half),
                    jnp.concatenate([ones_low, ones_high], axis=0),
                ],
                axis=1,
            )
            both = product(jnp.concatenate(parts, axis=1), values)
            ctx_ref[rows, pl.ds(pair * PAIR, PAIR)] = (both[:, :PAIR] / both[:, PAIR:]).astype(BF16)


def attention_forward(x, seg, w, bias, rows_per_step=2):
    row_count, length = seg.shape
    tokens, width = x.shape
    block = rows_per_step * length
    return pl.pallas_call(
        functools.partial(attention_kernel, length, width),
        grid=(row_count // rows_per_step,),
        in_specs=[
            pl.BlockSpec((block, width), lambda i: (i, 0)),
            pl.BlockSpec((row_count, length), lambda i: (0, 0)),
            pl.BlockSpec((width, 3 * width), lambda i: (0, 0), pipeline_mode=pl.Buffered(1)),
            pl.BlockSpec((1, 3 * width), lambda i: (0, 0)),
        ],
        out_specs=[
            pl.BlockSpec((block, 3 * width), lambda i: (i, 0)),
            pl.BlockSpec((block, width), lambda i: (i, 0)),
        ],
        out_shape=[
            jax.ShapeDtypeStruct((tokens, 3 * width), BF16),
            jax.ShapeDtypeStruct((tokens, width), BF16),
        ],
        compiler_params=pltpu.CompilerParams(vmem_limit_bytes=VMEM_LIMIT),
        cost_estimate=pl.CostEstimate(
            flops=2 * tokens * width * 3 * width + 8 * tokens * length * width,
            bytes_accessed=tokens * width * 10 + 6 * width * width,
            transcendentals=tokens * length * (width // HEAD),
        ),
        name="attention_forward",
    )(x, seg, w, bias)


def feedforward_kernel(
    length,
    chunk,
    x_ref,
    ctx_ref,
    seg_ref,
    pooled_grad_ref,
    out_w_ref,
    up_w_ref,
    down_w_ref,
    vec_ref,
    up_bias_ref,
    pooled_ref,
    active_ref,
    hidden_ref,
    normed_ref,
    branch_ref,
    first_ref,
    attended_ref,
    context_ref,
    small_ref,
    up_small_ref,
    slope_ref,
):
    step = pl.program_id(0)
    tokens, width = x_ref.shape
    hidden = up_w_ref.shape[1]
    segments = pooled_grad_ref.shape[1]
    out_bias, gain_one, shift_one = vec_ref[0:1, :], vec_ref[1:2, :], vec_ref[2:3, :]
    down_bias, gain_two, shift_two = vec_ref[3:4, :], vec_ref[4:5, :], vec_ref[5:6, :]

    @pl.when(step == 0)
    def _():
        small_ref[...] = jnp.zeros_like(small_ref)
        up_small_ref[...] = jnp.zeros_like(up_small_ref)

    first_sum = x_ref[...].astype(F32) + product(ctx_ref[...], out_w_ref[...]) + out_bias
    xhat_one, rstd_one = normalise(first_sum)
    normed_one = xhat_one * gain_one + shift_one
    normed_low = normed_one.astype(BF16)
    normed_ref[...] = normed_low
    second_sum = normed_one + down_bias
    for start in range(0, hidden, chunk):
        cols = pl.ds(start, chunk)
        pre = product(normed_low, up_w_ref[:, cols]) + up_bias_ref[:, cols]
        cumulative, tilt = normal_parts(pre)
        active = (pre * cumulative).astype(BF16)
        slope_ref[:, cols] = cumulative + tilt
        active_ref[:, cols] = active
        second_sum = second_sum + product(active, down_w_ref[cols, :])
    xhat_two, rstd_two = normalise(second_sum)
    final = xhat_two * gain_two + shift_two
    final_high = final.astype(BF16)
    final_low = (final - final_high.astype(F32)).astype(BF16)
    token_parts = []
    for local in range(tokens // length):
        rows = slice(local * length, (local + 1) * length)
        along_lanes, along_rows = segment_grid(seg_ref, step * (tokens // length) + local, length)
        index = lax.broadcasted_iota(jnp.int32, (8, length), 0).astype(F32)
        member = (along_lanes[:8, :] == index).astype(F32)
        population = jnp.sum(member, axis=1, keepdims=True)
        member_low = member.astype(BF16)
        sums = product(member_low, final_high[rows]) + product(member_low, final_low[rows])
        pooled_ref[local] = sums[:segments] / population[:segments]
        share = pooled_grad_ref[local] / population[:segments]
        wide = jnp.concatenate([along_rows] * (width // length), axis=1)
        token = jnp.broadcast_to(share[segments - 1 : segments], (length, width))
        for s in range(segments - 2, -1, -1):
            token = jnp.where(wide == float(s), share[s : s + 1], token)
        token_parts.append(token)
    token_grad = jnp.concatenate(token_parts, axis=0)
    second_grad = normalise_back(token_grad, gain_two, xhat_two, rstd_two)
    branch = second_grad.astype(BF16)
    branch_ref[...] = branch
    small_ref[24:32, :] += fold(branch.astype(F32))
    small_ref[32:40, :] += fold(token_grad * xhat_two)
    small_ref[40:48, :] += fold(token_grad)
    normed_grad = second_grad
    for start in range(0, hidden, chunk):
        cols = pl.ds(start, chunk)
        grad = (times_transpose(branch, down_w_ref[cols, :]) * slope_ref[:, cols]).astype(BF16)
        hidden_ref[:, cols] = grad
        up_small_ref[:, cols] += fold(grad.astype(F32))
        normed_grad = normed_grad + times_transpose(grad, up_w_ref[:, cols])
    first_grad = normalise_back(normed_grad, gain_one, xhat_one, rstd_one)
    first_ref[...] = first_grad
    attended = first_grad.astype(BF16)
    attended_ref[...] = attended
    context_ref[...] = times_transpose(attended, out_w_ref[...]).astype(BF16)
    small_ref[0:8, :] += fold(attended.astype(F32))
    small_ref[8:16, :] += fold(normed_grad * xhat_one)
    small_ref[16:24, :] += fold(normed_grad)


def feedforward(x, ctx, seg, pooled_grad, out_w, up_w, down_w, vectors, up_bias, rows_per_step=2, chunk=768):
    row_count, length = seg.shape
    tokens, width = x.shape
    hidden = up_w.shape[1]
    segments = pooled_grad.shape[1]
    block = rows_per_step * length

    def tiled(columns):
        return pl.BlockSpec((block, columns), lambda i: (i, 0))

    def whole(shape):
        return pl.BlockSpec(shape, lambda i: (0,) * len(shape), pipeline_mode=pl.Buffered(1))

    def kept(shape):
        return pl.BlockSpec(shape, lambda i: (0,) * len(shape))

    def rows(columns, dtype):
        return jax.ShapeDtypeStruct((tokens, columns), dtype)

    return pl.pallas_call(
        functools.partial(feedforward_kernel, length, chunk),
        grid=(row_count // rows_per_step,),
        in_specs=[
            tiled(width),
            tiled(width),
            whole((row_count, length)),
            pl.BlockSpec((rows_per_step, segments, width), lambda i: (i, 0, 0)),
            whole((width, width)),
            whole((width, hidden)),
            whole((hidden, width)),
            whole((8, width)),
            whole((1, hidden)),
        ],
        out_specs=[
            pl.BlockSpec((rows_per_step, segments, width), lambda i: (i, 0, 0)),
            tiled(hidden),
            tiled(hidden),
            tiled(width),
            tiled(width),
            tiled(width),
            tiled(width),
            tiled(width),
            kept((48, width)),
            kept((8, hidden)),
        ],
        out_shape=[
            jax.ShapeDtypeStruct((row_count, segments, width), F32),
            rows(hidden, BF16),
            rows(hidden, BF16),
            rows(width, BF16),
            rows(width, BF16),
            rows(width, F32),
            rows(width, BF16),
            rows(width, BF16),
            jax.ShapeDtypeStruct((48, width), F32),
            jax.ShapeDtypeStruct((8, hidden), F32),
        ],
        scratch_shapes=[pltpu.VMEM((block, hidden), F32)],
        compiler_params=pltpu.CompilerParams(vmem_limit_bytes=VMEM_LIMIT),
        cost_estimate=pl.CostEstimate(
            flops=tokens * width * (4 * width + 8 * hidden),
            bytes_accessed=tokens * (width * 18 + hidden * 4) + 4 * width * hidden,
            transcendentals=2 * tokens * hidden,
        ),
        name="feedforward",
    )(x, ctx, seg, pooled_grad, out_w, up_w, down_w, vectors, up_bias)


def attention_back_kernel(length, width, qkv_ref, grad_ref, seg_ref, out_ref, small_ref):
    tokens = grad_ref.shape[0]
    step = pl.program_id(0)

    @pl.when(step == 0)
    def _():
        small_ref[...] = jnp.zeros_like(small_ref)

    low_half, high_half = lane_halves()
    scale = HEAD**-0.5
    for local in range(tokens // length):
        rows = pl.ds(local * length, length)
        along_lanes, along_rows = segment_grid(seg_ref, step * (tokens // length) + local, length)
        same = along_lanes == along_rows
        same = jnp.concatenate([same, same], axis=1)
        for pair in range(width // PAIR):
            at = (pl.ds(pair * PAIR, PAIR), pl.ds(width + pair * PAIR, PAIR), pl.ds(2 * width + pair * PAIR, PAIR))
            q = split_heads(qkv_ref[rows, at[0]] * BF16(scale), low_half, high_half)
            k = qkv_ref[rows, at[1]]
            v = qkv_ref[rows, at[2]]
            ctx_grad = split_heads(grad_ref[rows, at[0]], low_half, high_half)
            scores = jnp.where(same, times_transpose(k, q), -1e30)
            weights = jnp.exp(scores - jnp.max(scores, axis=0, keepdims=True))
            weights = weights * (1.0 / jnp.sum(weights, axis=0, keepdims=True))
            probs_grad = times_transpose(v, ctx_grad)
            inner = jnp.sum(weights * probs_grad, axis=0, keepdims=True)
            scores_grad = (weights * (probs_grad - inner)).astype(BF16)
            values_grad = product(weights.astype(BF16), ctx_grad).astype(BF16)
            keys_grad = product(scores_grad, q).astype(BF16)
            turned = jnp.concatenate([scores_grad[:, :length].T, scores_grad[:, length:].T], axis=1)
            queries_grad = product(turned, split_heads(k * BF16(scale), low_half, high_half)).astype(BF16)
            out_ref[rows, at[0]] = queries_grad
            out_ref[rows, at[1]] = keys_grad
            out_ref[rows, at[2]] = values_grad
            small_ref[:, at[0]] += fold(queries_grad.astype(F32))
            small_ref[:, at[1]] += fold(values_grad.astype(F32))


def attention_backward(qkv, ctx_grad, seg, rows_per_step=2):
    row_count, length = seg.shape
    tokens, width = ctx_grad.shape
    block = rows_per_step * length
    return pl.pallas_call(
        functools.partial(attention_back_kernel, length, width),
        grid=(row_count // rows_per_step,),
        in_specs=[
            pl.BlockSpec((block, 3 * width), lambda i: (i, 0)),
            pl.BlockSpec((block, width), lambda i: (i, 0)),
            pl.BlockSpec((row_count, length), lambda i: (0, 0)),
        ],
        out_specs=[
            pl.BlockSpec((block, 3 * width), lambda i: (i, 0)),
            pl.BlockSpec((8, 2 * width), lambda i: (0, 0)),
        ],
        out_shape=[
            jax.ShapeDtypeStruct((tokens, 3 * width), BF16),
            jax.ShapeDtypeStruct((8, 2 * width), F32),
        ],
        compiler_params=pltpu.CompilerParams(vmem_limit_bytes=VMEM_LIMIT),
        cost_estimate=pl.CostEstimate(
            flops=20 * tokens * length * width,
            bytes_accessed=tokens * width * 14,
            transcendentals=tokens * length * (width // HEAD),
        ),
        name="attention_backward",
    )(qkv, ctx_grad, seg)


def body(
    hidden_in,
    segment_ids,
    pooled_grad,
    qkv_weight,
    qv_bias,
    out_weight,
    out_bias,
    first_gain,
    first_shift,
    up_weight,
    up_bias,
    down_weight,
    down_bias,
    second_gain,
    second_shift,
):
    row_count, length, width = hidden_in.shape
    x = hidden_in.reshape(row_count * length, width)

    def gather(shard):
        return lax.all_gather(shard, "fsdp", axis=0, tiled=True)

    small = jnp.concatenate(
        [qv_bias, out_bias, first_gain, first_shift, up_bias, down_bias, second_gain, second_shift]
    ).astype(BF16)
    small = lax.all_gather(small, "fsdp", axis=0, tiled=False).astype(F32)
    unit = out_bias.shape[0]
    ends = [0]
    for part in (qv_bias, out_bias, first_gain, first_shift, up_bias, down_bias, second_gain, second_shift):
        ends.append(ends[-1] + part.shape[0])
    qv, ob, g1, s1, ub, db, g2, s2 = (small[:, a:b].reshape(1, -1) for a, b in zip(ends[:-1], ends[1:]))
    zeros = jnp.zeros((1, width), F32)
    vectors = jnp.concatenate([ob, g1, s1, db, g2, s2, zeros, zeros], axis=0)
    qkv_bias = jnp.concatenate([qv[:, :width], zeros, qv[:, width:]], axis=1)
    qkv_matrix = gather(qkv_weight)
    out_matrix = gather(out_weight)
    up_matrix = gather(up_weight)
    down_matrix = gather(down_weight)
    qkv, ctx = attention_forward(x, segment_ids, qkv_matrix, qkv_bias)
    pooled, active, hidden_grad, normed, branch, first_grad, attended, ctx_grad, sums, up_sums = feedforward(
        x, ctx, segment_ids, pooled_grad, out_matrix, up_matrix, down_matrix, vectors, ub
    )

    def scatter(grad):
        return lax.psum_scatter(grad.astype(BF16), "fsdp", scatter_dimension=0, tiled=True)

    grad_down = scatter(transpose_times(active, branch))
    grad_up = scatter(transpose_times(normed, hidden_grad))
    grad_out = scatter(transpose_times(ctx, attended))
    qkv_grad, qv_sums = attention_backward(qkv, ctx_grad, segment_ids)
    grad_qkv = scatter(transpose_times(x, qkv_grad))
    grad_input = first_grad + times_transpose(qkv_grad, qkv_matrix)
    grad_qkv, grad_out, grad_up, grad_down = lax.psum(
        tuple(g.astype(F32) for g in (grad_qkv, grad_out, grad_up, grad_down)), "dp"
    )
    sums = jnp.sum(sums.reshape(6, 8, width), axis=1)
    vector_sums = jnp.concatenate(
        [jnp.sum(qv_sums, axis=0), sums.reshape(-1), jnp.sum(up_sums, axis=0)]
    )
    vector_sums = lax.psum(vector_sums, ("dp", "fsdp"))
    me = lax.axis_index("fsdp")

    def mine(start, size):
        return lax.dynamic_slice(vector_sums, (start + me * size,), (size,))

    at = 2 * width
    return (
        pooled,
        grad_input.reshape(row_count, length, width),
        grad_qkv,
        mine(0, 2 * unit),
        grad_out,
        mine(at, unit),
        mine(at + width, unit),
        mine(at + 2 * width, unit),
        grad_up,
        mine(at + 6 * width, up_bias.shape[0]),
        grad_down,
        mine(at + 3 * width, unit),
        mine(at + 4 * width, unit),
        mine(at + 5 * width, unit),
    )


def solution(mesh):
    rows = ("dp", "fsdp")
    in_specs = (P(rows, None, None), P(rows, None), P(rows, None, None)) + (
        P("fsdp", None),
        P("fsdp"),
        P("fsdp", None),
        P("fsdp"),
        P("fsdp"),
        P("fsdp"),
        P("fsdp", None),
        P("fsdp"),
        P("fsdp", None),
        P("fsdp"),
        P("fsdp"),
        P("fsdp"),
    )
    out_specs = (
        P(rows, None, None),
        P(rows, None, None),
        P("fsdp", None),
        P("fsdp"),
        P("fsdp", None),
        P("fsdp"),
        P("fsdp"),
        P("fsdp"),
        P("fsdp", None),
        P("fsdp"),
        P("fsdp", None),
        P("fsdp"),
        P("fsdp"),
        P("fsdp"),
    )
    return jax.shard_map(body, mesh=mesh, in_specs=in_specs, out_specs=out_specs, check_vma=False)
```

time: 911 us -> 662 us (0.73)
  matrix products: 283 us -> 60 us
  Pallas kernels: 0 us -> 134 us
  local copies, waits for them, and re-layouts: 120 us -> 21.8 us
  waiting for transfers between devices: 310 us -> 256 us
  other arithmetic: 45.7 us -> 0.71 us
  blocking collectives: 129 us -> 164 us
    dot_general x20 -> x5, matrix products: 283 us -> 60 us  [the longest x4 46.2 us: transpose_times(): lax.dot_general(left, right, (((0,), (0,)), ((), ())), preferred_element_...]
    pallas_call x0 -> x3, Pallas kernels: none -> 134 us  [the longest x1 84.1 us: feedforward(): pl.pallas_call(functools.partial(feedforward_kernel, length, chunk), grid...]
    all_gather x4, waiting for transfers between devices: 0.05 us -> 105 us  [gather(): return lax.all_gather(shard, 'fsdp', axis=0, tiled=True)]
    reduce_scatter x3, waiting for transfers between devices: 248 us -> 149 us  [scatter(): lax.psum_scatter(grad.astype(BF16), 'fsdp', scatter_dimension=0, tiled=True)]
    psum x1 -> x2, blocking collectives: 5.54 us -> 101 us  [the longest x1 60.1 us: body(): lax.psum(tuple((g.astype(F32) for g in (grad_qkv, grad_out, grad_up, grad...]
    psum x1 -> x0, waiting for transfers between devices: 60.1 us -> none  [body(): lax.psum((attention_parts[0], attention_parts[1], attention_parts[2], att...]
    unnamed x2 -> x1, blocking collectives: 123 us -> 63.3 us
    unnamed x120 -> x18, local copies, waits for them, and re-layouts: 67.3 us -> 12.3 us
  transfers between devices with their start and end apart: 9 -> 8, of which waited for: 4 -> 4; matrix products, arithmetic and copies ran while one was open for 27% -> 11% of each run, Pallas kernels for 0% -> 8%
where the time goes in v1:
time: 662 us; the launch traced here: 653 us
  waiting for transfers between devices  256 us (39%)
  blocking collectives  164 us (25%)
  Pallas kernels  134 us (20%)
  matrix products  60 us (9%)
  local copies, waits for them, and re-layouts  21.8 us (3%)
  between operations  15.4 us (2%)
    reduce_scatter x3, waiting for transfers between devices, scatter(): lax.psum_scatter(grad.astype(BF16), 'fsdp', scatter_dimension=0, tiled=True)  149 us
    all_gather x4, waiting for transfers between devices, gather(): return lax.all_gather(shard, 'fsdp', axis=0, tiled=True)  105 us
    pallas_call x1, Pallas kernels, feedforward(): pl.pallas_call(functools.partial(feedforward_kernel, length, chunk), grid...  84.1 us
    unnamed x1, blocking collectives  63.3 us
    psum x1, blocking collectives, body(): lax.psum(tuple((g.astype(F32) for g in (grad_qkv, grad_out, grad_up, grad...  60.1 us
    dot_general x4, matrix products, transpose_times(): lax.dot_general(left, right, (((0,), (0,)), ((), ())), preferred_element_...  46.2 us
    psum x1, blocking collectives, body(): vector_sums = lax.psum(vector_sums, ('dp', 'fsdp'))  40.7 us
    pallas_call x1, Pallas kernels, attention_backward(): pl.pallas_call(functools.partial(attention_back_kernel, length, width), g...  30 us
  transfers between devices with their start and end apart: 8, of which 4 were waited for; matrix products, arithmetic and copies ran while one was open for 11% of the time, Pallas kernels for 8%

profile of v1, /device:TPU:0, one launch (start us, length us, event | category | flops | bytes accessed | tf_op | source)
XLA Modules:
  0.0 652.6 jit_solution(3450855778561631798)
XLA Ops:
  7.2 0.7 all-gather.6.cloned.1.call-update
  8.0 0.7 all-gather.8.cloned.1.call-update
  8.7 0.7 all-gather.10.cloned.1.call-update
  9.4 0.5 all-gather.12.cloned.1.call-update
  10.0 1.2 dynamic-slice
  11.9 5.4 concatenate.15
  17.4 0.2 dynamic-update-slice
  17.6 63.3 %all-reduce = bf16[9216]{0:T(1024)(128)(2,1)S(1)} all-reduce(bf16[9216]{0:T(1024)(128)(2,1)S(1)} %dynamic-update-slice), channel_id=2, replica_groups=mesh['dp'=2,'fsdp'=16] {'fsdp'}, use_global_device_ids=true, to_apply=%add | all-reduce | flops 9216 | bytes 36864
  80.9 0.1 reshape.77
  81.0 0.1 slice.49
  81.1 0.1 fusion.2
  81.1 0.1 reshape.66
  81.2 0.1 reshape.67
  81.3 0.1 reshape.68
  81.4 0.1 reshape.69
  81.5 0.1 reshape.70
  81.6 0.1 reshape.71
  81.6 0.1 reshape.65
  81.7 0.7 reshape.72.up_bias_ref
  82.4 0.6 concatenate.18.vec_ref
  83.1 0.6 fusion.1.bias_ref
  83.7 20.2 %attention_forward.1 = (bf16[2048,2304]{1,0:T(8,128)(2,1)}, bf16[2048,768]{1,0:T(8,128)(2,1)}) custom-call(bf16[2048,768]{1,0:T(8,128)(2,1)} %bitcast.18, s32[16,128]{1,0:T(8,128)} %seg_ref.5, bf16[768,2304]{1,0:T(8,128)(2,1)} %all-gather.6.cloned.1.call-done.w_ref, f32[1,2304]{1,0:T(1,128)} %fusion.1.bias_ref), custom_call_target="tpu_custom_call" | custom-call | flops 8858370048 | bytes 19267584 | tf_op jit(solution)/shard_map/attention_forward/pallas_call | solution.py:129
  103.9 51.0 %all-gather.10.cloned.1.call-done.up_w_ref = bf16[768,3072]{1,0:T(8,128)(2,1)} async-done(((bf16[48,3072]{1,0:T(8,128)(2,1)}), bf16[768,3072]{1,0:T(8,128)(2,1)}) %all-gather.10.cloned.1.call-update) | async-done | bytes 4718608 | tf_op jit(solution)/shard_map/all_gather | solution.py:407
  154.9 54.0 %all-gather.12.cloned.1.call-done.down_w_ref = bf16[3072,768]{1,0:T(8,128)(2,1)} async-done(((bf16[192,768]{1,0:T(8,128)(2,1)}), bf16[3072,768]{1,0:T(8,128)(2,1)}) %all-gather.12.cloned.1.call-update) | async-done | bytes 4718608 | tf_op jit(solution)/shard_map/all_gather | solution.py:407
  208.9 84.1 %feedforward.1 = (f32[16,4,768]{2,1,0:T(4,128)}, bf16[2048,3072]{1,0:T(8,128)(2,1)}, bf16[2048,3072]{1,0:T(8,128)(2,1)}, bf16[2048,768]{1,0:T(8,128)(2,1)}, bf16...) custom-call(bf16[2048,768]{1,0:T(8,128)(2,1)} %bitcast.19, ...), custom_call_target="tpu_custom_call" | custom-call | flops 43486543872 | bytes 62914560 | tf_op jit(solution)/shard_map/feedforward/pallas_call | solution.py:269
  293.0 5.6 convolution_convert_fusion.3
  298.6 0.0 reduce-scatter.13.cloned.1.call-start
  298.6 30.0 %attention_backward.1 = (bf16[2048,2304]{1,0:T(8,128)(2,1)}, f32[8,1536]{1,0:T(8,128)}) custom-call(bf16[2048,2304]{1,0:T(8,128)(2,1)} %get-tuple-element.31.qkv_ref, bf16[2048,768]{1,0:T(8,128)(2,1)} %get-tuple-element.32.grad_ref, s32[16,128]{1,0:T(8,128)} %seg_ref.5), custom_call_target="tpu_custom_call" | custom-call | flops 4026531840 | bytes 22020096 | tf_op jit(solution)/shard_map/attention_backward/pallas_call | solution.py:360
  328.6 11.2 %fusion = bf16[768,2304]{0,1:T(8,128)(2,1)S(1)} fusion(bf16[2048,2304]{1,0:T(8,128)(2,1)} %get-tuple-element.33, bf16[2048,768]{1,0:T(8,128)(2,1)} %bitcast.20), kind=kOutput, calls=%fused_computation.3 | convolution fusion | flops 7249526784 | bytes 16121856 | tf_op jit(solution)/shard_map/dot_general | solution.py:40
  339.8 4.0 copy.31
  343.8 0.0 reduce-scatter.11.cloned.1.call-start
  343.9 1.8 copy-done.5
  345.7 14.7 %convolution_convert_fusion = bf16[3072,768]{1,0:T(8,128)(2,1)} fusion(bf16[2048,3072]{1,0:T(8,128)(2,1)} %get-tuple-element.40, bf16[2048,768]{1,0:T(8,128)(2,1)S(1)} %copy-done.5), kind=kOutput, calls=%fused_computation | convolution fusion | flops 9666035712 | bytes 20447232 | tf_op jit(solution)/shard_map/dot_general | solution.py:40
  360.4 0.0 reduce-scatter.9.cloned.1.call-start
  360.5 1.8 copy-done.4
  362.3 14.7 %convolution_convert_fusion.1 = bf16[768,3072]{1,0:T(8,128)(2,1)} fusion(bf16[2048,768]{1,0:T(8,128)(2,1)S(1)} %copy-done.4, bf16[2048,3072]{1,0:T(8,128)(2,1)} %get-tuple-element.39), kind=kOutput, calls=%fused_computation.1 | convolution fusion | flops 9666035712 | bytes 20447232 | tf_op jit(solution)/shard_map/dot_general | solution.py:40
  377.0 0.8 copy-done.2
  377.8 0.1 copy-done
  378.0 40.7 %psum.36 = f32[9216]{0:T(1024)S(1)} all-reduce(f32[9216]{0:T(1024)S(1)} %pad_maximum_fusion), channel_id=1, replica_groups=mesh['dp'=2,'fsdp'=16] {'dp','fsdp'}, use_global_device_ids=true, to_apply=%region_5.0 | all-reduce | flops 9216 | bytes 73728 | tf_op jit(solution)/shard_map/psum | solution.py:446
  418.7 0.6 dynamic_slice.28
  419.3 0.6 dynamic_slice.24
  419.9 0.6 fusion.3
  420.5 13.8 %convolution_add_fusion = f32[2048,768]{1,0:T(8,128)} fusion(f32[2048,768]{1,0:T(8,128)} %get-tuple-element.30, bf16[2048,2304]{1,0:T(8,128)(2,1)} %get-tuple-element.33, bf16[768,2304]{1,0:T(8,128)(2,1)} %all-gather.6.cloned.1.call-done.w_ref), kind=kOutput, calls=%fused_computation.4 | convolution fusion | flops 7249330176 | bytes 25559040 | tf_op jit(solution)/shard_map/dot_general | solution.py:36
  434.3 1.3 copy.32
  435.6 69.5 %reduce-scatter.11.cloned.1.call-done = bf16[192,768]{1,0:T(8,128)(2,1)} async-done(((bf16[3072,768]{1,0:T(8,128)(2,1)}), bf16[192,768]{1,0:T(8,128)(2,1)}) %reduce-scatter.11.cloned.1.call-update) | async-done | bytes 294928 | tf_op jit(solution)/shard_map/reduce_scatter | solution.py:431
  505.1 79.0 %reduce-scatter.9.cloned.1.call-done = bf16[48,3072]{1,0:T(8,128)(2,1)} async-done(((bf16[768,3072]{1,0:T(8,128)(2,1)}), bf16[48,3072]{1,0:T(8,128)(2,1)}) %reduce-scatter.9.cloned.1.call-update) | async-done | bytes 294928 | tf_op jit(solution)/shard_map/reduce_scatter | solution.py:431
  584.1 60.1 %all-reduce.3 = (f32[48,2304]{0,1:T(8,128)S(1)}, f32[48,768]{1,0:T(8,128)}, f32[48,3072]{1,0:T(8,128)}, f32[192,768]{1,0:T(8,128)}) all-reduce(bf16[48,2304]{0,1:T(8,128)(2,1)S(1)} %copy.32, bf16[48,768]{1,0:T(8,128)(2,1)} %reduce-scatter.7.cloned.1.call-done, ...), channel_id=1, replica_groups=mesh['dp'=2,'fsdp'=16] {'dp'}, use_global_device_ids=true, to_apply=%region_1.0 | all-reduce | flops 442368 | bytes 2654208 | tf_op jit(solution)/shard_map/psum | solution.py:439
  644.2 1.1 copy.30
  (32 shorter events, 0.4 us)
Async XLA Ops:
  7.2 76.5 %all-gather.6.cloned.1.call-start = ((), (), s32[]{:S(2)}) async-start(), calls=%async_computation.4 | async-start | bytes 3760128 | tf_op jit(solution)/shard_map/all_gather | solution.py:407
  7.9 96.0 %all-gather.8.cloned.1.call-start = ((), (), s32[]{:S(2)}) async-start(), calls=%async_computation.5 | async-start | bytes 1253376 | tf_op jit(solution)/shard_map/all_gather | solution.py:407
  8.7 146.2 %all-gather.10.cloned.1.call-start = ((), (), s32[]{:S(2)}) async-start(), calls=%async_computation.6 | async-start | bytes 5013504 | tf_op jit(solution)/shard_map/all_gather | solution.py:407
  9.4 199.5 %all-gather.12.cloned.1.call-start = ((), (), s32[]{:S(2)}) async-start(), calls=%async_computation.7 | async-start | bytes 5013504 | tf_op jit(solution)/shard_map/all_gather | solution.py:407
  10.0 424.3 %reduce-scatter.7.cloned.1.call-start = ((), (), s32[]{:S(2)}) async-start(), calls=%async_computation.8 | async-start | bytes 1253376 | tf_op jit(solution)/shard_map/reduce_scatter | solution.py:431
  208.9 84.1 %copy-start.3 = (bf16[2048,768]{1,0:T(8,128)(2,1)S(1)}, bf16[2048,768]{1,0:T(8,128)(2,1)}, u32[]{:S(2)}) copy-start(bf16[2048,768]{1,0:T(8,128)(2,1)} %get-tuple-element.28.ctx_ref) | copy-start | bytes 9437188
  298.6 135.7 %reduce-scatter.13.cloned.1.call-start = ((), (), s32[]{:S(2)}) async-start(), calls=%async_computation.11 | async-start | bytes 3760128
  343.8 1.9 copy-start.5
  343.8 161.2 %reduce-scatter.11.cloned.1.call-start = ((), (), s32[]{:S(2)}) async-start(), calls=%async_computation.10 | async-start | bytes 5013504 | tf_op jit(solution)/shard_map/reduce_scatter | solution.py:431
  360.4 1.9 copy-start.4
  360.4 223.7 %reduce-scatter.9.cloned.1.call-start = ((), (), s32[]{:S(2)}) async-start(), calls=%async_computation.9 | async-start | bytes 5013504 | tf_op jit(solution)/shard_map/reduce_scatter | solution.py:431
  376.9 0.8 copy-start.2
  376.9 0.9 copy-start
  376.9 1.0 copy-start.1
Sparse Core Ops, SparseCore 0:
  10.3 50.3 all-gather.5
  63.0 37.3 all-gather.7
  102.7 52.2 all-gather.9
  157.0 51.7 all-gather.11
  298.7 56.6 reduce-scatter.6
  359.1 67.9 reduce-scatter.12
  431.0 74.0 reduce-scatter.10
  509.4 74.6 reduce-scatter.8

commit v2 on v1

--- a/solution.py
+++ b/solution.py
@@ -86,13 +86,48 @@
     return along_lanes, along_lanes.T
 
 
-def attention_kernel(length, width, x_ref, seg_ref, w_ref, bias_ref, qkv_ref, ctx_ref):
+BLOCK = 384
+SMALL = 16
+
+
+def place_of(place_ref):
+    return place_ref[0], place_ref[1], place_ref[2], place_ref[3]
+
+
+def shard_slots(place_ref):
+    y, z, x, core = place_of(place_ref)
+    for other in range(2):
+        for plane in range(4):
+            for turn in range(4):
+                if plane < 3:
+                    buffer, at = plane, turn
+                else:
+                    buffer, at = 3 + turn // 2, turn % 2
+                owner = ((z - turn) & 3) * 4 + (x ^ (plane & 1)) * 2 + (core ^ other)
+                yield 5 * other + buffer, at, owner, y ^ (plane >> 1), plane < 2
+
+
+def run_copies(copies, sems):
+    started = []
+    for number, (source, target) in enumerate(copies):
+        copy = pltpu.make_async_copy(source, target, sems.at[number])
+        copy.start()
+        started.append(copy)
+    for copy in started:
+        copy.wait()
+
+
+def aligned(index, unit):
+    return pl.multiple_of(index * unit, unit)
+
+
+def attention_rows(length, width, x_ref, seg_ref, w_ref, bias_ref, qkv_ref, ctx_ref):
     tokens = x_ref.shape[0]
     step = pl.program_id(0)
     x = x_ref[...]
     for part in range(3):
         cols = pl.ds(part * width, width)
-        qkv_ref[:, cols] = (product(x, w_ref[:, cols]) + bias_ref[:, cols]).astype(BF16)
+        qkv_ref[:, cols] = (product(x, w_ref[:, cols]) + bias_ref[0:1, cols]).astype(BF16)
     low_half, high_half = lane_halves()
     ones_low = jnp.broadcast_to(low_half, (length, PAIR))
     ones_high = jnp.broadcast_to(high_half, (length, PAIR))
@@ -122,27 +157,58 @@
             ctx_ref[rows, pl.ds(pair * PAIR, PAIR)] = (both[:, :PAIR] / both[:, PAIR:]).astype(BF16)
 
 
-def attention_forward(x, seg, w, bias, rows_per_step=2):
+def attention_gathered_kernel(length, width, place_ref, x_ref, seg_ref, *rest):
+    buffers, (qkv_ref, ctx_ref, w_ref, small_ref, bias_ref, sems) = rest[:10], rest[10:]
+    unit = width // 16
+
+    @pl.when(pl.program_id(0) == 0)
+    def _():
+        copies = []
+        for buffer, at, owner, half, first in shard_slots(place_ref):
+            source = buffers[buffer].at[at]
+            for block in range(3):
+                target = w_ref.at[
+                    pl.ds(aligned(owner, unit), unit), pl.ds(aligned(half * 3 + block, BLOCK), BLOCK)
+                ]
+                copies.append((source.at[pl.ds(block * unit, unit)], target))
+            if first:
+                copies.append((source.at[pl.ds(3 * unit, SMALL)], small_ref.at[owner]))
+        run_copies(copies, sems)
+        piece = 2 * unit
+        lane = lax.broadcasted_iota(jnp.int32, (8, width), 1)
+        for part, first in ((0, 0), (2, 8)):
+            total = jnp.zeros((8, width), F32)
+            for s in range(8):
+                row = small_ref[first + s].astype(F32)[:8]
+                row = jnp.where(lane < piece, jnp.concatenate([row, row], axis=1), 0.0)
+                total = total + (pltpu.roll(row, s * piece, 1) if s else row)
+            bias_ref[:, pl.ds(part * width, width)] = total
+        bias_ref[:, pl.ds(width, width)] = jnp.zeros((8, width), F32)
+
+    attention_rows(length, width, x_ref, seg_ref, w_ref, bias_ref, qkv_ref, ctx_ref)
+
+
+def attention_whole_kernel(length, width, x_ref, seg_ref, w_ref, bias_ref, qkv_ref, ctx_ref):
+    attention_rows(length, width, x_ref, seg_ref, w_ref, bias_ref, qkv_ref, ctx_ref)
+
+
+def attention_forward(x, seg, weights, place=None, rows_per_step=2):
     row_count, length = seg.shape
     tokens, width = x.shape
     block = rows_per_step * length
-    return pl.pallas_call(
-        functools.partial(attention_kernel, length, width),
-        grid=(row_count // rows_per_step,),
-        in_specs=[
-            pl.BlockSpec((block, width), lambda i: (i, 0)),
-            pl.BlockSpec((row_count, length), lambda i: (0, 0)),
-            pl.BlockSpec((width, 3 * width), lambda i: (0, 0), pipeline_mode=pl.Buffered(1)),
-            pl.BlockSpec((1, 3 * width), lambda i: (0, 0)),
-        ],
-        out_specs=[
-            pl.BlockSpec((block, 3 * width), lambda i: (i, 0)),
-            pl.BlockSpec((block, width), lambda i: (i, 0)),
-        ],
-        out_shape=[
-            jax.ShapeDtypeStruct((tokens, 3 * width), BF16),
-            jax.ShapeDtypeStruct((tokens, width), BF16),
-        ],
+    in_specs = [
+        pl.BlockSpec((block, width), lambda i, *_: (i, 0)),
+        pl.BlockSpec((row_count, length), lambda i, *_: (0, 0)),
+    ]
+    out_specs = [
+        pl.BlockSpec((block, 3 * width), lambda i, *_: (i, 0)),
+        pl.BlockSpec((block, width), lambda i, *_: (i, 0)),
+    ]
+    out_shape = [
+        jax.ShapeDtypeStruct((tokens, 3 * width), BF16),
+        jax.ShapeDtypeStruct((tokens, width), BF16),
+    ]
+    settings = dict(
         compiler_params=pltpu.CompilerParams(vmem_limit_bytes=VMEM_LIMIT),
         cost_estimate=pl.CostEstimate(
             flops=2 * tokens * width * 3 * width + 8 * tokens * length * width,
@@ -150,10 +216,39 @@
             transcendentals=tokens * length * (width // HEAD),
         ),
         name="attention_forward",
-    )(x, seg, w, bias)
-
-
-def feedforward_kernel(
+    )
+    grid = (row_count // rows_per_step,)
+    matrix_spec = pl.BlockSpec((width, 3 * width), lambda i, *_: (0, 0), pipeline_mode=pl.Buffered(1))
+    if place is None:
+        in_specs += [matrix_spec, pl.BlockSpec((1, 3 * width), lambda i: (0, 0))]
+        return pl.pallas_call(
+            functools.partial(attention_whole_kernel, length, width),
+            grid=grid,
+            in_specs=in_specs,
+            out_specs=out_specs,
+            out_shape=out_shape,
+            **settings,
+        )(x, seg, *weights)
+    spec = pltpu.PrefetchScalarGridSpec(
+        num_scalar_prefetch=1,
+        grid=grid,
+        in_specs=in_specs + [pl.BlockSpec(memory_space=pl.ANY)] * 10,
+        out_specs=out_specs + [pl.BlockSpec((width, 3 * width), lambda i, *_: (0, 0))],
+        scratch_shapes=[
+            pltpu.VMEM((16, SMALL, BLOCK), BF16),
+            pltpu.VMEM((8, 3 * width), F32),
+            pltpu.SemaphoreType.DMA((112,)),
+        ],
+    )
+    return pl.pallas_call(
+        functools.partial(attention_gathered_kernel, length, width),
+        grid_spec=spec,
+        out_shape=out_shape + [jax.ShapeDtypeStruct((width, 3 * width), BF16)],
+        **settings,
+    )(place, x, seg, *weights)
+
+
+def feedforward_rows(
     length,
     chunk,
     x_ref,
@@ -247,64 +342,101 @@
     small_ref[16:24, :] += fold(normed_grad)
 
 
-def feedforward(x, ctx, seg, pooled_grad, out_w, up_w, down_w, vectors, up_bias, rows_per_step=2, chunk=768):
+def feedforward_gathered_kernel(length, chunk, place_ref, x_ref, ctx_ref, seg_ref, pooled_grad_ref, *rest):
+    buffers, outs = rest[:10], rest[10:20]
+    slope_ref, out_w_ref, up_w_ref, down_w_ref, vec_ref, up_bias_ref, gathered_ref, sems = rest[20:]
+    width, hidden = up_w_ref.shape
+    unit = width // 16
+    ratio = hidden // width
+
+    @pl.when(pl.program_id(0) == 0)
+    def _():
+        copies = []
+        for buffer, at, owner, half, first in shard_slots(place_ref):
+            source = buffers[buffer].at[at]
+            rows = pl.ds(aligned(owner, unit), unit)
+            for block in range(ratio):
+                cols = pl.ds(aligned(half * ratio + block, BLOCK), BLOCK)
+                copies.append((source.at[pl.ds(block * unit, unit)], up_w_ref.at[rows, cols]))
+            cols = pl.ds(aligned(half, BLOCK), BLOCK)
+            down_rows = pl.ds(aligned(owner, ratio * unit), ratio * unit)
+            copies.append((source.at[pl.ds(ratio * unit, ratio * unit)], down_w_ref.at[down_rows, cols]))
+            copies.append((source.at[pl.ds(2 * ratio * unit, unit)], out_w_ref.at[rows, cols]))
+            if first:
+                at_small = (2 * ratio + 1) * unit
+                copies.append((source.at[pl.ds(at_small, SMALL)], gathered_ref.at[owner]))
+        run_copies(copies, sems)
+        lane = lax.broadcasted_iota(jnp.int32, (8, width), 1)
+        total = jnp.zeros((8, width), F32)
+        for s in range(16):
+            row = gathered_ref[s].astype(F32)[:8]
+            row = jnp.where(lane < unit, jnp.concatenate([row, row], axis=1), 0.0)
+            total = total + (pltpu.roll(row, s * unit, 1) if s else row)
+        vec_ref[...] = total
+        lane = lax.broadcasted_iota(jnp.int32, (8, BLOCK), 1)
+        for s in range(0, 16, 2):
+            low = gathered_ref[s].astype(F32)[:8]
+            high = gathered_ref[s + 1].astype(F32)[:8]
+            high = pltpu.roll(high, BLOCK // 2, 1)
+            both = jnp.where(lane < BLOCK // 2, low, high)
+            up_bias_ref[:, pl.ds((s // 2) * BLOCK, BLOCK)] = both[6:7, :]
+
+    feedforward_rows(
+        length, chunk, x_ref, ctx_ref, seg_ref, pooled_grad_ref,
+        out_w_ref, up_w_ref, down_w_ref, vec_ref, up_bias_ref, *outs, slope_ref,
+    )
+
+
+def feedforward(x, ctx, seg, pooled_grad, weights, hidden, place=None, rows_per_step=2, chunk=768):
     row_count, length = seg.shape
     tokens, width = x.shape
-    hidden = up_w.shape[1]
     segments = pooled_grad.shape[1]
     block = rows_per_step * length
 
     def tiled(columns):
-        return pl.BlockSpec((block, columns), lambda i: (i, 0))
+        return pl.BlockSpec((block, columns), lambda i, *_: (i, 0))
 
     def whole(shape):
-        return pl.BlockSpec(shape, lambda i: (0,) * len(shape), pipeline_mode=pl.Buffered(1))
+        return pl.BlockSpec(shape, lambda i, *_: (0,) * len(shape), pipeline_mode=pl.Buffered(1))
 
     def kept(shape):
-        return pl.BlockSpec(shape, lambda i: (0,) * len(shape))
+        return pl.BlockSpec(shape, lambda i, *_: (0,) * len(shape))
 
     def rows(columns, dtype):
         return jax.ShapeDtypeStruct((tokens, columns), dtype)
 
-    return pl.pallas_call(
-        functools.partial(feedforward_kernel, length, chunk),
-        grid=(row_count // rows_per_step,),
-        in_specs=[
-            tiled(width),
-            tiled(width),
-            whole((row_count, length)),
-            pl.BlockSpec((rows_per_step, segments, width), lambda i: (i, 0, 0)),
-            whole((width, width)),
-            whole((width, hidden)),
-            whole((hidden, width)),
-            whole((8, width)),
-            whole((1, hidden)),
-        ],
-        out_specs=[
-            pl.BlockSpec((rows_per_step, segments, width), lambda i: (i, 0, 0)),
-            tiled(hidden),
-            tiled(hidden),
-            tiled(width),
-            tiled(width),
-            tiled(width),
-            tiled(width),
-            tiled(width),
-            kept((48, width)),
-            kept((8, hidden)),
-        ],
-        out_shape=[
-            jax.ShapeDtypeStruct((row_count, segments, width), F32),
-            rows(hidden, BF16),
-            rows(hidden, BF16),
-            rows(width, BF16),
-            rows(width, BF16),
-            rows(width, F32),
-            rows(width, BF16),
-            rows(width, BF16),
-            jax.ShapeDtypeStruct((48, width), F32),
-            jax.ShapeDtypeStruct((8, hidden), F32),
-        ],
-        scratch_shapes=[pltpu.VMEM((block, hidden), F32)],
+    grid = (row_count // rows_per_step,)
+    in_specs = [
+        tiled(width),
+        tiled(width),
+        whole((row_count, length)),
+        pl.BlockSpec((rows_per_step, segments, width), lambda i, *_: (i, 0, 0)),
+    ]
+    out_specs = [
+        pl.BlockSpec((rows_per_step, segments, width), lambda i, *_: (i, 0, 0)),
+        tiled(hidden),
+        tiled(hidden),
+        tiled(width),
+        tiled(width),
+        tiled(width),
+        tiled(width),
+        tiled(width),
+        kept((48, width)),
+        kept((8, hidden)),
+    ]
+    out_shape = [
+        jax.ShapeDtypeStruct((row_count, segments, width), F32),
+        rows(hidden, BF16),
+        rows(hidden, BF16),
+        rows(width, BF16),
+        rows(width, BF16),
+        rows(width, F32),
+        rows(width, BF16),
+        rows(width, BF16),
+        jax.ShapeDtypeStruct((48, width), F32),
+        jax.ShapeDtypeStruct((8, hidden), F32),
+    ]
+    settings = dict(
         compiler_params=pltpu.CompilerParams(vmem_limit_bytes=VMEM_LIMIT),
         cost_estimate=pl.CostEstimate(
             flops=tokens * width * (4 * width + 8 * hidden),
@@ -312,7 +444,47 @@
             transcendentals=2 * tokens * hidden,
         ),
         name="feedforward",
-    )(x, ctx, seg, pooled_grad, out_w, up_w, down_w, vectors, up_bias)
+    )
+    slope = pltpu.VMEM((block, hidden), F32)
+    if place is None:
+        in_specs += [
+            whole((width, width)),
+            whole((width, hidden)),
+            whole((hidden, width)),
+            whole((8, width)),
+            whole((1, hidden)),
+        ]
+        return pl.pallas_call(
+            functools.partial(feedforward_rows, length, chunk),
+            grid=grid,
+            in_specs=in_specs,
+            out_specs=out_specs,
+            out_shape=out_shape,
+            scratch_shapes=[slope],
+            **settings,
+        )(x, ctx, seg, pooled_grad, *weights)
+    spec = pltpu.PrefetchScalarGridSpec(
+        num_scalar_prefetch=1,
+        grid=grid,
+        in_specs=in_specs + [pl.BlockSpec(memory_space=pl.ANY)] * 10,
+        out_specs=out_specs,
+        scratch_shapes=[
+            slope,
+            pltpu.VMEM((width, width), BF16),
+            pltpu.VMEM((width, hidden), BF16),
+            pltpu.VMEM((hidden, width), BF16),
+            pltpu.VMEM((8, width), F32),
+            pltpu.VMEM((1, hidden), F32),
+            pltpu.VMEM((16, SMALL, BLOCK), BF16),
+            pltpu.SemaphoreType.DMA((32 * (hidden // width + 2) + 16,)),
+        ],
+    )
+    return pl.pallas_call(
+        functools.partial(feedforward_gathered_kernel, length, chunk),
+        grid_spec=spec,
+        out_shape=out_shape,
+        **settings,
+    )(place, x, ctx, seg, pooled_grad, *weights)
 
 
 def attention_back_kernel(length, width, qkv_ref, grad_ref, seg_ref, out_ref, small_ref):
@@ -383,7 +555,415 @@
     )(qkv, ctx_grad, seg)
 
 
-def body(
+def cut_columns(half_index, shard, out_ref, row_at, blocks):
+    rows = shard.shape[0]
+    for half in range(2):
+
+        @pl.when(half_index == half)
+        def _():
+            for block in range(blocks):
+                cols = pl.ds((half * blocks + block) * BLOCK, BLOCK)
+                out_ref[pl.ds(row_at + block * rows, rows), :] = shard[:, cols]
+
+
+def pack_attention_kernel(place_ref, qkv_ref, small_ref, out_ref):
+    unit = qkv_ref.shape[0]
+    cut_columns(place_ref[0], qkv_ref, out_ref, 0, 3)
+    out_ref[pl.ds(3 * unit, SMALL), :] = small_ref[...]
+
+
+def pack_feedforward_kernel(place_ref, up_ref, down_ref, out_w_ref, small_ref, out_ref):
+    unit = up_ref.shape[0]
+    ratio = down_ref.shape[0] // unit
+    cut_columns(place_ref[0], up_ref, out_ref, 0, ratio)
+    cut_columns(place_ref[0], down_ref, out_ref, ratio * unit, 1)
+    cut_columns(place_ref[0], out_w_ref, out_ref, 2 * ratio * unit, 1)
+    out_ref[pl.ds((2 * ratio + 1) * unit, SMALL), :] = small_ref[...]
+
+
+def pack(kernel, name, place, rows, *shards):
+    spec = pltpu.PrefetchScalarGridSpec(
+        num_scalar_prefetch=1,
+        grid=(1,),
+        in_specs=[pl.BlockSpec(s.shape, lambda i, *_: (0, 0)) for s in shards],
+        out_specs=pl.BlockSpec((rows, BLOCK), lambda i, *_: (0, 0)),
+    )
+    return pl.pallas_call(
+        kernel, grid_spec=spec, out_shape=jax.ShapeDtypeStruct((rows, BLOCK), BF16), name=name
+    )(place, *shards)
+
+
+def store_shards(place_ref, keep_ref, send_ref, plane_z, half, row_at, rows, values):
+    y, z, x, core = place_of(place_ref)
+    turn = (z - plane_z) & 3
+    first = core == 0
+    for plane_x in range(2):
+        even = values(plane_z * 4 + plane_x * 2)
+        odd = values(plane_z * 4 + plane_x * 2 + 1)
+        at = (half ^ y, plane_x ^ x, turn, pl.ds(row_at, rows))
+        keep_ref[at] = jnp.where(first, even, odd)
+        send_ref[at] = jnp.where(first, odd, even)
+
+
+def down_gradient_kernel(place_ref, active_ref, branch_ref, keep_ref, send_ref):
+    grad = transpose_times(active_ref[...], branch_ref[...]).astype(BF16)
+    rows = grad.shape[0] // 4
+    for half in range(2):
+
+        def values(s):
+            return grad[(s % 4) * rows : (s % 4 + 1) * rows, half * BLOCK : (half + 1) * BLOCK]
+
+        y, z, x, core = place_of(place_ref)
+        turn = (z - pl.program_id(0)) & 3
+        first = core == 0
+        for plane_x in range(2):
+            even, odd = values(plane_x * 2), values(plane_x * 2 + 1)
+            at = (half ^ y, plane_x ^ x, turn)
+            keep_ref[at] = jnp.where(first, even, odd)
+            send_ref[at] = jnp.where(first, odd, even)
+
+
+def store_columns(place_ref, keep_ref, send_ref, grad, first_block, blocks):
+    unit = grad.shape[0] // 16
+    for part in range(2):
+        number = first_block + part
+        half = number // blocks
+        row_at = (number - half * blocks) * unit
+        if not isinstance(row_at, int):
+            row_at = pl.multiple_of(row_at, unit)
+
+        def values(s):
+            return grad[s * unit : (s + 1) * unit, part * BLOCK : (part + 1) * BLOCK]
+
+        for plane_z in range(4):
+            store_shards(place_ref, keep_ref, send_ref, plane_z, half, row_at, unit, values)
+
+
+def store_small(place_ref, keep_ref, send_ref, row_at, values):
+    for half in range(2):
+        for plane_z in range(4):
+            store_shards(place_ref, keep_ref, send_ref, plane_z, half, row_at, SMALL, values)
+
+
+def up_gradient_kernel(
+    place_ref, normed_ref, hidden_ref, ctx_ref, attended_ref, sums_ref, up_sums_ref, keep_ref, send_ref, turned_ref
+):
+    step = pl.program_id(0)
+    last = pl.num_programs(0) - 1
+    width = normed_ref.shape[1]
+    unit = width // 16
+    blocks = last
+
+    @pl.when(step == 0)
+    def _():
+        turned_ref[...] = normed_ref[...].T
+
+    @pl.when(step < last)
+    def _():
+        grad = product(turned_ref[...], hidden_ref[...]).astype(BF16)
+        store_columns(place_ref, keep_ref, send_ref, grad, 2 * step, blocks)
+
+    @pl.when(step == last)
+    def _():
+        grad = transpose_times(ctx_ref[...], attended_ref[...]).astype(BF16)
+        steps = up_sums_ref.shape[1] // width
+        for part in range(2):
+
+            def values(s):
+                return grad[s * unit : (s + 1) * unit, part * BLOCK : (part + 1) * BLOCK]
+
+            for plane_z in range(4):
+                store_shards(place_ref, keep_ref, send_ref, plane_z, part, steps * unit, unit, values)
+        row = lax.broadcasted_iota(jnp.int32, (SMALL, width), 0)
+        vectors = jnp.zeros((SMALL, width), F32)
+        for number in range(6):
+            total = jnp.sum(sums_ref[pl.ds(8 * number, 8), :], axis=0, keepdims=True)
+            vectors = jnp.where(row == number, total, vectors)
+        up_total = jnp.sum(up_sums_ref[...], axis=0, keepdims=True)
+        row = row[:, :BLOCK]
+
+        def small(s):
+            rolled = pltpu.roll(vectors, width - s * unit, 1) if s else vectors
+            up = jnp.broadcast_to(up_total[:, (s // 2) * BLOCK : (s // 2 + 1) * BLOCK], (SMALL, BLOCK))
+            up = pltpu.roll(up, BLOCK // 2, 1) if s % 2 else up
+            return jnp.where(row == 6, up, rolled[:, :BLOCK]).astype(BF16)
+
+        store_small(place_ref, keep_ref, send_ref, (steps + 1) * unit, small)
+
+
+def qkv_gradient_kernel(place_ref, x_ref, grad_ref, sums_ref, keep_ref, send_ref, turned_ref):
+    step = pl.program_id(0)
+    width = x_ref.shape[1]
+    unit = width // 16
+
+    @pl.when(step == 0)
+    def _():
+        turned_ref[...] = x_ref[...].T
+        total = jnp.sum(sums_ref[...], axis=0, keepdims=True)
+
+        def small(s):
+            part = total[:, (s // 8) * width : (s // 8 + 1) * width]
+            part = jnp.broadcast_to(part, (SMALL, width))
+            shift = (s % 8) * 2 * unit
+            part = pltpu.roll(part, width - shift, 1) if shift else part
+            return part[:, :BLOCK].astype(BF16)
+
+        store_small(place_ref, keep_ref, send_ref, 3 * unit, small)
+
+    grad = product(turned_ref[...], grad_ref[...]).astype(BF16)
+    store_columns(place_ref, keep_ref, send_ref, grad, 2 * step, 3)
+
+
+def weight_gradient(kernel, name, place, rows, steps, arrays, specs, flops, turned=None):
+    shape = (2, 2, 4, rows, BLOCK)
+    whole = pl.BlockSpec(shape, lambda i, *_: (0,) * 5)
+    spec = pltpu.PrefetchScalarGridSpec(
+        num_scalar_prefetch=1,
+        grid=(steps,),
+        in_specs=specs,
+        out_specs=[whole, whole],
+        scratch_shapes=[] if turned is None else [pltpu.VMEM(turned, BF16)],
+    )
+    return pl.pallas_call(
+        kernel,
+        grid_spec=spec,
+        out_shape=[jax.ShapeDtypeStruct(shape, BF16)] * 2,
+        compiler_params=pltpu.CompilerParams(vmem_limit_bytes=VMEM_LIMIT),
+        cost_estimate=pl.CostEstimate(
+            flops=flops, bytes_accessed=sum(2 * a.size for a in arrays), transcendentals=0
+        ),
+        name=name,
+    )(place, *arrays)
+
+
+def resident(shape):
+    return pl.BlockSpec(shape, lambda i, *_: (0,) * len(shape), pipeline_mode=pl.Buffered(1))
+
+
+def input_gradient_kernel(first_ref, grad_ref, w_ref, out_ref):
+    out_ref[...] = first_ref[...] + times_transpose(grad_ref[...], w_ref[...])
+
+
+def input_gradient(first_grad, qkv_grad, matrix, rows=512):
+    tokens, width = first_grad.shape
+    return pl.pallas_call(
+        input_gradient_kernel,
+        grid=(tokens // rows,),
+        in_specs=[
+            pl.BlockSpec((rows, width), lambda i: (i, 0)),
+            pl.BlockSpec((rows, 3 * width), lambda i: (i, 0)),
+            resident(matrix.shape),
+        ],
+        out_specs=pl.BlockSpec((rows, width), lambda i: (i, 0)),
+        out_shape=jax.ShapeDtypeStruct((tokens, width), F32),
+        compiler_params=pltpu.CompilerParams(vmem_limit_bytes=VMEM_LIMIT),
+        cost_estimate=pl.CostEstimate(
+            flops=6 * tokens * width * width, bytes_accessed=14 * tokens * width, transcendentals=0
+        ),
+        name="input_gradient",
+    )(first_grad, qkv_grad, matrix)
+
+
+AXES = ("dp", "fsdp")
+DEVICES = 32
+
+
+def across(value, mask):
+    return lax.ppermute(value, AXES, [(i, i ^ mask) for i in range(DEVICES)])
+
+
+def along_z(value, distance):
+    def target(i):
+        return i - i % 16 + (i % 16 + 4 * distance) % 16
+
+    return lax.ppermute(value, AXES, [(i, target(i)) for i in range(DEVICES)])
+
+
+CORE, X, Y = 1, 2, 16
+
+
+def gather_shards(own):
+    turned = [along_z(own, d) for d in (1, 2, 3)]
+    here = jnp.stack([own] + turned)
+    from_x = across(here, X)
+    from_y = across(here, Y)
+    diagonal_low = across(from_x[:2], Y)
+    diagonal_high = across(from_y[2:], X)
+    mine = (here, from_x, from_y, diagonal_low, diagonal_high)
+    return mine + tuple(across(piece, CORE) for piece in mine)
+
+
+def reduce_shards(keep, send):
+    def wide(value):
+        return value.astype(F32)
+
+    got = across(send, CORE)
+
+    def pair(at):
+        return wide(keep[at]) + wide(got[at])
+
+    low, high = slice(0, 2), slice(2, 4)
+    every = slice(None)
+    low_x = across(pair((every, 1, low)).astype(BF16), X)
+    high_y = across(pair((1, every, high)).astype(BF16), Y)
+    low_y = across((pair((1, 0, low)) + wide(low_x[1])).astype(BF16), Y)
+    high_x = across((pair((0, 1, high)) + wide(high_y[1])).astype(BF16), X)
+    low_sum = pair((0, 0, low)) + wide(low_x[0]) + wide(low_y)
+    high_sum = pair((0, 0, high)) + wide(high_y[0]) + wide(high_x)
+    total = low_sum[0]
+    for turn in (1, 2, 3):
+        part = low_sum[1] if turn == 1 else high_sum[turn - 2]
+        total = total + wide(along_z(part.astype(BF16), 4 - turn))
+    return total
+
+
+def both_halves(mine, y):
+    theirs = across(mine.astype(BF16), Y).astype(F32)
+    swap = y == 0
+    return jnp.where(swap, mine, theirs), jnp.where(swap, theirs, mine)
+
+
+def join_columns(halves, unit, blocks):
+    parts = []
+    for half in halves:
+        cols = half.reshape(blocks, unit, BLOCK)
+        parts += [cols[b] for b in range(blocks)]
+    return jnp.concatenate(parts, axis=1)
+
+
+def rows_of(vectors, rows):
+    padded = [jnp.pad(v, (0, BLOCK - v.shape[0])) for v in vectors]
+    padded += [jnp.zeros((BLOCK,), BF16)] * (rows - len(padded))
+    return jnp.stack(padded)
+
+
+def body_by_permutes(
+    hidden_in,
+    segment_ids,
+    pooled_grad,
+    qkv_weight,
+    qv_bias,
+    out_weight,
+    out_bias,
+    first_gain,
+    first_shift,
+    up_weight,
+    up_bias,
+    down_weight,
+    down_bias,
+    second_gain,
+    second_shift,
+):
+    row_count, length, width = hidden_in.shape
+    tokens = row_count * length
+    x = hidden_in.reshape(tokens, width)
+    unit = qkv_weight.shape[0]
+    hidden = up_weight.shape[1]
+    ratio = hidden // width
+    y, shard = lax.axis_index("dp"), lax.axis_index("fsdp")
+    place = jnp.stack([y, shard // 4, shard // 2 % 2, shard % 2]).astype(jnp.int32)
+
+    attention_rows_count = 3 * unit + SMALL
+    feedforward_rows_count = (2 * ratio + 1) * unit + SMALL
+    own_attention = pack(
+        pack_attention_kernel,
+        "pack_attention",
+        place,
+        attention_rows_count,
+        qkv_weight,
+        rows_of([qv_bias], SMALL),
+    )
+    own_feedforward = pack(
+        pack_feedforward_kernel,
+        "pack_feedforward",
+        place,
+        feedforward_rows_count,
+        up_weight,
+        down_weight,
+        out_weight,
+        rows_of([out_bias, first_gain, first_shift, down_bias, second_gain, second_shift, up_bias], SMALL),
+    )
+    attention_pieces = gather_shards(own_attention)
+    feedforward_pieces = gather_shards(own_feedforward)
+    qkv, ctx, qkv_matrix = attention_forward(x, segment_ids, attention_pieces, place)
+    pooled, active, hidden_grad, normed, branch, first_grad, attended, ctx_grad, sums, up_sums = feedforward(
+        x, ctx, segment_ids, pooled_grad, feedforward_pieces, hidden, place
+    )
+    down_keep, down_send = weight_gradient(
+        down_gradient_kernel,
+        "down_gradient",
+        place,
+        ratio * unit,
+        4,
+        (active, branch),
+        [pl.BlockSpec((tokens, hidden // 4), lambda i, *_: (0, i)), resident((tokens, width))],
+        2 * tokens * hidden * width,
+    )
+    down_total = reduce_shards(down_keep, down_send)
+    up_keep, up_send = weight_gradient(
+        up_gradient_kernel,
+        "up_gradient",
+        place,
+        (ratio + 1) * unit + SMALL,
+        ratio + 1,
+        (normed, hidden_grad, ctx, attended, sums, up_sums),
+        [
+            resident((tokens, width)),
+            pl.BlockSpec((tokens, width), lambda i, *_: (0, jnp.minimum(i, ratio - 1))),
+            resident((tokens, width)),
+            resident((tokens, width)),
+            resident(sums.shape),
+            resident(up_sums.shape),
+        ],
+        2 * tokens * width * (hidden + width),
+        (width, tokens),
+    )
+    up_total = reduce_shards(up_keep, up_send)
+    qkv_grad, qv_sums = attention_backward(qkv, ctx_grad, segment_ids)
+    qkv_keep, qkv_send = weight_gradient(
+        qkv_gradient_kernel,
+        "qkv_gradient",
+        place,
+        3 * unit + SMALL,
+        3,
+        (x, qkv_grad, qv_sums),
+        [
+            resident((tokens, width)),
+            pl.BlockSpec((tokens, width), lambda i, *_: (0, i)),
+            resident(qv_sums.shape),
+        ],
+        6 * tokens * width * width,
+        (width, tokens),
+    )
+    qkv_total = reduce_shards(qkv_keep, qkv_send)
+    grad_input = input_gradient(first_grad, qkv_grad, qkv_matrix)
+
+    grad_down = jnp.concatenate(both_halves(down_total, y), axis=1)
+    up_part, up_small = up_total[: (ratio + 1) * unit], up_total[(ratio + 1) * unit :]
+    up_low, up_high = both_halves(up_part, y)
+    grad_up = join_columns((up_low[: ratio * unit], up_high[: ratio * unit]), unit, ratio)
+    grad_out = join_columns((up_low[ratio * unit :], up_high[ratio * unit :]), unit, 1)
+    qkv_part, qkv_small = qkv_total[: 3 * unit], qkv_total[3 * unit :]
+    grad_qkv = join_columns(both_halves(qkv_part, y), unit, 3)
+    return (
+        pooled,
+        grad_input.reshape(row_count, length, width),
+        grad_qkv,
+        qkv_small[0, : 2 * unit],
+        grad_out,
+        up_small[0, :unit],
+        up_small[1, :unit],
+        up_small[2, :unit],
+        grad_up,
+        up_small[6, : ratio * unit],
+        grad_down,
+        up_small[3, :unit],
+        up_small[4, :unit],
+        up_small[5, :unit],
+    )
+
+
+def body_by_collectives(
     hidden_in,
     segment_ids,
     pooled_grad,
@@ -422,9 +1002,9 @@
     out_matrix = gather(out_weight)
     up_matrix = gather(up_weight)
     down_matrix = gather(down_weight)
-    qkv, ctx = attention_forward(x, segment_ids, qkv_matrix, qkv_bias)
+    qkv, ctx = attention_forward(x, segment_ids, (qkv_matrix, qkv_bias))
     pooled, active, hidden_grad, normed, branch, first_grad, attended, ctx_grad, sums, up_sums = feedforward(
-        x, ctx, segment_ids, pooled_grad, out_matrix, up_matrix, down_matrix, vectors, ub
+        x, ctx, segment_ids, pooled_grad, (out_matrix, up_matrix, down_matrix, vectors, ub), up_matrix.shape[1]
     )
 
     def scatter(grad):
@@ -500,4 +1080,5 @@
         P("fsdp"),
         P("fsdp"),
     )
+    body = body_by_permutes if dict(mesh.shape) == {"dp": 2, "fsdp": 16} else body_by_collectives
     return jax.shard_map(body, mesh=mesh, in_specs=in_specs, out_specs=out_specs, check_vma=False)

time: 662 us -> 431 us (0.65); the launches traced: 653 us -> 431 us
  blocking collectives: 164 us -> 0 us
  waiting for transfers between devices: 256 us -> 136 us
  Pallas kernels: 134 us -> 213 us
  matrix products: 60 us -> 0 us
  starting transfers between devices: 0.32 us -> 52.6 us
  between operations: 15.4 us -> 1.27 us
  other arithmetic: 0.71 us -> 14.2 us
  local copies, waits for them, and re-layouts: 21.8 us -> 13.6 us
    reduce_scatter x3 -> x0, waiting for transfers between devices: 149 us -> none  [scatter(): lax.psum_scatter(grad.astype(BF16), 'fsdp', scatter_dimension=0, tiled=True)]
    ppermute x0 -> x51, waiting for transfers between devices: none -> 136 us  [the longest x36 89.1 us: across(): return lax.ppermute(value, AXES, [(i, i ^ mask) for i in range(DEVICES)])]
    all_gather x4 -> x0, waiting for transfers between devices: 105 us -> none  [gather(): return lax.all_gather(shard, 'fsdp', axis=0, tiled=True)]
    psum x2 -> x0, blocking collectives: 101 us -> none  [the longest x1 60.1 us: body(): lax.psum(tuple((g.astype(F32) for g in (grad_qkv, grad_out, grad_up, grad...]
    pallas_call x2 -> x8, Pallas kernels: 104 us -> 183 us  [the longest x1 87.8 us: feedforward(): pl.pallas_call(functools.partial(feedforward_gathered_kernel, length, chu...]
    unnamed x1 -> x0, blocking collectives: 63.3 us -> none
    dot_general x5 -> x0, matrix products: 60 us -> none  [the longest x4 46.2 us: transpose_times(): lax.dot_general(left, right, (((0,), (0,)), ((), ())), preferred_element_...]
    ppermute x0 -> x51, starting transfers between devices: none -> 52.6 us  [the longest x36 30.6 us: across(): return lax.ppermute(value, AXES, [(i, i ^ mask) for i in range(DEVICES)])]
  transfers between devices with their start and end apart: 8 -> 51, of which waited for: 4 -> 25; matrix products, arithmetic and copies ran while one was open for 11% -> 4% of each run, Pallas kernels for 8% -> 18%
where the time goes in v2:
time: 431 us
  Pallas kernels  213 us (49%)
  waiting for transfers between devices  136 us (32%)
  starting transfers between devices  52.6 us (12%)
  other arithmetic  14.2 us (3%)
  local copies, waits for them, and re-layouts  13.6 us (3%)
    ppermute x36, waiting for transfers between devices, across(): return lax.ppermute(value, AXES, [(i, i ^ mask) for i in range(DEVICES)])  89.1 us
    pallas_call x1, Pallas kernels, feedforward(): pl.pallas_call(functools.partial(feedforward_gathered_kernel, length, chu...  87.8 us
    pallas_call x3, Pallas kernels, weight_gradient(): pl.pallas_call(kernel, grid_spec=spec, out_shape=[jax.ShapeDtypeStruct(sh...  53.4 us
    ppermute x15, waiting for transfers between devices, along_z(): return lax.ppermute(value, AXES, [(i, target(i)) for i in range(DEVICES)])  46.8 us
    ppermute x36, starting transfers between devices, across(): return lax.ppermute(value, AXES, [(i, i ^ mask) for i in range(DEVICES)])  30.6 us
    pallas_call x1, Pallas kernels, attention_backward(): pl.pallas_call(functools.partial(attention_back_kernel, length, width), g...  30.2 us
    pallas_call x1, Pallas kernels, attention_forward(): pl.pallas_call(functools.partial(attention_gathered_kernel, length, width...  23 us
    ppermute x15, starting transfers between devices, along_z(): return lax.ppermute(value, AXES, [(i, target(i)) for i in range(DEVICES)])  22 us
  transfers between devices with their start and end apart: 51, of which 25 were waited for; matrix products, arithmetic and copies ran while one was open for 4% of the time, Pallas kernels for 18%

profile of v2, /device:TPU:0, one launch (start us, length us, event | category | flops | bytes accessed | tf_op | source)
XLA Modules:
  0.0 430.6 jit_solution(13396760879933568738)
XLA Ops:
  7.2 2.5 pack_feedforward.1
  9.7 5.0 %collective-permute-start.14 = (bf16[448,384]{1,0:T(8,128)(2,1)}, bf16[448,384]{1,0:T(8,128)(2,1)S(1)}, u32[]{:S(2)}, u32[]{:S(2)}) collective-permute-start(bf16[448,384]{1,0:T(8,128)(2,1)} %pack_feedforward.1), channel_id=1, source_target_pairs={{0,12},{1,13},{2,14},{3,15},{4,0},{5,1},{6,2},{7,3},{8,4},{9,5},{1... | collective-permute-start | bytes 1032200 | tf_op jit(solution)/shard_map/ppermute | solution.py:779
  15.8 7.8 %collective-permute-done.14 = bf16[448,384]{1,0:T(8,128)(2,1)S(1)} collective-permute-done((bf16[448,384]{1,0:T(8,128)(2,1)}, bf16[448,384]{1,0:T(8,128)(2,1)S(1)}, u32[]{:S(2)}, u32[]{:S(2)}) %collective-permute-start.14) | collective-permute-done | bytes 344096 | tf_op jit(solution)/shard_map/ppermute | solution.py:779
  23.6 20.7 %collective-permute-done.13 = bf16[448,384]{1,0:T(8,128)(2,1)S(1)} collective-permute-done((bf16[448,384]{1,0:T(8,128)(2,1)}, bf16[448,384]{1,0:T(8,128)(2,1)S(1)}, u32[]{:S(2)}, u32[]{:S(2)}) %collective-permute-start.13) | collective-permute-done | bytes 344096 | tf_op jit(solution)/shard_map/ppermute | solution.py:779
  45.5 1.6 collective-permute-start.16
  47.1 1.5 collective-permute-start.15
  49.8 2.3 pack_attention.1
  52.1 2.8 collective-permute-start.1
  54.9 2.0 collective-permute-start
  58.2 7.0 %collective-permute-done.1 = bf16[160,384]{1,0:T(8,128)(2,1)S(1)} collective-permute-done((bf16[160,384]{1,0:T(8,128)(2,1)}, bf16[160,384]{1,0:T(8,128)(2,1)S(1)}, u32[]{:S(2)}, u32[]{:S(2)}) %collective-permute-start.1) | collective-permute-done | bytes 122912 | tf_op jit(solution)/shard_map/ppermute | solution.py:779
  67.3 19.9 %collective-permute-done.4.rest_2_ = bf16[4,160,384]{2,1,0:T(8,128)(2,1)S(1)} collective-permute-done((bf16[4,160,384]{2,1,0:T(8,128)(2,1)S(1)}, bf16[4,160,384]{2,1,0:T(8,128)(2,1)S(1)}, u32[]{:S(2)}, u32[]{:S(2)}) %collective-permute-start.4) | collective-permute-done | bytes 491552 | tf_op jit(solution)/shard_map/ppermute | solution.py:772
  87.2 1.6 collective-permute-start.6
  88.8 1.5 collective-permute-start.5
  90.3 3.3 collective-permute-done.6.rest_4_
  93.6 1.5 collective-permute-done.5.rest_3_
  98.1 1.6 collective-permute-start.18
  102.1 13.9 %collective-permute-done.18.rest_4_ = bf16[2,448,384]{2,1,0:T(8,128)(2,1)} collective-permute-done((bf16[2,448,384]{2,1,0:T(8,128)(2,1)S(1)}, bf16[2,448,384]{2,1,0:T(8,128)(2,1)}, u32[]{:S(2)}, u32[]{:S(2)}) %collective-permute-start.18) | collective-permute-done | bytes 688160 | tf_op jit(solution)/shard_map/ppermute | solution.py:772
  117.2 23.0 %attention_forward.1 = (bf16[2048,2304]{1,0:T(8,128)(2,1)}, bf16[2048,768]{1,0:T(8,128)(2,1)}, bf16[768,2304]{1,0:T(8,128)(2,1)}) custom-call(s32[4]{0:T(128)} %pad_add_fusion.place_ref, bf16[2048,768]{1,0:T(8,128)(2,1)} %bitcast.189, s32[16,128]{1,0:T(8,128)} %seg_ref.5, bf16[4,160,384]{2,1,0:T(8,128)(2,1)} %copy-done.3, bf16[4,160,384]{2,1,0:T(8,128)(2,1)} %copy-done.5, ...), custom_call_target="tpu_custom_call" | custom-call | flops 8858370048 | bytes 19267584 | tf_op jit(solution)/shard_map/attention_forward/pallas_call | solution.py:243
  141.3 87.8 %feedforward.1 = (f32[16,4,768]{2,1,0:T(4,128)}, bf16[2048,3072]{1,0:T(8,128)(2,1)}, bf16[2048,3072]{1,0:T(8,128)(2,1)}, bf16[2048,768]{1,0:T(8,128)(2,1)}, bf16...) custom-call(s32[4]{0:T(128)} %pad_add_fusion.place_ref, ...), custom_call_target="tpu_custom_call" | custom-call | flops 43486543872 | bytes 62914560 | tf_op jit(solution)/shard_map/feedforward/pallas_call | solution.py:482
  229.2 30.2 %attention_backward.1 = (bf16[2048,2304]{1,0:T(8,128)(2,1)}, f32[8,1536]{1,0:T(8,128)}) custom-call(bf16[2048,2304]{1,0:T(8,128)(2,1)} %get-tuple-element.38.qkv_ref, bf16[2048,768]{1,0:T(8,128)(2,1)} %get-tuple-element.39.grad_ref, s32[16,128]{1,0:T(8,128)} %seg_ref.5), custom_call_target="tpu_custom_call" | custom-call | flops 4026531840 | bytes 22020096 | tf_op jit(solution)/shard_map/attention_backward/pallas_call | solution.py:532
  259.4 14.4 %qkv_gradient.1 = (bf16[2,2,4,160,384]{4,3,2,1,0:T(8,128)(2,1)}, bf16[2,2,4,160,384]{4,3,2,1,0:T(8,128)(2,1)}) custom-call(s32[4]{0:T(128)} %pad_add_fusion.place_ref, bf16[2048,768]{1,0:T(8,128)(2,1)} %bitcast.191, bf16[2048,2304]{1,0:T(8,128)(2,1)} %get-tuple-element.40.grad_ref, f32[8,1536]{1,0:T(8,128)} %get-tuple-element.42.sums_ref), custom_call_target="tpu_custom_call" | custom-call | flops 7247757312 | bytes 12607488 | tf_op jit(solution)/shard_map/qkv_gradient/pallas_call | solution.py:727
  274.3 16.5 %down_gradient.1 = (bf16[2,2,4,192,384]{4,3,2,1,0:T(8,128)(2,1)}, bf16[2,2,4,192,384]{4,3,2,1,0:T(8,128)(2,1)}) custom-call(s32[4]{0:T(128)} %pad_add_fusion.place_ref, bf16[2048,3072]{1,0:T(8,128)(2,1)} %get-tuple-element.52.active_ref, bf16[2048,768]{1,0:T(8,128)(2,1)} %get-tuple-element.53.branch_ref), custom_call_target="tpu_custom_call" | custom-call | flops 9663676416 | bytes 15728640 | tf_op jit(solution)/shard_map/down_gradient/pallas_call | solution.py:727
  290.8 22.5 %up_gradient.1 = (bf16[2,2,4,256,384]{4,3,2,1,0:T(8,128)(2,1)}, bf16[2,2,4,256,384]{4,3,2,1,0:T(8,128)(2,1)}) custom-call(s32[4]{0:T(128)} %pad_add_fusion.place_ref, bf16[2048,768]{1,0:T(8,128)(2,1)} %get-tuple-element.45.normed_ref, bf16[2048,3072]{1,0:T(8,128)(2,1)} %get-tuple-element.46.hidden_ref, bf16[2048,768]{1,0:T(8,128)(2,1)} %get-tuple-element.35.ctx_ref, ...), custom_call_target="tpu_custom_call" | custom-call | flops 12079595520 | bytes 22142976 | tf_op jit(solution)/shard_map/up_gradient/pallas_call | solution.py:727
  313.8 2.1 fusion.15
  316.3 13.8 %input_gradient.1 = f32[2048,768]{1,0:T(8,128)} custom-call(f32[2048,768]{1,0:T(8,128)} %get-tuple-element.37.first_ref, bf16[2048,2304]{1,0:T(8,128)(2,1)} %get-tuple-element.40.grad_ref, bf16[768,2304]{1,0:T(8,128)(2,1)} %get-tuple-element.41.w_ref), custom_call_target="tpu_custom_call" | custom-call | flops 7247757312 | bytes 22020096 | tf_op jit(solution)/shard_map/input_gradient/pallas_call | solution.py:749
  330.2 1.4 fusion.14
  331.6 1.6 collective-permute-start.25
  335.2 1.6 collective-permute-start.43
  336.8 9.0 %collective-permute-done.25 = bf16[2,2,160,384]{3,2,1,0:T(8,128)(2,1)S(1)} collective-permute-done((bf16[2,2,160,384]{3,2,1,0:T(8,128)(2,1)S(1)}, bf16[2,2,160,384]{3,2,1,0:T(8,128)(2,1)S(1)}, u32[]{:S(2)}, u32[]{:S(2)}) %collective-permute-start.25) | collective-permute-done | bytes 491552 | tf_op jit(solution)/shard_map/ppermute | solution.py:772
  345.8 5.3 %collective-permute-done.29 = bf16[2,160,384]{2,1,0:T(8,128)(2,1)S(1)} collective-permute-done((bf16[2,160,384]{2,1,0:T(8,128)(2,1)S(1)}, bf16[2,160,384]{2,1,0:T(8,128)(2,1)S(1)}, u32[]{:S(2)}, u32[]{:S(2)}) %collective-permute-start.29) | collective-permute-done | bytes 245792 | tf_op jit(solution)/shard_map/ppermute | solution.py:772
  351.1 1.6 fusion.18
  352.7 1.6 collective-permute-start.26
  355.0 3.1 collective-permute-start.30
  358.2 3.5 collective-permute-done.26
  364.1 2.6 collective-permute-start.27
  366.8 1.6 collective-permute-start.44
  370.3 1.5 collective-permute-start.32
  373.4 1.6 collective-permute-start.37
  374.9 8.0 %collective-permute-done.32 = bf16[144,384]{1,0:T(8,128)(2,1)S(1)} collective-permute-done((bf16[144,384]{1,0:T(8,128)(2,1)S(1)}, bf16[144,384]{1,0:T(8,128)(2,1)S(1)}, u32[]{:S(2)}, u32[]{:S(2)}) %collective-permute-start.32) | collective-permute-done | bytes 110624 | tf_op jit(solution)/shard_map/ppermute | solution.py:772
  383.4 1.6 collective-permute-start.47
  385.1 11.9 %collective-permute-done.37 = bf16[2,2,256,384]{3,2,1,0:T(8,128)(2,1)S(1)} collective-permute-done((bf16[2,2,256,384]{3,2,1,0:T(8,128)(2,1)S(1)}, bf16[2,2,256,384]{3,2,1,0:T(8,128)(2,1)S(1)}, u32[]{:S(2)}, u32[]{:S(2)}) %collective-permute-start.37) | collective-permute-done | bytes 786464 | tf_op jit(solution)/shard_map/ppermute | solution.py:772
  398.3 3.1 collective-permute-start.48
  401.5 3.9 collective-permute-done.38
  406.7 2.0 collective-permute-done.49
  408.8 2.6 collective-permute-start.50
  411.6 3.1 collective-permute-done.35
  417.2 5.5 %collective-permute-done.39 = bf16[256,384]{1,0:T(8,128)(2,1)S(1)} collective-permute-done((bf16[256,384]{1,0:T(8,128)(2,1)S(1)}, bf16[256,384]{1,0:T(8,128)(2,1)S(1)}, u32[]{:S(2)}, u32[]{:S(2)}) %collective-permute-start.39) | collective-permute-done | bytes 196640 | tf_op jit(solution)/shard_map/ppermute | solution.py:779
  425.6 3.9 collective-permute-done.41
  (176 shorter events, 41.0 us)
Async XLA Ops:
  9.7 13.9 %collective-permute-start.14 = (bf16[448,384]{1,0:T(8,128)(2,1)}, bf16[448,384]{1,0:T(8,128)(2,1)S(1)}, u32[]{:S(2)}, u32[]{:S(2)}) collective-permute-start(bf16[448,384]{1,0:T(8,128)(2,1)} %pack_feedforward.1), channel_id=1, source_target_pairs={{0,12},{1,13},{2,14},{3,15},{4,0},{5,1},{6,2},{7,3},{8,4},{9,5},{1... | collective-permute-start | bytes 1032200 | tf_op jit(solution)/shard_map/ppermute | solution.py:779
  14.7 29.5 %collective-permute-start.13 = (bf16[448,384]{1,0:T(8,128)(2,1)}, bf16[448,384]{1,0:T(8,128)(2,1)S(1)}, u32[]{:S(2)}, u32[]{:S(2)}) collective-permute-start(bf16[448,384]{1,0:T(8,128)(2,1)} %pack_feedforward.1), channel_id=1, source_target_pairs={{0,8},{1,9},{2,10},{3,11},{4,12},{5,13},{6,14},{7,15},{8,0},{9,1},... | collective-permute-start | bytes 1032200 | tf_op jit(solution)/shard_map/ppermute | solution.py:779
  14.7 29.5 %collective-permute-start.12 = (bf16[448,384]{1,0:T(8,128)(2,1)}, bf16[448,384]{1,0:T(8,128)(2,1)S(1)}, u32[]{:S(2)}, u32[]{:S(2)}) collective-permute-start(bf16[448,384]{1,0:T(8,128)(2,1)} %pack_feedforward.1), channel_id=1, source_target_pairs={{0,4},{1,5},{2,6},{3,7},{4,8},{5,9},{6,10},{7,11},{8,12},{9,13},{1... | collective-permute-start | bytes 1032200 | tf_op jit(solution)/shard_map/ppermute | solution.py:779
  45.5 49.6 %collective-permute-start.16 = (bf16[4,448,384]{2,1,0:T(8,128)(2,1)S(1)}, bf16[4,448,384]{2,1,0:T(8,128)(2,1)}, u32[]{:S(2)}, u32[]{:S(2)}) collective-permute-start(bf16[4,448,384]{2,1,0:T(8,128)(2,1)S(1)} %pad_maximum_fusion.rest_0_), channel_id=1, source_target_pairs={{0,16},{1,17},{2,18},{3,19},{4,20},{5,21},{6,22},{7,23},{8,24},{9,... | collective-permute-start | bytes 4128776 | tf_op jit(solution)/shard_map/ppermute | solution.py:772
  47.1 48.5 %collective-permute-start.15 = (bf16[4,448,384]{2,1,0:T(8,128)(2,1)S(1)}, bf16[4,448,384]{2,1,0:T(8,128)(2,1)}, u32[]{:S(2)}, u32[]{:S(2)}) collective-permute-start(bf16[4,448,384]{2,1,0:T(8,128)(2,1)S(1)} %pad_maximum_fusion.rest_0_), channel_id=1, source_target_pairs={{0,2},{1,3},{2,0},{3,1},{4,6},{5,7},{6,4},{7,5},{8,10},{9,11},{10,... | collective-permute-start | bytes 4128776 | tf_op jit(solution)/shard_map/ppermute | solution.py:772
  52.1 6.1 %collective-permute-start.2 = (bf16[160,384]{1,0:T(8,128)(2,1)}, bf16[160,384]{1,0:T(8,128)(2,1)S(1)}, u32[]{:S(2)}, u32[]{:S(2)}) collective-permute-start(bf16[160,384]{1,0:T(8,128)(2,1)} %pack_attention.1), channel_id=1, source_target_pairs={{0,12},{1,13},{2,14},{3,15},{4,0},{5,1},{6,2},{7,3},{8,4},{9,5},{1... | collective-permute-start | bytes 368648 | tf_op jit(solution)/shard_map/ppermute | solution.py:779
  52.1 13.1 %collective-permute-start.1 = (bf16[160,384]{1,0:T(8,128)(2,1)}, bf16[160,384]{1,0:T(8,128)(2,1)S(1)}, u32[]{:S(2)}, u32[]{:S(2)}) collective-permute-start(bf16[160,384]{1,0:T(8,128)(2,1)} %pack_attention.1), channel_id=1, source_target_pairs={{0,8},{1,9},{2,10},{3,11},{4,12},{5,13},{6,14},{7,15},{8,0},{9,1},... | collective-permute-start | bytes 368648 | tf_op jit(solution)/shard_map/ppermute | solution.py:779
  54.9 10.3 %collective-permute-start = (bf16[160,384]{1,0:T(8,128)(2,1)}, bf16[160,384]{1,0:T(8,128)(2,1)S(1)}, u32[]{:S(2)}, u32[]{:S(2)}) collective-permute-start(bf16[160,384]{1,0:T(8,128)(2,1)} %pack_attention.1), channel_id=1, source_target_pairs={{0,4},{1,5},{2,6},{3,7},{4,8},{5,9},{6,10},{7,11},{8,12},{9,13},{1... | collective-permute-start | bytes 368648 | tf_op jit(solution)/shard_map/ppermute | solution.py:779
  66.1 21.0 %collective-permute-start.4 = (bf16[4,160,384]{2,1,0:T(8,128)(2,1)S(1)}, bf16[4,160,384]{2,1,0:T(8,128)(2,1)S(1)}, u32[]{:S(2)}, u32[]{:S(2)}) collective-permute-start(bf16[4,160,384]{2,1,0:T(8,128)(2,1)S(1)} %pad_maximum_fusion.2.rest_0_), channel_id=1, source_target_pairs={{0,16},{1,17},{2,18},{3,19},{4,20},{5,21},{6,22},{7,23},{8,24},{9,... | collective-permute-start | bytes 1474568 | tf_op jit(solution)/shard_map/ppermute | solution.py:772
  66.7 22.1 %collective-permute-start.3 = (bf16[4,160,384]{2,1,0:T(8,128)(2,1)S(1)}, bf16[4,160,384]{2,1,0:T(8,128)(2,1)S(1)}, u32[]{:S(2)}, u32[]{:S(2)}) collective-permute-start(bf16[4,160,384]{2,1,0:T(8,128)(2,1)S(1)} %pad_maximum_fusion.2.rest_0_), channel_id=1, source_target_pairs={{0,2},{1,3},{2,0},{3,1},{4,6},{5,7},{6,4},{7,5},{8,10},{9,11},{10,... | collective-permute-start | bytes 1474568 | tf_op jit(solution)/shard_map/ppermute | solution.py:772
  87.2 6.5 %collective-permute-start.6 = (bf16[2,160,384]{2,1,0:T(8,128)(2,1)S(1)}, bf16[2,160,384]{2,1,0:T(8,128)(2,1)S(1)}, u32[]{:S(2)}, u32[]{:S(2)}) collective-permute-start(bf16[2,160,384]{2,1,0:T(8,128)(2,1)S(1)} %slice.404), channel_id=1, source_target_pairs={{0,2},{1,3},{2,0},{3,1},{4,6},{5,7},{6,4},{7,5},{8,10},{9,11},{10,... | collective-permute-start | bytes 737288 | tf_op jit(solution)/shard_map/ppermute | solution.py:772
  88.8 6.3 %collective-permute-start.5 = (bf16[2,160,384]{2,1,0:T(8,128)(2,1)S(1)}, bf16[2,160,384]{2,1,0:T(8,128)(2,1)S(1)}, u32[]{:S(2)}, u32[]{:S(2)}) collective-permute-start(bf16[2,160,384]{2,1,0:T(8,128)(2,1)S(1)} %slice.403), channel_id=1, source_target_pairs={{0,16},{1,17},{2,18},{3,19},{4,20},{5,21},{6,22},{7,23},{8,24},{9,... | collective-permute-start | bytes 737288 | tf_op jit(solution)/shard_map/ppermute | solution.py:772
  90.3 7.7 %collective-permute-start.7 = (bf16[4,160,384]{2,1,0:T(8,128)(2,1)S(1)}, bf16[4,160,384]{2,1,0:T(8,128)(2,1)S(1)}, u32[]{:S(2)}, u32[]{:S(2)}) collective-permute-start(bf16[4,160,384]{2,1,0:T(8,128)(2,1)S(1)} %pad_maximum_fusion.2.rest_0_), channel_id=1, source_target_pairs={{0,1},{1,0},{2,3},{3,2},{4,5},{5,4},{6,7},{7,6},{8,9},{9,8},{10,11... | collective-permute-start | bytes 1474568 | tf_op jit(solution)/shard_map/ppermute | solution.py:772
  93.6 6.0 %collective-permute-start.9 = (bf16[4,160,384]{2,1,0:T(8,128)(2,1)S(1)}, bf16[4,160,384]{2,1,0:T(8,128)(2,1)S(1)}, u32[]{:S(2)}, u32[]{:S(2)}) collective-permute-start(bf16[4,160,384]{2,1,0:T(8,128)(2,1)S(1)} %collective-permute-done.4.rest_2_), channel_id=1, source_target_pairs={{0,1},{1,0},{2,3},{3,2},{4,5},{5,4},{6,7},{7,6},{8,9},{9,8},{10,11... | collective-permute-start | bytes 1474568 | tf_op jit(solution)/shard_map/ppermute | solution.py:772
  98.1 18.0 %collective-permute-start.18 = (bf16[2,448,384]{2,1,0:T(8,128)(2,1)S(1)}, bf16[2,448,384]{2,1,0:T(8,128)(2,1)}, u32[]{:S(2)}, u32[]{:S(2)}) collective-permute-start(bf16[2,448,384]{2,1,0:T(8,128)(2,1)S(1)} %slice.406), channel_id=1, source_target_pairs={{0,2},{1,3},{2,0},{3,1},{4,6},{5,7},{6,4},{7,5},{8,10},{9,11},{10,... | collective-permute-start | bytes 2064392 | tf_op jit(solution)/shard_map/ppermute | solution.py:772
  99.6 17.6 %collective-permute-start.17 = (bf16[2,448,384]{2,1,0:T(8,128)(2,1)S(1)}, bf16[2,448,384]{2,1,0:T(8,128)(2,1)}, u32[]{:S(2)}, u32[]{:S(2)}) collective-permute-start(bf16[2,448,384]{2,1,0:T(8,128)(2,1)S(1)} %slice.405), channel_id=1, source_target_pairs={{0,16},{1,17},{2,18},{3,19},{4,20},{5,21},{6,22},{7,23},{8,24},{9,... | collective-permute-start | bytes 2064392 | tf_op jit(solution)/shard_map/ppermute | solution.py:772
  100.1 40.1 %collective-permute-start.19 = (bf16[4,448,384]{2,1,0:T(8,128)(2,1)S(1)}, bf16[4,448,384]{2,1,0:T(8,128)(2,1)}, u32[]{:S(2)}, u32[]{:S(2)}) collective-permute-start(bf16[4,448,384]{2,1,0:T(8,128)(2,1)S(1)} %pad_maximum_fusion.rest_0_), channel_id=1, source_target_pairs={{0,1},{1,0},{2,3},{3,2},{4,5},{5,4},{6,7},{7,6},{8,9},{9,8},{10,11... | collective-permute-start | bytes 4128776 | tf_op jit(solution)/shard_map/ppermute | solution.py:772
  100.2 40.0 %collective-permute-start.21 = (bf16[4,448,384]{2,1,0:T(8,128)(2,1)}, bf16[4,448,384]{2,1,0:T(8,128)(2,1)}, u32[]{:S(2)}, u32[]{:S(2)}) collective-permute-start(bf16[4,448,384]{2,1,0:T(8,128)(2,1)} %collective-permute-done.16.rest_2_), channel_id=1, source_target_pairs={{0,1},{1,0},{2,3},{3,2},{4,5},{5,4},{6,7},{7,6},{8,9},{9,8},{10,11... | collective-permute-start | bytes 4128776 | tf_op jit(solution)/shard_map/ppermute | solution.py:772
  101.7 38.6 %collective-permute-start.20 = (bf16[4,448,384]{2,1,0:T(8,128)(2,1)}, bf16[4,448,384]{2,1,0:T(8,128)(2,1)}, u32[]{:S(2)}, u32[]{:S(2)}) collective-permute-start(bf16[4,448,384]{2,1,0:T(8,128)(2,1)} %collective-permute-done.15.rest_1_), channel_id=1, source_target_pairs={{0,1},{1,0},{2,3},{3,2},{4,5},{5,4},{6,7},{7,6},{8,9},{9,8},{10,11... | collective-permute-start | bytes 4128776 | tf_op jit(solution)/shard_map/ppermute | solution.py:772
  116.0 24.2 %collective-permute-start.23 = (bf16[2,448,384]{2,1,0:T(8,128)(2,1)}, bf16[2,448,384]{2,1,0:T(8,128)(2,1)S(1)}, u32[]{:S(2)}, u32[]{:S(2)}) collective-permute-start(bf16[2,448,384]{2,1,0:T(8,128)(2,1)} %collective-permute-done.18.rest_4_), channel_id=1, source_target_pairs={{0,1},{1,0},{2,3},{3,2},{4,5},{5,4},{6,7},{7,6},{8,9},{9,8},{10,11... | collective-permute-start | bytes 2064392 | tf_op jit(solution)/shard_map/ppermute | solution.py:772
  117.2 23.0 %collective-permute-start.22 = (bf16[2,448,384]{2,1,0:T(8,128)(2,1)}, bf16[2,448,384]{2,1,0:T(8,128)(2,1)S(1)}, u32[]{:S(2)}, u32[]{:S(2)}) collective-permute-start(bf16[2,448,384]{2,1,0:T(8,128)(2,1)} %collective-permute-done.17.rest_3_), channel_id=1, source_target_pairs={{0,1},{1,0},{2,3},{3,2},{4,5},{5,4},{6,7},{7,6},{8,9},{9,8},{10,11... | collective-permute-start | bytes 2064392 | tf_op jit(solution)/shard_map/ppermute | solution.py:772
  273.8 40.0 %collective-permute-start.24 = (bf16[2,2,4,160,384]{4,3,2,1,0:T(8,128)(2,1)}, bf16[2,2,4,160,384]{4,3,2,1,0:T(8,128)(2,1)}, u32[]{:S(2)}, u32[]{:S(2)}) collective-permute-start(bf16[2,2,4,160,384]{4,3,2,1,0:T(8,128)(2,1)} %get-tuple-element.44), channel_id=1, source_target_pairs={{0,1},{1,0},{2,3},{3,2},{4,5},{5,4},{6,7},{7,6},{8,9},{9,8},{10,11... | collective-permute-start | bytes 5898248 | tf_op jit(solution)/shard_map/ppermute | solution.py:772
  290.8 44.3 %collective-permute-start.42 = (bf16[2,2,4,192,384]{4,3,2,1,0:T(8,128)(2,1)}, bf16[2,2,4,192,384]{4,3,2,1,0:T(8,128)(2,1)S(1)}, u32[]{:S(2)}, u32[]{:S(2)}) collective-permute-start(bf16[2,2,4,192,384]{4,3,2,1,0:T(8,128)(2,1)} %get-tuple-element.55), channel_id=1, source_target_pairs={{0,1},{1,0},{2,3},{3,2},{4,5},{5,4},{6,7},{7,6},{8,9},{9,8},{10,11... | collective-permute-start | bytes 7077896 | tf_op jit(solution)/shard_map/ppermute | solution.py:772
  313.3 59.0 %collective-permute-start.33 = (bf16[2,2,4,256,384]{4,3,2,1,0:T(8,128)(2,1)}, bf16[2,2,4,256,384]{4,3,2,1,0:T(8,128)(2,1)S(1)}, u32[]{:S(2)}, u32[]{:S(2)}) collective-permute-start(bf16[2,2,4,256,384]{4,3,2,1,0:T(8,128)(2,1)} %get-tuple-element.51), channel_id=1, source_target_pairs={{0,1},{1,0},{2,3},{3,2},{4,5},{5,4},{6,7},{7,6},{8,9},{9,8},{10,11... | collective-permute-start | bytes 9437192 | tf_op jit(solution)/shard_map/ppermute | solution.py:772
  315.9 17.3 %collective-permute-start.28 = (bf16[2,2,160,384]{3,2,1,0:T(8,128)(2,1)}, bf16[2,2,160,384]{3,2,1,0:T(8,128)(2,1)}, u32[]{:S(2)}, u32[]{:S(2)}) collective-permute-start(bf16[2,2,160,384]{3,2,1,0:T(8,128)(2,1)} %fusion.15), channel_id=1, source_target_pairs={{0,16},{1,17},{2,18},{3,19},{4,20},{5,21},{6,22},{7,23},{8,24},{9,... | collective-permute-start | bytes 1474568 | tf_op jit(solution)/shard_map/ppermute | solution.py:772
  331.6 14.2 %collective-permute-start.25 = (bf16[2,2,160,384]{3,2,1,0:T(8,128)(2,1)S(1)}, bf16[2,2,160,384]{3,2,1,0:T(8,128)(2,1)S(1)}, u32[]{:S(2)}, u32[]{:S(2)}) collective-permute-start(bf16[2,2,160,384]{3,2,1,0:T(8,128)(2,1)S(1)} %fusion.14), channel_id=1, source_target_pairs={{0,2},{1,3},{2,0},{3,1},{4,6},{5,7},{6,4},{7,5},{8,10},{9,11},{10,... | collective-permute-start | bytes 1474568 | tf_op jit(solution)/shard_map/ppermute | solution.py:772
  334.5 16.6 %collective-permute-start.29 = (bf16[2,160,384]{2,1,0:T(8,128)(2,1)S(1)}, bf16[2,160,384]{2,1,0:T(8,128)(2,1)S(1)}, u32[]{:S(2)}, u32[]{:S(2)}) collective-permute-start(bf16[2,160,384]{2,1,0:T(8,128)(2,1)S(1)} %fusion.16), channel_id=1, source_target_pairs={{0,2},{1,3},{2,0},{3,1},{4,6},{5,7},{6,4},{7,5},{8,10},{9,11},{10,... | collective-permute-start | bytes 737288 | tf_op jit(solution)/shard_map/ppermute | solution.py:772
  335.2 28.8 %collective-permute-start.43 = (bf16[2,2,192,384]{3,2,1,0:T(8,128)(2,1)S(1)}, bf16[2,2,192,384]{3,2,1,0:T(8,128)(2,1)S(1)}, u32[]{:S(2)}, u32[]{:S(2)}) collective-permute-start(bf16[2,2,192,384]{3,2,1,0:T(8,128)(2,1)S(1)} %fusion.7), channel_id=1, source_target_pairs={{0,2},{1,3},{2,0},{3,1},{4,6},{5,7},{6,4},{7,5},{8,10},{9,11},{10,... | collective-permute-start | bytes 1769480 | tf_op jit(solution)/shard_map/ppermute | solution.py:772
  352.7 9.0 %collective-permute-start.26 = (bf16[2,160,384]{2,1,0:T(8,128)(2,1)S(1)}, bf16[2,160,384]{2,1,0:T(8,128)(2,1)S(1)}, u32[]{:S(2)}, u32[]{:S(2)}) collective-permute-start(bf16[2,160,384]{2,1,0:T(8,128)(2,1)S(1)} %get-tuple-element.63), channel_id=1, source_target_pairs={{0,16},{1,17},{2,18},{3,19},{4,20},{5,21},{6,22},{7,23},{8,24},{9,... | collective-permute-start | bytes 737288 | tf_op jit(solution)/shard_map/ppermute | solution.py:772
  354.5 28.6 %collective-permute-start.46 = (bf16[2,2,192,384]{3,2,1,0:T(8,128)(2,1)S(1)}, bf16[2,2,192,384]{3,2,1,0:T(8,128)(2,1)S(1)}, u32[]{:S(2)}, u32[]{:S(2)}) collective-permute-start(bf16[2,2,192,384]{3,2,1,0:T(8,128)(2,1)S(1)} %fusion.8), channel_id=1, source_target_pairs={{0,16},{1,17},{2,18},{3,19},{4,20},{5,21},{6,22},{7,23},{8,24},{9,... | collective-permute-start | bytes 1769480 | tf_op jit(solution)/shard_map/ppermute | solution.py:772
  355.0 11.8 %collective-permute-start.30 = (bf16[160,384]{1,0:T(8,128)(2,1)S(1)}, bf16[160,384]{1,0:T(8,128)(2,1)S(1)}, u32[]{:S(2)}, u32[]{:S(2)}) collective-permute-start(bf16[160,384]{1,0:T(8,128)(2,1)S(1)} %get-tuple-element.84), channel_id=1, source_target_pairs={{0,8},{1,9},{2,10},{3,11},{4,12},{5,13},{6,14},{7,15},{8,0},{9,1},... | collective-permute-start | bytes 368648 | tf_op jit(solution)/shard_map/ppermute | solution.py:779
  361.6 8.0 %collective-permute-start.31 = (bf16[160,384]{1,0:T(8,128)(2,1)S(1)}, bf16[160,384]{1,0:T(8,128)(2,1)S(1)}, u32[]{:S(2)}, u32[]{:S(2)}) collective-permute-start(bf16[160,384]{1,0:T(8,128)(2,1)S(1)} %get-tuple-element.85), channel_id=1, source_target_pairs={{0,4},{1,5},{2,6},{3,7},{4,8},{5,9},{6,10},{7,11},{8,12},{9,13},{1... | collective-permute-start | bytes 368648 | tf_op jit(solution)/shard_map/ppermute | solution.py:779
  364.1 6.1 %collective-permute-start.27 = (bf16[160,384]{1,0:T(8,128)(2,1)S(1)}, bf16[160,384]{1,0:T(8,128)(2,1)S(1)}, u32[]{:S(2)}, u32[]{:S(2)}) collective-permute-start(bf16[160,384]{1,0:T(8,128)(2,1)S(1)} %fusion.32), channel_id=1, source_target_pairs={{0,12},{1,13},{2,14},{3,15},{4,0},{5,1},{6,2},{7,3},{8,4},{9,5},{1... | collective-permute-start | bytes 368648 | tf_op jit(solution)/shard_map/ppermute | solution.py:779
  366.8 16.3 %collective-permute-start.44 = (bf16[2,192,384]{2,1,0:T(8,128)(2,1)S(1)}, bf16[2,192,384]{2,1,0:T(8,128)(2,1)S(1)}, u32[]{:S(2)}, u32[]{:S(2)}) collective-permute-start(bf16[2,192,384]{2,1,0:T(8,128)(2,1)S(1)} %fusion.12), channel_id=1, source_target_pairs={{0,16},{1,17},{2,18},{3,19},{4,20},{5,21},{6,22},{7,23},{8,24},{9,... | collective-permute-start | bytes 884744 | tf_op jit(solution)/shard_map/ppermute | solution.py:772
  370.3 12.7 %collective-permute-start.32 = (bf16[144,384]{1,0:T(8,128)(2,1)S(1)}, bf16[144,384]{1,0:T(8,128)(2,1)S(1)}, u32[]{:S(2)}, u32[]{:S(2)}) collective-permute-start(bf16[144,384]{1,0:T(8,128)(2,1)S(1)} %slice.620), channel_id=1, source_target_pairs={{0,16},{1,17},{2,18},{3,19},{4,20},{5,21},{6,22},{7,23},{8,24},{9,... | collective-permute-start | bytes 331784 | tf_op jit(solution)/shard_map/ppermute | solution.py:772
  372.5 29.0 %collective-permute-start.34 = (bf16[2,2,256,384]{3,2,1,0:T(8,128)(2,1)S(1)}, bf16[2,2,256,384]{3,2,1,0:T(8,128)(2,1)S(1)}, u32[]{:S(2)}, u32[]{:S(2)}) collective-permute-start(bf16[2,2,256,384]{3,2,1,0:T(8,128)(2,1)S(1)} %fusion), channel_id=1, source_target_pairs={{0,2},{1,3},{2,0},{3,1},{4,6},{5,7},{6,4},{7,5},{8,10},{9,11},{10,... | collective-permute-start | bytes 2359304 | tf_op jit(solution)/shard_map/ppermute | solution.py:772
  373.4 23.6 %collective-permute-start.37 = (bf16[2,2,256,384]{3,2,1,0:T(8,128)(2,1)S(1)}, bf16[2,2,256,384]{3,2,1,0:T(8,128)(2,1)S(1)}, u32[]{:S(2)}, u32[]{:S(2)}) collective-permute-start(bf16[2,2,256,384]{3,2,1,0:T(8,128)(2,1)S(1)} %fusion.1), channel_id=1, source_target_pairs={{0,16},{1,17},{2,18},{3,19},{4,20},{5,21},{6,22},{7,23},{8,24},{9,... | collective-permute-start | bytes 2359304 | tf_op jit(solution)/shard_map/ppermute | solution.py:772
  383.4 14.8 %collective-permute-start.47 = (bf16[2,192,384]{2,1,0:T(8,128)(2,1)S(1)}, bf16[2,192,384]{2,1,0:T(8,128)(2,1)S(1)}, u32[]{:S(2)}, u32[]{:S(2)}) collective-permute-start(bf16[2,192,384]{2,1,0:T(8,128)(2,1)S(1)} %get-tuple-element.61), channel_id=1, source_target_pairs={{0,2},{1,3},{2,0},{3,1},{4,6},{5,7},{6,4},{7,5},{8,10},{9,11},{10,... | collective-permute-start | bytes 884744 | tf_op jit(solution)/shard_map/ppermute | solution.py:772
  385.0 21.4 %collective-permute-start.45 = (bf16[192,384]{1,0:T(8,128)(2,1)S(1)}, bf16[192,384]{1,0:T(8,128)(2,1)S(1)}, u32[]{:S(2)}, u32[]{:S(2)}) collective-permute-start(bf16[192,384]{1,0:T(8,128)(2,1)S(1)} %fusion.31), channel_id=1, source_target_pairs={{0,12},{1,13},{2,14},{3,15},{4,0},{5,1},{6,2},{7,3},{8,4},{9,5},{1... | collective-permute-start | bytes 442376 | tf_op jit(solution)/shard_map/ppermute | solution.py:779
  397.1 8.3 %collective-permute-start.38 = (bf16[2,256,384]{2,1,0:T(8,128)(2,1)S(1)}, bf16[2,256,384]{2,1,0:T(8,128)(2,1)S(1)}, u32[]{:S(2)}, u32[]{:S(2)}) collective-permute-start(bf16[2,256,384]{2,1,0:T(8,128)(2,1)S(1)} %fusion.2), channel_id=1, source_target_pairs={{0,2},{1,3},{2,0},{3,1},{4,6},{5,7},{6,4},{7,5},{8,10},{9,11},{10,... | collective-permute-start | bytes 1179656 | tf_op jit(solution)/shard_map/ppermute | solution.py:772
  398.3 8.4 %collective-permute-start.48 = (bf16[192,384]{1,0:T(8,128)(2,1)S(1)}, bf16[192,384]{1,0:T(8,128)(2,1)S(1)}, u32[]{:S(2)}, u32[]{:S(2)}) collective-permute-start(bf16[192,384]{1,0:T(8,128)(2,1)S(1)} %get-tuple-element.82), channel_id=1, source_target_pairs={{0,8},{1,9},{2,10},{3,11},{4,12},{5,13},{6,14},{7,15},{8,0},{9,1},... | collective-permute-start | bytes 442376 | tf_op jit(solution)/shard_map/ppermute | solution.py:779
  401.5 7.3 %collective-permute-start.49 = (bf16[192,384]{1,0:T(8,128)(2,1)S(1)}, bf16[192,384]{1,0:T(8,128)(2,1)S(1)}, u32[]{:S(2)}, u32[]{:S(2)}) collective-permute-start(bf16[192,384]{1,0:T(8,128)(2,1)S(1)} %get-tuple-element.83), channel_id=1, source_target_pairs={{0,4},{1,5},{2,6},{3,7},{4,8},{5,9},{6,10},{7,11},{8,12},{9,13},{1... | collective-permute-start | bytes 442376 | tf_op jit(solution)/shard_map/ppermute | solution.py:779
  405.8 9.0 %collective-permute-start.35 = (bf16[2,256,384]{2,1,0:T(8,128)(2,1)S(1)}, bf16[2,256,384]{2,1,0:T(8,128)(2,1)S(1)}, u32[]{:S(2)}, u32[]{:S(2)}) collective-permute-start(bf16[2,256,384]{2,1,0:T(8,128)(2,1)S(1)} %get-tuple-element.59), channel_id=1, source_target_pairs={{0,16},{1,17},{2,18},{3,19},{4,20},{5,21},{6,22},{7,23},{8,24},{9,... | collective-permute-start | bytes 1179656 | tf_op jit(solution)/shard_map/ppermute | solution.py:772
  408.8 7.5 %collective-permute-start.50 = (bf16[192,384]{1,0:T(8,128)(2,1)S(1)}, bf16[192,384]{1,0:T(8,128)(2,1)S(1)}, u32[]{:S(2)}, u32[]{:S(2)}) collective-permute-start(bf16[192,384]{1,0:T(8,128)(2,1)S(1)} %get-tuple-element.56), channel_id=1, source_target_pairs={{0,16},{1,17},{2,18},{3,19},{4,20},{5,21},{6,22},{7,23},{8,24},{9,... | collective-permute-start | bytes 442376 | tf_op jit(solution)/shard_map/ppermute | solution.py:772
  411.4 11.3 %collective-permute-start.39 = (bf16[256,384]{1,0:T(8,128)(2,1)S(1)}, bf16[256,384]{1,0:T(8,128)(2,1)S(1)}, u32[]{:S(2)}, u32[]{:S(2)}) collective-permute-start(bf16[256,384]{1,0:T(8,128)(2,1)S(1)} %get-tuple-element.74), channel_id=1, source_target_pairs={{0,8},{1,9},{2,10},{3,11},{4,12},{5,13},{6,14},{7,15},{8,0},{9,1},... | collective-permute-start | bytes 589832 | tf_op jit(solution)/shard_map/ppermute | solution.py:779
  411.5 11.2 %collective-permute-start.40 = (bf16[256,384]{1,0:T(8,128)(2,1)S(1)}, bf16[256,384]{1,0:T(8,128)(2,1)S(1)}, u32[]{:S(2)}, u32[]{:S(2)}) collective-permute-start(bf16[256,384]{1,0:T(8,128)(2,1)S(1)} %get-tuple-element.75), channel_id=1, source_target_pairs={{0,4},{1,5},{2,6},{3,7},{4,8},{5,9},{6,10},{7,11},{8,12},{9,13},{1... | collective-permute-start | bytes 589832 | tf_op jit(solution)/shard_map/ppermute | solution.py:779
  414.9 8.3 %collective-permute-start.36 = (bf16[256,384]{1,0:T(8,128)(2,1)S(1)}, bf16[256,384]{1,0:T(8,128)(2,1)S(1)}, u32[]{:S(2)}, u32[]{:S(2)}) collective-permute-start(bf16[256,384]{1,0:T(8,128)(2,1)S(1)} %fusion.30), channel_id=1, source_target_pairs={{0,12},{1,13},{2,14},{3,15},{4,0},{5,1},{6,2},{7,3},{8,4},{9,5},{1... | collective-permute-start | bytes 589832 | tf_op jit(solution)/shard_map/ppermute | solution.py:779
  423.9 5.6 %collective-permute-start.41 = (bf16[240,384]{1,0:T(8,128)(2,1)S(1)}, bf16[240,384]{1,0:T(8,128)(2,1)S(1)}, u32[]{:S(2)}, u32[]{:S(2)}) collective-permute-start(bf16[240,384]{1,0:T(8,128)(2,1)S(1)} %slice.619), channel_id=1, source_target_pairs={{0,16},{1,17},{2,18},{3,19},{4,20},{5,21},{6,22},{7,23},{8,24},{9,... | collective-permute-start | bytes 552968 | tf_op jit(solution)/shard_map/ppermute | solution.py:772
  (21 other events, 268.2 us)

commit v3 on v2

--- a/solution.py
+++ b/solution.py
@@ -15,18 +15,6 @@
 BF16 = jnp.bfloat16
 VMEM_LIMIT = 60000 * 1024
 
-ERFC_SLOPE = 0.33
-ERFC_TERMS = (
-    0.18635788923911423,
-    0.18295457713165508,
-    0.20123280917878972,
-    0.04718951182123742,
-    0.408562666534809,
-    -0.35122255207376696,
-    0.46028245445329624,
-    -0.1353573694779288,
-)
-
 
 def product(left, right):
     return jnp.dot(left, right, preferred_element_type=F32)
@@ -41,14 +29,8 @@
 
 
 def normal_parts(u):
-    density = jnp.exp(-0.5 * u * u)
-    t = 1.0 / (1.0 + (ERFC_SLOPE / math.sqrt(2.0)) * jnp.abs(u))
-    poly = jnp.full_like(t, 0.5 * ERFC_TERMS[-1])
-    for term in ERFC_TERMS[-2::-1]:
-        poly = poly * t + 0.5 * term
-    tail = poly * t * density
-    cumulative = jnp.where(u >= 0.0, 1.0 - tail, tail)
-    return cumulative, u * (density * (1.0 / math.sqrt(2.0 * math.pi)))
+    cumulative = 0.5 + 0.5 * lax.erf(u * math.sqrt(0.5))
+    return cumulative, u * (jnp.exp(-0.5 * u * u) * (1.0 / math.sqrt(2.0 * math.pi)))
 
 
 def normalise(rows):
@@ -94,17 +76,17 @@
     return place_ref[0], place_ref[1], place_ref[2], place_ref[3]
 
 
-def shard_slots(place_ref):
+def shard_slots(place_ref, whole_planes):
     y, z, x, core = place_of(place_ref)
     for other in range(2):
         for plane in range(4):
             for turn in range(4):
-                if plane < 3:
+                if plane < whole_planes:
                     buffer, at = plane, turn
                 else:
-                    buffer, at = 3 + turn // 2, turn % 2
+                    buffer, at = 2 * plane - whole_planes + turn // 2, turn % 2
                 owner = ((z - turn) & 3) * 4 + (x ^ (plane & 1)) * 2 + (core ^ other)
-                yield 5 * other + buffer, at, owner, y ^ (plane >> 1), plane < 2
+                yield (8 - whole_planes) * other + buffer, at, owner, y ^ (plane >> 1), plane < 2
 
 
 def run_copies(copies, sems):
@@ -121,9 +103,9 @@
     return pl.multiple_of(index * unit, unit)
 
 
-def attention_rows(length, width, x_ref, seg_ref, w_ref, bias_ref, qkv_ref, ctx_ref):
+def attention_rows(length, width, first, x_ref, seg_ref, w_ref, bias_ref, qkv_ref, ctx_ref):
     tokens = x_ref.shape[0]
-    step = pl.program_id(0)
+    step = pl.program_id(0) + first
     x = x_ref[...]
     for part in range(3):
         cols = pl.ds(part * width, width)
@@ -158,13 +140,13 @@
 
 
 def attention_gathered_kernel(length, width, place_ref, x_ref, seg_ref, *rest):
-    buffers, (qkv_ref, ctx_ref, w_ref, small_ref, bias_ref, sems) = rest[:10], rest[10:]
+    buffers, (qkv_ref, ctx_ref, w_ref, bias_ref, small_ref, sems) = rest[:10], rest[10:]
     unit = width // 16
 
     @pl.when(pl.program_id(0) == 0)
     def _():
         copies = []
-        for buffer, at, owner, half, first in shard_slots(place_ref):
+        for buffer, at, owner, half, first in shard_slots(place_ref, 3):
             source = buffers[buffer].at[at]
             for block in range(3):
                 target = w_ref.at[
@@ -185,24 +167,26 @@
             bias_ref[:, pl.ds(part * width, width)] = total
         bias_ref[:, pl.ds(width, width)] = jnp.zeros((8, width), F32)
 
-    attention_rows(length, width, x_ref, seg_ref, w_ref, bias_ref, qkv_ref, ctx_ref)
-
-
-def attention_whole_kernel(length, width, x_ref, seg_ref, w_ref, bias_ref, qkv_ref, ctx_ref):
-    attention_rows(length, width, x_ref, seg_ref, w_ref, bias_ref, qkv_ref, ctx_ref)
-
-
-def attention_forward(x, seg, weights, place=None, rows_per_step=2):
+    attention_rows(length, width, 0, x_ref, seg_ref, w_ref, bias_ref, qkv_ref, ctx_ref)
+
+
+def attention_whole_kernel(length, width, first, x_ref, seg_ref, w_ref, bias_ref, *outs):
+    attention_rows(length, width, first, x_ref, seg_ref, w_ref, bias_ref, *outs[-2:])
+
+
+def attention_forward(x, seg, weights, place=None, part=(0, 1), earlier=(), rows_per_step=2):
     row_count, length = seg.shape
     tokens, width = x.shape
     block = rows_per_step * length
+    steps = row_count // rows_per_step // part[1]
+    first = part[0] * steps
     in_specs = [
-        pl.BlockSpec((block, width), lambda i, *_: (i, 0)),
+        pl.BlockSpec((block, width), lambda i, *_: (i + first, 0)),
         pl.BlockSpec((row_count, length), lambda i, *_: (0, 0)),
     ]
     out_specs = [
-        pl.BlockSpec((block, 3 * width), lambda i, *_: (i, 0)),
-        pl.BlockSpec((block, width), lambda i, *_: (i, 0)),
+        pl.BlockSpec((block, 3 * width), lambda i, *_: (i + first, 0)),
+        pl.BlockSpec((block, width), lambda i, *_: (i + first, 0)),
     ]
     out_shape = [
         jax.ShapeDtypeStruct((tokens, 3 * width), BF16),
@@ -211,39 +195,49 @@
     settings = dict(
         compiler_params=pltpu.CompilerParams(vmem_limit_bytes=VMEM_LIMIT),
         cost_estimate=pl.CostEstimate(
-            flops=2 * tokens * width * 3 * width + 8 * tokens * length * width,
-            bytes_accessed=tokens * width * 10 + 6 * width * width,
-            transcendentals=tokens * length * (width // HEAD),
+            flops=(2 * tokens * width * 3 * width + 8 * tokens * length * width) // part[1],
+            bytes_accessed=tokens * width * 10 // part[1] + 6 * width * width,
+            transcendentals=tokens * length * (width // HEAD) // part[1],
         ),
         name="attention_forward",
     )
-    grid = (row_count // rows_per_step,)
-    matrix_spec = pl.BlockSpec((width, 3 * width), lambda i, *_: (0, 0), pipeline_mode=pl.Buffered(1))
     if place is None:
-        in_specs += [matrix_spec, pl.BlockSpec((1, 3 * width), lambda i: (0, 0))]
+        in_specs += [
+            pl.BlockSpec((width, 3 * width), lambda i: (0, 0), pipeline_mode=pl.Buffered(1)),
+            pl.BlockSpec(weights[1].shape, lambda i: (0, 0)),
+        ]
+        in_specs += [pl.BlockSpec(memory_space=pl.ANY)] * len(earlier)
         return pl.pallas_call(
-            functools.partial(attention_whole_kernel, length, width),
-            grid=grid,
+            functools.partial(attention_whole_kernel, length, width, first),
+            grid=(steps,),
             in_specs=in_specs,
             out_specs=out_specs,
             out_shape=out_shape,
+            input_output_aliases={4 + n: n for n in range(len(earlier))},
             **settings,
-        )(x, seg, *weights)
+        )(x, seg, *weights, *earlier)
     spec = pltpu.PrefetchScalarGridSpec(
         num_scalar_prefetch=1,
-        grid=grid,
+        grid=(steps,),
         in_specs=in_specs + [pl.BlockSpec(memory_space=pl.ANY)] * 10,
-        out_specs=out_specs + [pl.BlockSpec((width, 3 * width), lambda i, *_: (0, 0))],
+        out_specs=out_specs
+        + [
+            pl.BlockSpec((width, 3 * width), lambda i, *_: (0, 0)),
+            pl.BlockSpec((8, 3 * width), lambda i, *_: (0, 0)),
+        ],
         scratch_shapes=[
             pltpu.VMEM((16, SMALL, BLOCK), BF16),
-            pltpu.VMEM((8, 3 * width), F32),
             pltpu.SemaphoreType.DMA((112,)),
         ],
     )
     return pl.pallas_call(
         functools.partial(attention_gathered_kernel, length, width),
         grid_spec=spec,
-        out_shape=out_shape + [jax.ShapeDtypeStruct((width, 3 * width), BF16)],
+        out_shape=out_shape
+        + [
+            jax.ShapeDtypeStruct((width, 3 * width), BF16),
+            jax.ShapeDtypeStruct((8, 3 * width), F32),
+        ],
         **settings,
     )(place, x, seg, *weights)
 
@@ -343,8 +337,8 @@
 
 
 def feedforward_gathered_kernel(length, chunk, place_ref, x_ref, ctx_ref, seg_ref, pooled_grad_ref, *rest):
-    buffers, outs = rest[:10], rest[10:20]
-    slope_ref, out_w_ref, up_w_ref, down_w_ref, vec_ref, up_bias_ref, gathered_ref, sems = rest[20:]
+    buffers, outs = rest[:16], rest[16:26]
+    slope_ref, out_w_ref, up_w_ref, down_w_ref, vec_ref, up_bias_ref, gathered_ref, sems = rest[26:]
     width, hidden = up_w_ref.shape
     unit = width // 16
     ratio = hidden // width
@@ -352,7 +346,7 @@
     @pl.when(pl.program_id(0) == 0)
     def _():
         copies = []
-        for buffer, at, owner, half, first in shard_slots(place_ref):
+        for buffer, at, owner, half, first in shard_slots(place_ref, 0):
             source = buffers[buffer].at[at]
             rows = pl.ds(aligned(owner, unit), unit)
             for block in range(ratio):
@@ -387,7 +381,7 @@
     )
 
 
-def feedforward(x, ctx, seg, pooled_grad, weights, hidden, place=None, rows_per_step=2, chunk=768):
+def feedforward(x, ctx, seg, pooled_grad, weights, hidden, place=None, rows_per_step=4, chunk=768):
     row_count, length = seg.shape
     tokens, width = x.shape
     segments = pooled_grad.shape[1]
@@ -466,7 +460,7 @@
     spec = pltpu.PrefetchScalarGridSpec(
         num_scalar_prefetch=1,
         grid=grid,
-        in_specs=in_specs + [pl.BlockSpec(memory_space=pl.ANY)] * 10,
+        in_specs=in_specs + [pl.BlockSpec(memory_space=pl.ANY)] * 16,
         out_specs=out_specs,
         scratch_shapes=[
             slope,
@@ -487,13 +481,14 @@
     )(place, x, ctx, seg, pooled_grad, *weights)
 
 
-def attention_back_kernel(length, width, qkv_ref, grad_ref, seg_ref, out_ref, small_ref):
+def attention_back_kernel(length, width, first, qkv_ref, grad_ref, seg_ref, *rest):
+    out_ref, small_ref = rest[-2:]
     tokens = grad_ref.shape[0]
-    step = pl.program_id(0)
-
-    @pl.when(step == 0)
+    step = pl.program_id(0) + first
+
+    @pl.when(pl.program_id(0) == 0)
     def _():
-        small_ref[...] = jnp.zeros_like(small_ref)
+        small_ref[...] = rest[1][...] if first else jnp.zeros_like(small_ref)
 
     low_half, high_half = lane_halves()
     scale = HEAD**-0.5
@@ -525,34 +520,36 @@
             small_ref[:, at[1]] += fold(values_grad.astype(F32))
 
 
-def attention_backward(qkv, ctx_grad, seg, rows_per_step=2):
+def attention_backward(qkv, ctx_grad, seg, part=(0, 1), earlier=(), rows_per_step=2):
     row_count, length = seg.shape
     tokens, width = ctx_grad.shape
     block = rows_per_step * length
+    steps = row_count // rows_per_step // part[1]
+    first = part[0] * steps
+    sums_spec = pl.BlockSpec((8, 2 * width), lambda i: (0, 0))
     return pl.pallas_call(
-        functools.partial(attention_back_kernel, length, width),
-        grid=(row_count // rows_per_step,),
+        functools.partial(attention_back_kernel, length, width, first),
+        grid=(steps,),
         in_specs=[
-            pl.BlockSpec((block, 3 * width), lambda i: (i, 0)),
-            pl.BlockSpec((block, width), lambda i: (i, 0)),
+            pl.BlockSpec((block, 3 * width), lambda i: (i + first, 0)),
+            pl.BlockSpec((block, width), lambda i: (i + first, 0)),
             pl.BlockSpec((row_count, length), lambda i: (0, 0)),
-        ],
-        out_specs=[
-            pl.BlockSpec((block, 3 * width), lambda i: (i, 0)),
-            pl.BlockSpec((8, 2 * width), lambda i: (0, 0)),
-        ],
+        ]
+        + [pl.BlockSpec(memory_space=pl.ANY), sums_spec][: len(earlier)],
+        out_specs=[pl.BlockSpec((block, 3 * width), lambda i: (i + first, 0)), sums_spec],
         out_shape=[
             jax.ShapeDtypeStruct((tokens, 3 * width), BF16),
             jax.ShapeDtypeStruct((8, 2 * width), F32),
         ],
+        input_output_aliases={3: 0} if earlier else {},
         compiler_params=pltpu.CompilerParams(vmem_limit_bytes=VMEM_LIMIT),
         cost_estimate=pl.CostEstimate(
-            flops=20 * tokens * length * width,
-            bytes_accessed=tokens * width * 14,
-            transcendentals=tokens * length * (width // HEAD),
+            flops=20 * tokens * length * width // part[1],
+            bytes_accessed=tokens * width * 14 // part[1],
+            transcendentals=tokens * length * (width // HEAD) // part[1],
         ),
         name="attention_backward",
-    )(qkv, ctx_grad, seg)
+    )(qkv, ctx_grad, seg, *earlier)
 
 
 def cut_columns(half_index, shard, out_ref, row_at, blocks):
@@ -740,28 +737,34 @@
     return pl.BlockSpec(shape, lambda i, *_: (0,) * len(shape), pipeline_mode=pl.Buffered(1))
 
 
-def input_gradient_kernel(first_ref, grad_ref, w_ref, out_ref):
-    out_ref[...] = first_ref[...] + times_transpose(grad_ref[...], w_ref[...])
-
-
-def input_gradient(first_grad, qkv_grad, matrix, rows=512):
+def input_gradient_kernel(first_ref, grad_ref, w_ref, *outs):
+    outs[-1][...] = first_ref[...] + times_transpose(grad_ref[...], w_ref[...])
+
+
+def input_gradient(first_grad, qkv_grad, matrix, part=(0, 1, 1), earlier=(), rows=512):
     tokens, width = first_grad.shape
+    first = tokens // rows * part[0] // part[2]
+    steps = tokens // rows * part[1] // part[2] - first
     return pl.pallas_call(
         input_gradient_kernel,
-        grid=(tokens // rows,),
+        grid=(steps,),
         in_specs=[
-            pl.BlockSpec((rows, width), lambda i: (i, 0)),
-            pl.BlockSpec((rows, 3 * width), lambda i: (i, 0)),
+            pl.BlockSpec((rows, width), lambda i: (i + first, 0)),
+            pl.BlockSpec((rows, 3 * width), lambda i: (i + first, 0)),
             resident(matrix.shape),
-        ],
-        out_specs=pl.BlockSpec((rows, width), lambda i: (i, 0)),
+        ]
+        + [pl.BlockSpec(memory_space=pl.ANY)] * len(earlier),
+        out_specs=pl.BlockSpec((rows, width), lambda i: (i + first, 0)),
         out_shape=jax.ShapeDtypeStruct((tokens, width), F32),
+        input_output_aliases={3: 0} if earlier else {},
         compiler_params=pltpu.CompilerParams(vmem_limit_bytes=VMEM_LIMIT),
         cost_estimate=pl.CostEstimate(
-            flops=6 * tokens * width * width, bytes_accessed=14 * tokens * width, transcendentals=0
+            flops=6 * steps * rows * width * width,
+            bytes_accessed=14 * steps * rows * width,
+            transcendentals=0,
         ),
         name="input_gradient",
-    )(first_grad, qkv_grad, matrix)
+    )(first_grad, qkv_grad, matrix, *earlier)
 
 
 AXES = ("dp", "fsdp")
@@ -782,43 +785,59 @@
 CORE, X, Y = 1, 2, 16
 
 
-def gather_shards(own):
-    turned = [along_z(own, d) for d in (1, 2, 3)]
-    here = jnp.stack([own] + turned)
-    from_x = across(here, X)
-    from_y = across(here, Y)
-    diagonal_low = across(from_x[:2], Y)
-    diagonal_high = across(from_y[2:], X)
-    mine = (here, from_x, from_y, diagonal_low, diagonal_high)
-    return mine + tuple(across(piece, CORE) for piece in mine)
-
-
-def reduce_shards(keep, send):
-    def wide(value):
-        return value.astype(F32)
-
-    got = across(send, CORE)
-
-    def pair(at):
-        return wide(keep[at]) + wide(got[at])
-
-    low, high = slice(0, 2), slice(2, 4)
-    every = slice(None)
-    low_x = across(pair((every, 1, low)).astype(BF16), X)
-    high_y = across(pair((1, every, high)).astype(BF16), Y)
-    low_y = across((pair((1, 0, low)) + wide(low_x[1])).astype(BF16), Y)
-    high_x = across((pair((0, 1, high)) + wide(high_y[1])).astype(BF16), X)
-    low_sum = pair((0, 0, low)) + wide(low_x[0]) + wide(low_y)
-    high_sum = pair((0, 0, high)) + wide(high_y[0]) + wide(high_x)
-    total = low_sum[0]
-    for turn in (1, 2, 3):
-        part = low_sum[1] if turn == 1 else high_sum[turn - 2]
-        total = total + wide(along_z(part.astype(BF16), 4 - turn))
-    return total
-
-
-def both_halves(mine, y):
-    theirs = across(mine.astype(BF16), Y).astype(F32)
+def together(*values):
+    return lax.optimization_barrier(values)
+
+
+def shifts(own):
+    return tuple(along_z(own, d) for d in (1, 2, 3))
+
+
+class Reduction:
+    def __init__(self, keep, got):
+        self.keep, self.got = keep, got
+
+    def pair(self, *at):
+        return self.keep[at].astype(F32) + self.got[at].astype(F32)
+
+    def first(self):
+        low_x = self.pair(slice(None), 1, slice(0, 2)).astype(BF16)
+        high_y = self.pair(1, slice(None), slice(2, 4)).astype(BF16)
+        return low_x, high_y
+
+    @staticmethod
+    def send_first(values):
+        return across(values[0], X), across(values[1], Y)
+
+    def second(self, received):
+        low_x, high_y = self.received = received
+        low_y = (self.pair(1, 0, slice(0, 2)) + low_x[1].astype(F32)).astype(BF16)
+        high_x = (self.pair(0, 1, slice(2, 4)) + high_y[1].astype(F32)).astype(BF16)
+        return low_y, high_x
+
+    @staticmethod
+    def send_second(values):
+        return across(values[0], Y), across(values[1], X)
+
+    def third(self, received):
+        low = self.pair(0, 0, slice(0, 2)) + self.received[0][0].astype(F32) + received[0].astype(F32)
+        high = self.pair(0, 0, slice(2, 4)) + self.received[1][0].astype(F32) + received[1].astype(F32)
+        self.total = low[0]
+        return low[1].astype(BF16), high[0].astype(BF16), high[1].astype(BF16)
+
+    @staticmethod
+    def send_third(values):
+        return tuple(along_z(value, 3 - n) for n, value in enumerate(values))
+
+    def finish(self, received):
+        total = self.total
+        for part in received:
+            total = total + part.astype(F32)
+        return total
+
+
+def both_halves(mine, theirs, y):
+    theirs = theirs.astype(F32)
     swap = y == 0
     return jnp.where(swap, mine, theirs), jnp.where(swap, theirs, mine)
 
@@ -863,43 +882,59 @@
     y, shard = lax.axis_index("dp"), lax.axis_index("fsdp")
     place = jnp.stack([y, shard // 4, shard // 2 % 2, shard % 2]).astype(jnp.int32)
 
-    attention_rows_count = 3 * unit + SMALL
-    feedforward_rows_count = (2 * ratio + 1) * unit + SMALL
     own_attention = pack(
         pack_attention_kernel,
         "pack_attention",
         place,
-        attention_rows_count,
+        3 * unit + SMALL,
         qkv_weight,
-        rows_of([qv_bias], SMALL),
-    )
+        jnp.pad(qv_bias[None], ((0, SMALL - 1), (0, BLOCK - 2 * unit))),
+    )
+    vectors = [out_bias, first_gain, first_shift, down_bias, second_gain, second_shift, up_bias]
+    own_attention, *vectors = together(own_attention, *vectors)
     own_feedforward = pack(
         pack_feedforward_kernel,
         "pack_feedforward",
         place,
-        feedforward_rows_count,
+        (2 * ratio + 1) * unit + SMALL,
         up_weight,
         down_weight,
         out_weight,
-        rows_of([out_bias, first_gain, first_shift, down_bias, second_gain, second_shift, up_bias], SMALL),
-    )
-    attention_pieces = gather_shards(own_attention)
-    feedforward_pieces = gather_shards(own_feedforward)
-    qkv, ctx, qkv_matrix = attention_forward(x, segment_ids, attention_pieces, place)
+        rows_of(vectors, SMALL),
+    )
+    turned = shifts(own_attention)
+    own_attention, own_feedforward, *turned = together(own_attention, own_feedforward, *turned)
+    here_a = jnp.stack([own_attention, *turned])
+    x_a, y_a = across(here_a, X), across(here_a, Y)
+    here_a_core = across(here_a, CORE)
+    turn_f = along_z(own_feedforward, 1)
+    x_a, y_a, own_feedforward, turn_f = together(x_a, y_a, own_feedforward, turn_f)
+    low_a, high_a = across(x_a[:2], Y), across(y_a[2:], X)
+    x_a_core, y_a_core = across(x_a, CORE), across(y_a, CORE)
+    here_low = jnp.stack([own_feedforward, turn_f])
+    low_a, high_a, here_low, own_feedforward = together(low_a, high_a, here_low, own_feedforward)
+    turn_two, turn_three = along_z(own_feedforward, 2), along_z(own_feedforward, 3)
+    attention_pieces = (here_a, x_a, y_a, low_a, high_a)
+    attention_pieces += (here_a_core, x_a_core, y_a_core, across(low_a, CORE), across(high_a, CORE))
+    here_low, turn_three, *attention_pieces = together(here_low, turn_three, *attention_pieces)
+    x_low, y_low = across(here_low, X), across(here_low, Y)
+    here_low_core = across(here_low, CORE)
+    qkv, ctx, qkv_matrix, qkv_bias = attention_forward(x, segment_ids, attention_pieces, place, (0, 2))
+    x_low, y_low, turn_two, qkv, ctx = together(x_low, y_low, turn_two, qkv, ctx)
+    here_high, qkv, ctx = together(jnp.stack([turn_two, turn_three]), qkv, ctx)
+    x_high, y_high = across(here_high, X), across(here_high, Y)
+    x_low_core, y_low_core, here_high_core = across(x_low, CORE), across(y_low, CORE), across(here_high, CORE)
+    qkv, ctx = attention_forward(x, segment_ids, (qkv_matrix, qkv_bias), None, (1, 2), (qkv, ctx))
+    x_high, y_high, qkv, ctx = together(x_high, y_high, qkv, ctx)
+    both_low, both_high = across(x_low, Y), across(y_high, X)
+    x_high_core, y_high_core = across(x_high, CORE), across(y_high, CORE)
+    feedforward_pieces = (here_low, here_high, x_low, x_high, y_low, y_high, both_low, both_high)
+    feedforward_pieces += (here_low_core, here_high_core, x_low_core, x_high_core, y_low_core, y_high_core)
+    feedforward_pieces += (across(both_low, CORE), across(both_high, CORE))
     pooled, active, hidden_grad, normed, branch, first_grad, attended, ctx_grad, sums, up_sums = feedforward(
         x, ctx, segment_ids, pooled_grad, feedforward_pieces, hidden, place
     )
-    down_keep, down_send = weight_gradient(
-        down_gradient_kernel,
-        "down_gradient",
-        place,
-        ratio * unit,
-        4,
-        (active, branch),
-        [pl.BlockSpec((tokens, hidden // 4), lambda i, *_: (0, i)), resident((tokens, width))],
-        2 * tokens * hidden * width,
-    )
-    down_total = reduce_shards(down_keep, down_send)
+
     up_keep, up_send = weight_gradient(
         up_gradient_kernel,
         "up_gradient",
@@ -918,8 +953,34 @@
         2 * tokens * width * (hidden + width),
         (width, tokens),
     )
-    up_total = reduce_shards(up_keep, up_send)
-    qkv_grad, qv_sums = attention_backward(qkv, ctx_grad, segment_ids)
+    up_keep, up_send, active = together(up_keep, up_send, active)
+    up_got = across(up_send, CORE)
+    down_keep, down_send = weight_gradient(
+        down_gradient_kernel,
+        "down_gradient",
+        place,
+        ratio * unit,
+        4,
+        (active, branch),
+        [pl.BlockSpec((tokens, hidden // 4), lambda i, *_: (0, i)), resident((tokens, width))],
+        2 * tokens * hidden * width,
+    )
+    up_got, down_keep, down_send = together(up_got, down_keep, down_send)
+    up = Reduction(up_keep, up_got)
+    *up_first, down_send, ctx_grad = together(*up.first(), down_send, ctx_grad)
+    up_first = up.send_first(up_first)
+    down_got = across(down_send, CORE)
+    qkv_grad, qv_sums = attention_backward(qkv, ctx_grad, segment_ids, (0, 2))
+    *up_first, down_got, qkv_grad, qv_sums = together(*up_first, down_got, qkv_grad, qv_sums)
+    down = Reduction(down_keep, down_got)
+    *up_second, low_d, high_d, qv_sums = together(*up.second(up_first), *down.first(), qv_sums)
+    up_second = up.send_second(up_second)
+    down_first = down.send_first((low_d, high_d))
+    qkv_grad, qv_sums = attention_backward(qkv, ctx_grad, segment_ids, (1, 2), (qkv_grad, qv_sums))
+    *up_second, low_d, high_d, qkv_grad, qv_sums = together(*up_second, *down_first, qkv_grad, qv_sums)
+    u1, u2, u3, low_d, high_d, qv_sums = together(*up.third(up_second), *down.second((low_d, high_d)), qv_sums)
+    up_third = up.send_third((u1, u2, u3))
+    down_second = down.send_second((low_d, high_d))
     qkv_keep, qkv_send = weight_gradient(
         qkv_gradient_kernel,
         "qkv_gradient",
@@ -935,16 +996,40 @@
         6 * tokens * width * width,
         (width, tokens),
     )
-    qkv_total = reduce_shards(qkv_keep, qkv_send)
-    grad_input = input_gradient(first_grad, qkv_grad, qkv_matrix)
-
-    grad_down = jnp.concatenate(both_halves(down_total, y), axis=1)
+    *up_third, low_d, high_d, qkv_keep, qkv_send = together(*up_third, *down_second, qkv_keep, qkv_send)
+    up_total = up.finish(up_third)
     up_part, up_small = up_total[: (ratio + 1) * unit], up_total[(ratio + 1) * unit :]
-    up_low, up_high = both_halves(up_part, y)
+    up_half, qkv_send, qkv_grad = together(up_part.astype(BF16), qkv_send, qkv_grad)
+    qkv_got = across(qkv_send, CORE)
+    up_theirs = across(up_half, Y)
+    grad_input = input_gradient(first_grad, qkv_grad, qkv_matrix, (0, 1, 4))
+    qkv_got, up_theirs, grad_input = together(qkv_got, up_theirs, grad_input)
+    up_low, up_high = both_halves(up_part, up_theirs, y)
     grad_up = join_columns((up_low[: ratio * unit], up_high[: ratio * unit]), unit, ratio)
     grad_out = join_columns((up_low[ratio * unit :], up_high[ratio * unit :]), unit, 1)
+    qkv_sum = Reduction(qkv_keep, qkv_got)
+    low_q, high_q, d1, d2, d3, grad_up, grad_out, grad_input = together(
+        *qkv_sum.first(), *down.third((low_d, high_d)), grad_up, grad_out, grad_input
+    )
+    qkv_first = qkv_sum.send_first((low_q, high_q))
+    down_third = down.send_third((d1, d2, d3))
+    grad_input = input_gradient(first_grad, qkv_grad, qkv_matrix, (1, 3, 4), (grad_input,))
+    *qkv_first, grad_input = together(*qkv_first, grad_input)
+    *qkv_second, grad_input = together(*qkv_sum.second(qkv_first), grad_input)
+    qkv_second = qkv_sum.send_second(qkv_second)
+    grad_input = input_gradient(first_grad, qkv_grad, qkv_matrix, (3, 4, 4), (grad_input,))
+    low_q, high_q, *down_third, grad_input = together(*qkv_second, *down_third, grad_input)
+    qkv_second = low_q, high_q
+    qkv_third = together(*qkv_sum.third(qkv_second))
+    down_total = down.finish(down_third)
+    qkv_third = qkv_sum.send_third(qkv_third)
+    down_theirs = across(down_total.astype(BF16), Y)
+    grad_down = jnp.concatenate(both_halves(down_total, down_theirs, y), axis=1)
+    *qkv_third, grad_down = together(*qkv_third, grad_down)
+    qkv_total = qkv_sum.finish(qkv_third)
     qkv_part, qkv_small = qkv_total[: 3 * unit], qkv_total[3 * unit :]
-    grad_qkv = join_columns(both_halves(qkv_part, y), unit, 3)
+    qkv_theirs = across(qkv_part.astype(BF16), Y)
+    grad_qkv = join_columns(both_halves(qkv_part, qkv_theirs, y), unit, 3)
     return (
         pooled,
         grad_input.reshape(row_count, length, width),

time: 431 us -> 371 us (0.86); the launches traced: 431 us -> 364 us
  waiting for transfers between devices: 136 us -> 64.9 us
  other arithmetic: 14.2 us -> 25.7 us
  Pallas kernels: 213 us -> 207 us
    ppermute x36 -> x41, waiting for transfers between devices: 89.1 us -> 37.8 us  [across(): return lax.ppermute(value, AXES, [(i, i ^ mask) for i in range(DEVICES)])]
    pallas_call x2 -> x6, Pallas kernels: 44 us -> 65.3 us  [the longest x2 32.5 us: attention_backward(): pl.pallas_call(functools.partial(attention_back_kernel, length, width, fi...]
    ppermute x15, waiting for transfers between devices: 46.8 us -> 27.1 us  [along_z(): return lax.ppermute(value, AXES, [(i, target(i)) for i in range(DEVICES)])]
    pallas_call x1, Pallas kernels: 87.8 us -> 68.7 us  [feedforward(): pl.pallas_call(functools.partial(feedforward_gathered_kernel, length, chu...]
    convert_element_type x10, other arithmetic: 5.85 us -> 14.9 us  [the longest x3 5.16 us: first(): low_x = self.pair(slice(None), 1, slice(0, 2)).astype(BF16)]
    pallas_call x1, Pallas kernels: 23 us -> 14.2 us  [attention_forward(): pl.pallas_call(functools.partial(attention_gathered_kernel, length, width...]
    ppermute x36 -> x41, starting transfers between devices: 30.6 us -> 27.5 us  [across(): return lax.ppermute(value, AXES, [(i, i ^ mask) for i in range(DEVICES)])]
  transfers between devices with their start and end apart: 51 -> 56, of which waited for: 25 -> 19; matrix products, arithmetic and copies ran while one was open for 4% -> 4% of each run, Pallas kernels for 18% -> 31%
where the time goes in v3:
time: 371 us; the launch traced here: 364 us
  Pallas kernels  207 us (56%)
  waiting for transfers between devices  64.9 us (17%)
  starting transfers between devices  50 us (13%)
  other arithmetic  25.7 us (7%)
  local copies, waits for them, and re-layouts  14.7 us (4%)
    pallas_call x1, Pallas kernels, feedforward(): pl.pallas_call(functools.partial(feedforward_gathered_kernel, length, chu...  68.7 us
    pallas_call x3, Pallas kernels, weight_gradient(): pl.pallas_call(kernel, grid_spec=spec, out_shape=[jax.ShapeDtypeStruct(sh...  53.8 us
    ppermute x41, waiting for transfers between devices, across(): return lax.ppermute(value, AXES, [(i, i ^ mask) for i in range(DEVICES)])  37.8 us
    pallas_call x2, Pallas kernels, attention_backward(): pl.pallas_call(functools.partial(attention_back_kernel, length, width, fi...  32.5 us
    ppermute x41, starting transfers between devices, across(): return lax.ppermute(value, AXES, [(i, i ^ mask) for i in range(DEVICES)])  27.5 us
    ppermute x15, waiting for transfers between devices, along_z(): return lax.ppermute(value, AXES, [(i, target(i)) for i in range(DEVICES)])  27.1 us
    ppermute x15, starting transfers between devices, along_z(): return lax.ppermute(value, AXES, [(i, target(i)) for i in range(DEVICES)])  22.5 us
    pallas_call x3, Pallas kernels, input_gradient(): pl.pallas_call(input_gradient_kernel, grid=(steps,), in_specs=[pl.BlockSp...  21.3 us
  transfers between devices with their start and end apart: 56, of which 19 were waited for; matrix products, arithmetic and copies ran while one was open for 4% of the time, Pallas kernels for 31%

profile of v3, /device:TPU:0, one launch (start us, length us, event | category | flops | bytes accessed | tf_op | source)
XLA Modules:
  0.0 363.7 jit_solution(14319016712433683491)
XLA Ops:
  2.5 2.3 pack_attention.1
  4.8 5.0 %collective-permute-start.2 = (bf16[160,384]{1,0:T(8,128)(2,1)}, bf16[160,384]{1,0:T(8,128)(2,1)S(1)}, u32[]{:S(2)}, u32[]{:S(2)}) collective-permute-start(bf16[160,384]{1,0:T(8,128)(2,1)} %pack_attention.1), channel_id=1, source_target_pairs={{0,12},{1,13},{2,14},{3,15},{4,0},{5,1},{6,2},{7,3},{8,4},{9,5},{1... | collective-permute-start | bytes 368648 | tf_op jit(solution)/shard_map/ppermute | solution.py:782
  16.8 2.5 pack_feedforward.1
  21.6 1.6 collective-permute-start.4
  23.2 1.5 collective-permute-start.3
  25.9 9.6 %collective-permute-done.5 = bf16[448,384]{1,0:T(8,128)(2,1)S(1)} collective-permute-done((bf16[448,384]{1,0:T(8,128)(2,1)}, bf16[448,384]{1,0:T(8,128)(2,1)S(1)}, u32[]{:S(2)}, u32[]{:S(2)}) %collective-permute-start.5) | collective-permute-done | bytes 344096 | tf_op jit(solution)/shard_map/ppermute | solution.py:782
  35.6 1.5 collective-permute-start.7
  39.1 2.7 collective-permute-done.7.rest_4_
  41.8 1.4 collective-permute-done.6.rest_3_
  43.3 1.4 collective-permute-start.8
  46.6 4.0 %collective-permute-done.8 = bf16[448,384]{1,0:T(8,128)(2,1)S(1)} collective-permute-done((bf16[448,384]{1,0:T(8,128)(2,1)S(1)}, bf16[448,384]{1,0:T(8,128)(2,1)S(1)}, u32[]{:S(2)}, u32[]{:S(2)}) %collective-permute-start.8) | collective-permute-done | bytes 344096 | tf_op jit(solution)/shard_map/ppermute | solution.py:782
  51.6 2.6 collective-permute-start.16
  54.3 14.2 %attention_forward.2 = (bf16[2048,2304]{1,0:T(8,128)(2,1)}, bf16[2048,768]{1,0:T(8,128)(2,1)}, bf16[768,2304]{1,0:T(8,128)(2,1)}, f32[8,2304]{1,0:T(8,128)}) custom-call(s32[4]{0:T(128)} %pad_add_fusion.place_ref, bf16[2048,768]{1,0:T(8,128)(2,1)} %bitcast.146, s32[16,128]{1,0:T(8,128)} %seg_ref.9, bf16[4,160,384]{2,1,0:T(8,128)(2,1)} %copy-done.7, ...), custom_call_target="tpu_custom_call" | custom-call | flops 4429185024 | bytes 11403264 | tf_op jit(solution)/shard_map/attention_forward/pallas_call | solution.py:233
  68.7 1.9 collective-permute-start.18
  70.6 2.0 collective-permute-start.17
  73.2 11.5 %attention_forward.3 = (bf16[2048,2304]{1,0:T(8,128)(2,1)}, bf16[2048,768]{1,0:T(8,128)(2,1)}) custom-call(bf16[2048,768]{1,0:T(8,128)(2,1)} %bitcast.147, s32[16,128]{1,0:T(8,128)} %seg_ref.9, bf16[768,2304]{1,0:T(8,128)(2,1)} %get-tuple-element.196.w_ref, f32[8,2304]{1,0:T(8,128)} %get-tuple-element.197.bias_ref, ...), custom_call_target="tpu_custom_call", output_to_operand_aliasing={{0}: (4, {}), {1}: (5, {})} | custom-call | flops 4429185024 | bytes 11403264 | tf_op jit(solution)/shard_map/attention_forward/pallas_call | solution.py:210
  86.0 16.6 %collective-permute-done.19.rest_6_ = bf16[2,448,384]{2,1,0:T(8,128)(2,1)S(1)} collective-permute-done((bf16[2,448,384]{2,1,0:T(8,128)(2,1)S(1)}, bf16[2,448,384]{2,1,0:T(8,128)(2,1)S(1)}, u32[]{:S(2)}, u32[]{:S(2)}) %collective-permute-start.19) | collective-permute-done | bytes 688160 | tf_op jit(solution)/shard_map/ppermute | solution.py:775
  105.9 68.7 %feedforward.1 = (f32[16,4,768]{2,1,0:T(4,128)}, bf16[2048,3072]{1,0:T(8,128)(2,1)}, bf16[2048,3072]{1,0:T(8,128)(2,1)}, bf16[2048,768]{1,0:T(8,128)(2,1)}, bf16...) custom-call(s32[4]{0:T(128)} %pad_add_fusion.place_ref, ...), custom_call_target="tpu_custom_call" | custom-call | flops 43486543872 | bytes 62914560 | tf_op jit(solution)/shard_map/feedforward/pallas_call | solution.py:476
  174.7 22.6 %up_gradient.1 = (bf16[2,2,4,256,384]{4,3,2,1,0:T(8,128)(2,1)}, bf16[2,2,4,256,384]{4,3,2,1,0:T(8,128)(2,1)}) custom-call(s32[4]{0:T(128)} %pad_add_fusion.place_ref, bf16[2048,768]{1,0:T(8,128)(2,1)} %get-tuple-element.208.normed_ref, bf16[2048,3072]{1,0:T(8,128)(2,1)} %get-tuple-element.209.hidden_ref, bf16[2048,768]{1,0:T(8,128)(2,1)} %get-tuple-element.202.ctx_ref, ...), custom_call_target="tpu_custom_call" | custom-call | flops 12079595520 | bytes 22142976 | tf_op jit(solution)/shard_map/up_gradient/pallas_call | solution.py:724
  197.4 16.8 %down_gradient.1 = (bf16[2,2,4,192,384]{4,3,2,1,0:T(8,128)(2,1)}, bf16[2,2,4,192,384]{4,3,2,1,0:T(8,128)(2,1)}) custom-call(s32[4]{0:T(128)} %pad_add_fusion.place_ref, bf16[2048,3072]{1,0:T(8,128)(2,1)} %get-tuple-element.218.active_ref, bf16[2048,768]{1,0:T(8,128)(2,1)} %get-tuple-element.219.branch_ref), custom_call_target="tpu_custom_call" | custom-call | flops 9663676416 | bytes 15728640 | tf_op jit(solution)/shard_map/down_gradient/pallas_call | solution.py:724
  214.2 2.2 fusion.1
  216.4 2.2 fusion
  220.1 16.2 %attention_backward.2 = (bf16[2048,2304]{1,0:T(8,128)(2,1)}, f32[8,1536]{1,0:T(8,128)}) custom-call(bf16[2048,2304]{1,0:T(8,128)(2,1)} %get-tuple-element.228.qkv_ref, bf16[2048,768]{1,0:T(8,128)(2,1)} %get-tuple-element.229.grad_ref, s32[16,128]{1,0:T(8,128)} %seg_ref.9), custom_call_target="tpu_custom_call" | custom-call | flops 2013265920 | bytes 11010048 | tf_op jit(solution)/shard_map/attention_backward/pallas_call | solution.py:530
  236.3 2.6 collective-permute-done.30
  239.0 2.0 fusion.8
  241.0 2.0 fusion.7
  243.0 1.7 fusion.4
  244.7 1.8 collective-permute-start.35
  248.8 16.3 %attention_backward.3 = (bf16[2048,2304]{1,0:T(8,128)(2,1)}, f32[8,1536]{1,0:T(8,128)}) custom-call(bf16[2048,2304]{1,0:T(8,128)(2,1)} %get-tuple-element.228.qkv_ref, bf16[2048,768]{1,0:T(8,128)(2,1)} %get-tuple-element.229.grad_ref, s32[16,128]{1,0:T(8,128)} %seg_ref.9, ...), custom_call_target="tpu_custom_call", output_to_operand_aliasing={{0}: (3, {})} | custom-call | flops 2013265920 | bytes 11010048 | tf_op jit(solution)/shard_map/attention_backward/pallas_call | solution.py:530
  265.1 3.9 %collective-permute-done.33 = bf16[2,256,384]{2,1,0:T(8,128)(2,1)S(1)} collective-permute-done((bf16[2,256,384]{2,1,0:T(8,128)(2,1)S(1)}, bf16[2,256,384]{2,1,0:T(8,128)(2,1)S(1)}, u32[]{:S(2)}, u32[]{:S(2)}) %collective-permute-start.33) | collective-permute-done | bytes 393248 | tf_op jit(solution)/shard_map/ppermute | solution.py:775
  269.0 2.1 fusion.3
  271.2 1.5 fusion.12
  272.7 1.7 collective-permute-start.38
  276.1 14.4 %qkv_gradient.1 = (bf16[2,2,4,160,384]{4,3,2,1,0:T(8,128)(2,1)}, bf16[2,2,4,160,384]{4,3,2,1,0:T(8,128)(2,1)}) custom-call(s32[4]{0:T(128)} %pad_add_fusion.place_ref, bf16[2048,768]{1,0:T(8,128)(2,1)} %bitcast.149, bf16[2048,2304]{1,0:T(8,128)(2,1)} %get-tuple-element.267.grad_ref, f32[8,1536]{1,0:T(8,128)} %get-tuple-element.256.sums_ref), custom_call_target="tpu_custom_call" | custom-call | flops 7247757312 | bytes 12607488 | tf_op jit(solution)/shard_map/qkv_gradient/pallas_call | solution.py:724
  293.3 1.8 fusion.10
  296.6 6.5 %input_gradient.3.outs_0_ = f32[2048,768]{1,0:T(8,128)} custom-call(f32[2048,768]{1,0:T(8,128)} %get-tuple-element.266.first_ref, bf16[2048,2304]{1,0:T(8,128)(2,1)} %get-tuple-element.267.grad_ref, bf16[768,2304]{1,0:T(8,128)(2,1)} %get-tuple-element.196.w_ref), custom_call_target="tpu_custom_call" | custom-call | flops 1811939328 | bytes 5505024 | tf_op jit(solution)/shard_map/input_gradient/pallas_call | solution.py:748
  306.1 1.4 collective-permute-start.44
  308.3 8.4 %input_gradient.4.outs_0_ = f32[2048,768]{1,0:T(8,128)} custom-call(f32[2048,768]{1,0:T(8,128)} %get-tuple-element.266.first_ref, bf16[2048,2304]{1,0:T(8,128)(2,1)} %get-tuple-element.267.grad_ref, bf16[768,2304]{1,0:T(8,128)(2,1)} %get-tuple-element.196.w_ref, f32[2048,768]{1,0:T(8,128)} %input_gradient.3.outs_0_), custom_call_target="tpu_custom_call", output_to_operand_aliasing={{}: (3, {})} | custom-call | flops 3623878656 | bytes 11010048 | tf_op jit(solution)/shard_map/input_gradient/pallas_call | solution.py:748
  316.7 3.0 collective-permute-done.44
  324.5 3.5 collective-permute-start.48
  327.9 1.6 collective-permute-start.50
  329.6 6.4 %input_gradient.5 = f32[2048,768]{1,0:T(8,128)} custom-call(f32[2048,768]{1,0:T(8,128)} %get-tuple-element.266.first_ref, bf16[2048,2304]{1,0:T(8,128)(2,1)} %get-tuple-element.267.grad_ref, bf16[768,2304]{1,0:T(8,128)(2,1)} %get-tuple-element.196.w_ref, f32[2048,768]{1,0:T(8,128)} %input_gradient.4.outs_0_), custom_call_target="tpu_custom_call", output_to_operand_aliasing={{}: (3, {})} | custom-call | flops 1811939328 | bytes 5505024 | tf_op jit(solution)/shard_map/input_gradient/pallas_call | solution.py:748
  335.9 4.3 %collective-permute-done.49 = bf16[192,384]{1,0:T(8,128)(2,1)S(1)} collective-permute-done((bf16[192,384]{1,0:T(8,128)(2,1)}, bf16[192,384]{1,0:T(8,128)(2,1)S(1)}, u32[]{:S(2)}, u32[]{:S(2)}) %collective-permute-start.49) | collective-permute-done | bytes 147488 | tf_op jit(solution)/shard_map/ppermute | solution.py:782
  340.9 1.6 fusion.17
  345.6 1.4 collective-permute-start.52
  347.0 1.9 collective-permute-start.53
  350.5 7.2 %collective-permute-done.52 = bf16[160,384]{1,0:T(8,128)(2,1)S(1)} collective-permute-done((bf16[160,384]{1,0:T(8,128)(2,1)S(1)}, bf16[160,384]{1,0:T(8,128)(2,1)S(1)}, u32[]{:S(2)}, u32[]{:S(2)}) %collective-permute-start.52) | collective-permute-done | bytes 122912 | tf_op jit(solution)/shard_map/ppermute | solution.py:782
  359.1 3.5 collective-permute-done.55
  (213 shorter events, 48.6 us)
Async XLA Ops:
  4.8 14.5 %collective-permute-start.2 = (bf16[160,384]{1,0:T(8,128)(2,1)}, bf16[160,384]{1,0:T(8,128)(2,1)S(1)}, u32[]{:S(2)}, u32[]{:S(2)}) collective-permute-start(bf16[160,384]{1,0:T(8,128)(2,1)} %pack_attention.1), channel_id=1, source_target_pairs={{0,12},{1,13},{2,14},{3,15},{4,0},{5,1},{6,2},{7,3},{8,4},{9,5},{1... | collective-permute-start | bytes 368648 | tf_op jit(solution)/shard_map/ppermute | solution.py:782
  9.8 10.8 %collective-permute-start.1 = (bf16[160,384]{1,0:T(8,128)(2,1)}, bf16[160,384]{1,0:T(8,128)(2,1)S(1)}, u32[]{:S(2)}, u32[]{:S(2)}) collective-permute-start(bf16[160,384]{1,0:T(8,128)(2,1)} %pack_attention.1), channel_id=1, source_target_pairs={{0,8},{1,9},{2,10},{3,11},{4,12},{5,13},{6,14},{7,15},{8,0},{9,1},... | collective-permute-start | bytes 368648 | tf_op jit(solution)/shard_map/ppermute | solution.py:782
  9.8 10.8 %collective-permute-start = (bf16[160,384]{1,0:T(8,128)(2,1)}, bf16[160,384]{1,0:T(8,128)(2,1)S(1)}, u32[]{:S(2)}, u32[]{:S(2)}) collective-permute-start(bf16[160,384]{1,0:T(8,128)(2,1)} %pack_attention.1), channel_id=1, source_target_pairs={{0,4},{1,5},{2,6},{3,7},{4,8},{5,9},{6,10},{7,11},{8,12},{9,13},{1... | collective-permute-start | bytes 368648 | tf_op jit(solution)/shard_map/ppermute | solution.py:782
  21.6 13.8 %collective-permute-start.4 = (bf16[4,160,384]{2,1,0:T(8,128)(2,1)S(1)}, bf16[4,160,384]{2,1,0:T(8,128)(2,1)S(1)}, u32[]{:S(2)}, u32[]{:S(2)}) collective-permute-start(bf16[4,160,384]{2,1,0:T(8,128)(2,1)S(1)} %pad_maximum_fusion.3.rest_0_), channel_id=1, source_target_pairs={{0,16},{1,17},{2,18},{3,19},{4,20},{5,21},{6,22},{7,23},{8,24},{9,... | collective-permute-start | bytes 1474568 | tf_op jit(solution)/shard_map/ppermute | solution.py:775
  23.2 12.3 %collective-permute-start.3 = (bf16[4,160,384]{2,1,0:T(8,128)(2,1)S(1)}, bf16[4,160,384]{2,1,0:T(8,128)(2,1)S(1)}, u32[]{:S(2)}, u32[]{:S(2)}) collective-permute-start(bf16[4,160,384]{2,1,0:T(8,128)(2,1)S(1)} %pad_maximum_fusion.3.rest_0_), channel_id=1, source_target_pairs={{0,2},{1,3},{2,0},{3,1},{4,6},{5,7},{6,4},{7,5},{8,10},{9,11},{10,... | collective-permute-start | bytes 1474568 | tf_op jit(solution)/shard_map/ppermute | solution.py:775
  24.7 10.8 %collective-permute-start.5 = (bf16[448,384]{1,0:T(8,128)(2,1)}, bf16[448,384]{1,0:T(8,128)(2,1)S(1)}, u32[]{:S(2)}, u32[]{:S(2)}) collective-permute-start(bf16[448,384]{1,0:T(8,128)(2,1)} %pack_feedforward.1), channel_id=1, source_target_pairs={{0,4},{1,5},{2,6},{3,7},{4,8},{5,9},{6,10},{7,11},{8,12},{9,13},{1... | collective-permute-start | bytes 1032200 | tf_op jit(solution)/shard_map/ppermute | solution.py:782
  25.9 18.8 %collective-permute-start.9 = (bf16[4,160,384]{2,1,0:T(8,128)(2,1)S(1)}, bf16[4,160,384]{2,1,0:T(8,128)(2,1)S(1)}, u32[]{:S(2)}, u32[]{:S(2)}) collective-permute-start(bf16[4,160,384]{2,1,0:T(8,128)(2,1)S(1)} %pad_maximum_fusion.3.rest_0_), channel_id=1, source_target_pairs={{0,1},{1,0},{2,3},{3,2},{4,5},{5,4},{6,7},{7,6},{8,9},{9,8},{10,11... | collective-permute-start | bytes 1474568 | tf_op jit(solution)/shard_map/ppermute | solution.py:775
  35.6 6.3 %collective-permute-start.7 = (bf16[2,160,384]{2,1,0:T(8,128)(2,1)S(1)}, bf16[2,160,384]{2,1,0:T(8,128)(2,1)S(1)}, u32[]{:S(2)}, u32[]{:S(2)}) collective-permute-start(bf16[2,160,384]{2,1,0:T(8,128)(2,1)S(1)} %slice.308), channel_id=1, source_target_pairs={{0,2},{1,3},{2,0},{3,1},{4,6},{5,7},{6,4},{7,5},{8,10},{9,11},{10,... | collective-permute-start | bytes 737288 | tf_op jit(solution)/shard_map/ppermute | solution.py:775
  37.6 7.6 %collective-permute-start.10 = (bf16[4,160,384]{2,1,0:T(8,128)(2,1)S(1)}, bf16[4,160,384]{2,1,0:T(8,128)(2,1)S(1)}, u32[]{:S(2)}, u32[]{:S(2)}) collective-permute-start(bf16[4,160,384]{2,1,0:T(8,128)(2,1)S(1)} %collective-permute-done.3.rest_1_), channel_id=1, source_target_pairs={{0,1},{1,0},{2,3},{3,2},{4,5},{5,4},{6,7},{7,6},{8,9},{9,8},{10,11... | collective-permute-start | bytes 1474568 | tf_op jit(solution)/shard_map/ppermute | solution.py:775
  37.6 7.6 %collective-permute-start.11 = (bf16[4,160,384]{2,1,0:T(8,128)(2,1)S(1)}, bf16[4,160,384]{2,1,0:T(8,128)(2,1)S(1)}, u32[]{:S(2)}, u32[]{:S(2)}) collective-permute-start(bf16[4,160,384]{2,1,0:T(8,128)(2,1)S(1)} %collective-permute-done.4.rest_2_), channel_id=1, source_target_pairs={{0,1},{1,0},{2,3},{3,2},{4,5},{5,4},{6,7},{7,6},{8,9},{9,8},{10,11... | collective-permute-start | bytes 1474568 | tf_op jit(solution)/shard_map/ppermute | solution.py:775
  43.3 7.3 %collective-permute-start.8 = (bf16[448,384]{1,0:T(8,128)(2,1)S(1)}, bf16[448,384]{1,0:T(8,128)(2,1)S(1)}, u32[]{:S(2)}, u32[]{:S(2)}) collective-permute-start(bf16[448,384]{1,0:T(8,128)(2,1)S(1)} %copy-done.3), channel_id=1, source_target_pairs={{0,12},{1,13},{2,14},{3,15},{4,0},{5,1},{6,2},{7,3},{8,4},{9,5},{1... | collective-permute-start | bytes 1032200 | tf_op jit(solution)/shard_map/ppermute | solution.py:782
  50.5 18.0 %collective-permute-start.15 = (bf16[2,448,384]{2,1,0:T(8,128)(2,1)S(1)}, bf16[2,448,384]{2,1,0:T(8,128)(2,1)S(1)}, u32[]{:S(2)}, u32[]{:S(2)}) collective-permute-start(bf16[2,448,384]{2,1,0:T(8,128)(2,1)S(1)} %pad_maximum_fusion.rest_0_), channel_id=1, source_target_pairs={{0,16},{1,17},{2,18},{3,19},{4,20},{5,21},{6,22},{7,23},{8,24},{9,... | collective-permute-start | bytes 2064392 | tf_op jit(solution)/shard_map/ppermute | solution.py:775
  51.0 17.5 %collective-permute-start.14 = (bf16[2,448,384]{2,1,0:T(8,128)(2,1)S(1)}, bf16[2,448,384]{2,1,0:T(8,128)(2,1)S(1)}, u32[]{:S(2)}, u32[]{:S(2)}) collective-permute-start(bf16[2,448,384]{2,1,0:T(8,128)(2,1)S(1)} %pad_maximum_fusion.rest_0_), channel_id=1, source_target_pairs={{0,2},{1,3},{2,0},{3,1},{4,6},{5,7},{6,4},{7,5},{8,10},{9,11},{10,... | collective-permute-start | bytes 2064392 | tf_op jit(solution)/shard_map/ppermute | solution.py:775
  51.6 16.9 %collective-permute-start.16 = (bf16[448,384]{1,0:T(8,128)(2,1)S(1)}, bf16[448,384]{1,0:T(8,128)(2,1)S(1)}, u32[]{:S(2)}, u32[]{:S(2)}) collective-permute-start(bf16[448,384]{1,0:T(8,128)(2,1)S(1)} %copy-done.3), channel_id=1, source_target_pairs={{0,8},{1,9},{2,10},{3,11},{4,12},{5,13},{6,14},{7,15},{8,0},{9,1},... | collective-permute-start | bytes 1032200 | tf_op jit(solution)/shard_map/ppermute | solution.py:782
  68.7 16.0 %collective-permute-start.18 = (bf16[2,448,384]{2,1,0:T(8,128)(2,1)S(1)}, bf16[2,448,384]{2,1,0:T(8,128)(2,1)S(1)}, u32[]{:S(2)}, u32[]{:S(2)}) collective-permute-start(bf16[2,448,384]{2,1,0:T(8,128)(2,1)S(1)} %pad_maximum_fusion.1.rest_1_), channel_id=1, source_target_pairs={{0,16},{1,17},{2,18},{3,19},{4,20},{5,21},{6,22},{7,23},{8,24},{9,... | collective-permute-start | bytes 2064392 | tf_op jit(solution)/shard_map/ppermute | solution.py:775
  70.6 14.3 %collective-permute-start.17 = (bf16[2,448,384]{2,1,0:T(8,128)(2,1)S(1)}, bf16[2,448,384]{2,1,0:T(8,128)(2,1)S(1)}, u32[]{:S(2)}, u32[]{:S(2)}) collective-permute-start(bf16[2,448,384]{2,1,0:T(8,128)(2,1)S(1)} %pad_maximum_fusion.1.rest_1_), channel_id=1, source_target_pairs={{0,2},{1,3},{2,0},{3,1},{4,6},{5,7},{6,4},{7,5},{8,10},{9,11},{10,... | collective-permute-start | bytes 2064392 | tf_op jit(solution)/shard_map/ppermute | solution.py:775
  72.6 12.4 %collective-permute-start.21 = (bf16[2,448,384]{2,1,0:T(8,128)(2,1)S(1)}, bf16[2,448,384]{2,1,0:T(8,128)(2,1)S(1)}, u32[]{:S(2)}, u32[]{:S(2)}) collective-permute-start(bf16[2,448,384]{2,1,0:T(8,128)(2,1)S(1)} %pad_maximum_fusion.rest_0_), channel_id=1, source_target_pairs={{0,1},{1,0},{2,3},{3,2},{4,5},{5,4},{6,7},{7,6},{8,9},{9,8},{10,11... | collective-permute-start | bytes 2064392 | tf_op jit(solution)/shard_map/ppermute | solution.py:775
  72.6 12.9 %collective-permute-start.22 = (bf16[2,448,384]{2,1,0:T(8,128)(2,1)S(1)}, bf16[2,448,384]{2,1,0:T(8,128)(2,1)}, u32[]{:S(2)}, u32[]{:S(2)}) collective-permute-start(bf16[2,448,384]{2,1,0:T(8,128)(2,1)S(1)} %pad_maximum_fusion.1.rest_1_), channel_id=1, source_target_pairs={{0,1},{1,0},{2,3},{3,2},{4,5},{5,4},{6,7},{7,6},{8,9},{9,8},{10,11... | collective-permute-start | bytes 2064392 | tf_op jit(solution)/shard_map/ppermute | solution.py:775
  73.2 12.5 %collective-permute-start.25 = (bf16[2,448,384]{2,1,0:T(8,128)(2,1)S(1)}, bf16[2,448,384]{2,1,0:T(8,128)(2,1)}, u32[]{:S(2)}, u32[]{:S(2)}) collective-permute-start(bf16[2,448,384]{2,1,0:T(8,128)(2,1)S(1)} %collective-permute-done.15.rest_4_), channel_id=1, source_target_pairs={{0,1},{1,0},{2,3},{3,2},{4,5},{5,4},{6,7},{7,6},{8,9},{9,8},{10,11... | collective-permute-start | bytes 2064392 | tf_op jit(solution)/shard_map/ppermute | solution.py:775
  84.7 17.9 %collective-permute-start.19 = (bf16[2,448,384]{2,1,0:T(8,128)(2,1)S(1)}, bf16[2,448,384]{2,1,0:T(8,128)(2,1)S(1)}, u32[]{:S(2)}, u32[]{:S(2)}) collective-permute-start(bf16[2,448,384]{2,1,0:T(8,128)(2,1)S(1)} %collective-permute-done.14.rest_2_), channel_id=1, source_target_pairs={{0,16},{1,17},{2,18},{3,19},{4,20},{5,21},{6,22},{7,23},{8,24},{9,... | collective-permute-start | bytes 2064392 | tf_op jit(solution)/shard_map/ppermute | solution.py:775
  84.9 17.9 %collective-permute-start.20 = (bf16[2,448,384]{2,1,0:T(8,128)(2,1)S(1)}, bf16[2,448,384]{2,1,0:T(8,128)(2,1)S(1)}, u32[]{:S(2)}, u32[]{:S(2)}) collective-permute-start(bf16[2,448,384]{2,1,0:T(8,128)(2,1)S(1)} %collective-permute-done.18.rest_5_), channel_id=1, source_target_pairs={{0,2},{1,3},{2,0},{3,1},{4,6},{5,7},{6,4},{7,5},{8,10},{9,11},{10,... | collective-permute-start | bytes 2064392 | tf_op jit(solution)/shard_map/ppermute | solution.py:775
  85.1 18.1 %collective-permute-start.23 = (bf16[2,448,384]{2,1,0:T(8,128)(2,1)S(1)}, bf16[2,448,384]{2,1,0:T(8,128)(2,1)S(1)}, u32[]{:S(2)}, u32[]{:S(2)}) collective-permute-start(bf16[2,448,384]{2,1,0:T(8,128)(2,1)S(1)} %collective-permute-done.14.rest_2_), channel_id=1, source_target_pairs={{0,1},{1,0},{2,3},{3,2},{4,5},{5,4},{6,7},{7,6},{8,9},{9,8},{10,11... | collective-permute-start | bytes 2064392 | tf_op jit(solution)/shard_map/ppermute | solution.py:775
  85.5 17.7 %collective-permute-start.26 = (bf16[2,448,384]{2,1,0:T(8,128)(2,1)S(1)}, bf16[2,448,384]{2,1,0:T(8,128)(2,1)S(1)}, u32[]{:S(2)}, u32[]{:S(2)}) collective-permute-start(bf16[2,448,384]{2,1,0:T(8,128)(2,1)S(1)} %collective-permute-done.18.rest_5_), channel_id=1, source_target_pairs={{0,1},{1,0},{2,3},{3,2},{4,5},{5,4},{6,7},{7,6},{8,9},{9,8},{10,11... | collective-permute-start | bytes 2064392 | tf_op jit(solution)/shard_map/ppermute | solution.py:775
  85.6 17.5 %collective-permute-start.24 = (bf16[2,448,384]{2,1,0:T(8,128)(2,1)S(1)}, bf16[2,448,384]{2,1,0:T(8,128)(2,1)S(1)}, u32[]{:S(2)}, u32[]{:S(2)}) collective-permute-start(bf16[2,448,384]{2,1,0:T(8,128)(2,1)S(1)} %collective-permute-done.17.rest_3_), channel_id=1, source_target_pairs={{0,1},{1,0},{2,3},{3,2},{4,5},{5,4},{6,7},{7,6},{8,9},{9,8},{10,11... | collective-permute-start | bytes 2064392 | tf_op jit(solution)/shard_map/ppermute | solution.py:775
  197.3 16.9 %collective-permute-start.29 = (bf16[2,2,4,256,384]{4,3,2,1,0:T(8,128)(2,1)}, bf16[2,2,4,256,384]{4,3,2,1,0:T(8,128)(2,1)}, u32[]{:S(2)}, u32[]{:S(2)}) collective-permute-start(bf16[2,2,4,256,384]{4,3,2,1,0:T(8,128)(2,1)} %get-tuple-element.217), channel_id=1, source_target_pairs={{0,1},{1,0},{2,3},{3,2},{4,5},{5,4},{6,7},{7,6},{8,9},{9,8},{10,11... | collective-permute-start | bytes 9437192 | tf_op jit(solution)/shard_map/ppermute | solution.py:775
  218.7 20.3 %collective-permute-start.32 = (bf16[2,2,4,192,384]{4,3,2,1,0:T(8,128)(2,1)}, bf16[2,2,4,192,384]{4,3,2,1,0:T(8,128)(2,1)}, u32[]{:S(2)}, u32[]{:S(2)}) collective-permute-start(bf16[2,2,4,192,384]{4,3,2,1,0:T(8,128)(2,1)} %get-tuple-element.227), channel_id=1, source_target_pairs={{0,1},{1,0},{2,3},{3,2},{4,5},{5,4},{6,7},{7,6},{8,9},{9,8},{10,11... | collective-permute-start | bytes 7077896 | tf_op jit(solution)/shard_map/ppermute | solution.py:775
  219.1 19.9 %collective-permute-start.30 = (bf16[2,2,256,384]{3,2,1,0:T(8,128)(2,1)}, bf16[2,2,256,384]{3,2,1,0:T(8,128)(2,1)}, u32[]{:S(2)}, u32[]{:S(2)}) collective-permute-start(bf16[2,2,256,384]{3,2,1,0:T(8,128)(2,1)} %fusion), channel_id=1, source_target_pairs={{0,2},{1,3},{2,0},{3,1},{4,6},{5,7},{6,4},{7,5},{8,10},{9,11},{10,... | collective-permute-start | bytes 2359304 | tf_op jit(solution)/shard_map/ppermute | solution.py:775
  219.1 19.9 %collective-permute-start.31 = (bf16[2,2,256,384]{3,2,1,0:T(8,128)(2,1)}, bf16[2,2,256,384]{3,2,1,0:T(8,128)(2,1)}, u32[]{:S(2)}, u32[]{:S(2)}) collective-permute-start(bf16[2,2,256,384]{3,2,1,0:T(8,128)(2,1)} %fusion.1), channel_id=1, source_target_pairs={{0,16},{1,17},{2,18},{3,19},{4,20},{5,21},{6,22},{7,23},{8,24},{9,... | collective-permute-start | bytes 2359304 | tf_op jit(solution)/shard_map/ppermute | solution.py:775
  244.7 24.4 %collective-permute-start.35 = (bf16[2,2,192,384]{3,2,1,0:T(8,128)(2,1)}, bf16[2,2,192,384]{3,2,1,0:T(8,128)(2,1)S(1)}, u32[]{:S(2)}, u32[]{:S(2)}) collective-permute-start(bf16[2,2,192,384]{3,2,1,0:T(8,128)(2,1)} %fusion.7), channel_id=1, source_target_pairs={{0,2},{1,3},{2,0},{3,1},{4,6},{5,7},{6,4},{7,5},{8,10},{9,11},{10,... | collective-permute-start | bytes 1769480 | tf_op jit(solution)/shard_map/ppermute | solution.py:775
  246.5 22.6 %collective-permute-start.36 = (bf16[2,2,192,384]{3,2,1,0:T(8,128)(2,1)}, bf16[2,2,192,384]{3,2,1,0:T(8,128)(2,1)S(1)}, u32[]{:S(2)}, u32[]{:S(2)}) collective-permute-start(bf16[2,2,192,384]{3,2,1,0:T(8,128)(2,1)} %fusion.8), channel_id=1, source_target_pairs={{0,16},{1,17},{2,18},{3,19},{4,20},{5,21},{6,22},{7,23},{8,24},{9,... | collective-permute-start | bytes 1769480 | tf_op jit(solution)/shard_map/ppermute | solution.py:775
  247.2 21.8 %collective-permute-start.33 = (bf16[2,256,384]{2,1,0:T(8,128)(2,1)S(1)}, bf16[2,256,384]{2,1,0:T(8,128)(2,1)S(1)}, u32[]{:S(2)}, u32[]{:S(2)}) collective-permute-start(bf16[2,256,384]{2,1,0:T(8,128)(2,1)S(1)} %get-tuple-element.237), channel_id=1, source_target_pairs={{0,16},{1,17},{2,18},{3,19},{4,20},{5,21},{6,22},{7,23},{8,24},{9,... | collective-permute-start | bytes 1179656 | tf_op jit(solution)/shard_map/ppermute | solution.py:775
  248.5 20.5 %collective-permute-start.34 = (bf16[2,256,384]{2,1,0:T(8,128)(2,1)S(1)}, bf16[2,256,384]{2,1,0:T(8,128)(2,1)}, u32[]{:S(2)}, u32[]{:S(2)}) collective-permute-start(bf16[2,256,384]{2,1,0:T(8,128)(2,1)S(1)} %get-tuple-element.238), channel_id=1, source_target_pairs={{0,2},{1,3},{2,0},{3,1},{4,6},{5,7},{6,4},{7,5},{8,10},{9,11},{10,... | collective-permute-start | bytes 1179656 | tf_op jit(solution)/shard_map/ppermute | solution.py:775
  272.7 17.9 %collective-permute-start.37 = (bf16[256,384]{1,0:T(8,128)(2,1)S(1)}, bf16[256,384]{1,0:T(8,128)(2,1)S(1)}, u32[]{:S(2)}, u32[]{:S(2)}) collective-permute-start(bf16[256,384]{1,0:T(8,128)(2,1)S(1)} %get-tuple-element.250), channel_id=1, source_target_pairs={{0,12},{1,13},{2,14},{3,15},{4,0},{5,1},{6,2},{7,3},{8,4},{9,5},{1... | collective-permute-start | bytes 589832 | tf_op jit(solution)/shard_map/ppermute | solution.py:782
  272.7 17.8 %collective-permute-start.38 = (bf16[256,384]{1,0:T(8,128)(2,1)S(1)}, bf16[256,384]{1,0:T(8,128)(2,1)S(1)}, u32[]{:S(2)}, u32[]{:S(2)}) collective-permute-start(bf16[256,384]{1,0:T(8,128)(2,1)S(1)} %get-tuple-element.251), channel_id=1, source_target_pairs={{0,8},{1,9},{2,10},{3,11},{4,12},{5,13},{6,14},{7,15},{8,0},{9,1},... | collective-permute-start | bytes 589832 | tf_op jit(solution)/shard_map/ppermute | solution.py:782
  274.4 16.2 %collective-permute-start.39 = (bf16[256,384]{1,0:T(8,128)(2,1)S(1)}, bf16[256,384]{1,0:T(8,128)(2,1)S(1)}, u32[]{:S(2)}, u32[]{:S(2)}) collective-permute-start(bf16[256,384]{1,0:T(8,128)(2,1)S(1)} %get-tuple-element.252), channel_id=1, source_target_pairs={{0,4},{1,5},{2,6},{3,7},{4,8},{5,9},{6,10},{7,11},{8,12},{9,13},{1... | collective-permute-start | bytes 589832 | tf_op jit(solution)/shard_map/ppermute | solution.py:782
  274.8 15.8 %collective-permute-start.40 = (bf16[2,192,384]{2,1,0:T(8,128)(2,1)S(1)}, bf16[2,192,384]{2,1,0:T(8,128)(2,1)S(1)}, u32[]{:S(2)}, u32[]{:S(2)}) collective-permute-start(bf16[2,192,384]{2,1,0:T(8,128)(2,1)S(1)} %get-tuple-element.253), channel_id=1, source_target_pairs={{0,16},{1,17},{2,18},{3,19},{4,20},{5,21},{6,22},{7,23},{8,24},{9,... | collective-permute-start | bytes 884744 | tf_op jit(solution)/shard_map/ppermute | solution.py:775
  275.5 15.1 %collective-permute-start.41 = (bf16[2,192,384]{2,1,0:T(8,128)(2,1)S(1)}, bf16[2,192,384]{2,1,0:T(8,128)(2,1)S(1)}, u32[]{:S(2)}, u32[]{:S(2)}) collective-permute-start(bf16[2,192,384]{2,1,0:T(8,128)(2,1)S(1)} %get-tuple-element.254), channel_id=1, source_target_pairs={{0,2},{1,3},{2,0},{3,1},{4,6},{5,7},{6,4},{7,5},{8,10},{9,11},{10,... | collective-permute-start | bytes 884744 | tf_op jit(solution)/shard_map/ppermute | solution.py:775
  292.1 11.0 %collective-permute-start.42 = (bf16[2,2,4,160,384]{4,3,2,1,0:T(8,128)(2,1)}, bf16[2,2,4,160,384]{4,3,2,1,0:T(8,128)(2,1)S(1)}, u32[]{:S(2)}, u32[]{:S(2)}) collective-permute-start(bf16[2,2,4,160,384]{4,3,2,1,0:T(8,128)(2,1)} %get-tuple-element.264), channel_id=1, source_target_pairs={{0,1},{1,0},{2,3},{3,2},{4,5},{5,4},{6,7},{7,6},{8,9},{9,8},{10,11... | collective-permute-start | bytes 5898248 | tf_op jit(solution)/shard_map/ppermute | solution.py:775
  292.1 10.9 %collective-permute-start.43 = (bf16[240,384]{1,0:T(8,128)(2,1)}, bf16[240,384]{1,0:T(8,128)(2,1)}, u32[]{:S(2)}, u32[]{:S(2)}) collective-permute-start(bf16[240,384]{1,0:T(8,128)(2,1)} %slice.550), channel_id=1, source_target_pairs={{0,16},{1,17},{2,18},{3,19},{4,20},{5,21},{6,22},{7,23},{8,24},{9,... | collective-permute-start | bytes 552968 | tf_op jit(solution)/shard_map/ppermute | solution.py:775
  306.1 13.7 %collective-permute-start.44 = (bf16[2,2,160,384]{3,2,1,0:T(8,128)(2,1)}, bf16[2,2,160,384]{3,2,1,0:T(8,128)(2,1)}, u32[]{:S(2)}, u32[]{:S(2)}) collective-permute-start(bf16[2,2,160,384]{3,2,1,0:T(8,128)(2,1)} %fusion.14), channel_id=1, source_target_pairs={{0,2},{1,3},{2,0},{3,1},{4,6},{5,7},{6,4},{7,5},{8,10},{9,11},{10,... | collective-permute-start | bytes 1474568 | tf_op jit(solution)/shard_map/ppermute | solution.py:775
  307.5 13.2 %collective-permute-start.45 = (bf16[2,2,160,384]{3,2,1,0:T(8,128)(2,1)S(1)}, bf16[2,2,160,384]{3,2,1,0:T(8,128)(2,1)}, u32[]{:S(2)}, u32[]{:S(2)}) collective-permute-start(bf16[2,2,160,384]{3,2,1,0:T(8,128)(2,1)S(1)} %fusion.15), channel_id=1, source_target_pairs={{0,16},{1,17},{2,18},{3,19},{4,20},{5,21},{6,22},{7,23},{8,24},{9,... | collective-permute-start | bytes 1474568 | tf_op jit(solution)/shard_map/ppermute | solution.py:775
  321.9 18.4 %collective-permute-start.46 = (bf16[2,160,384]{2,1,0:T(8,128)(2,1)S(1)}, bf16[2,160,384]{2,1,0:T(8,128)(2,1)}, u32[]{:S(2)}, u32[]{:S(2)}) collective-permute-start(bf16[2,160,384]{2,1,0:T(8,128)(2,1)S(1)} %get-tuple-element.279), channel_id=1, source_target_pairs={{0,16},{1,17},{2,18},{3,19},{4,20},{5,21},{6,22},{7,23},{8,24},{9,... | collective-permute-start | bytes 737288 | tf_op jit(solution)/shard_map/ppermute | solution.py:775
  322.8 18.2 %collective-permute-start.47 = (bf16[2,160,384]{2,1,0:T(8,128)(2,1)S(1)}, bf16[2,160,384]{2,1,0:T(8,128)(2,1)}, u32[]{:S(2)}, u32[]{:S(2)}) collective-permute-start(bf16[2,160,384]{2,1,0:T(8,128)(2,1)S(1)} %get-tuple-element.280), channel_id=1, source_target_pairs={{0,2},{1,3},{2,0},{3,1},{4,6},{5,7},{6,4},{7,5},{8,10},{9,11},{10,... | collective-permute-start | bytes 737288 | tf_op jit(solution)/shard_map/ppermute | solution.py:775
  324.5 11.5 %collective-permute-start.48 = (bf16[192,384]{1,0:T(8,128)(2,1)}, bf16[192,384]{1,0:T(8,128)(2,1)S(1)}, u32[]{:S(2)}, u32[]{:S(2)}) collective-permute-start(bf16[192,384]{1,0:T(8,128)(2,1)} %fusion.31), channel_id=1, source_target_pairs={{0,12},{1,13},{2,14},{3,15},{4,0},{5,1},{6,2},{7,3},{8,4},{9,5},{1... | collective-permute-start | bytes 442376 | tf_op jit(solution)/shard_map/ppermute | solution.py:782
  327.9 12.3 %collective-permute-start.49 = (bf16[192,384]{1,0:T(8,128)(2,1)}, bf16[192,384]{1,0:T(8,128)(2,1)S(1)}, u32[]{:S(2)}, u32[]{:S(2)}) collective-permute-start(bf16[192,384]{1,0:T(8,128)(2,1)} %get-tuple-element.282), channel_id=1, source_target_pairs={{0,8},{1,9},{2,10},{3,11},{4,12},{5,13},{6,14},{7,15},{8,0},{9,1},... | collective-permute-start | bytes 442376 | tf_op jit(solution)/shard_map/ppermute | solution.py:782
  327.9 12.3 %collective-permute-start.50 = (bf16[192,384]{1,0:T(8,128)(2,1)}, bf16[192,384]{1,0:T(8,128)(2,1)}, u32[]{:S(2)}, u32[]{:S(2)}) collective-permute-start(bf16[192,384]{1,0:T(8,128)(2,1)} %get-tuple-element.283), channel_id=1, source_target_pairs={{0,4},{1,5},{2,6},{3,7},{4,8},{5,9},{6,10},{7,11},{8,12},{9,13},{1... | collective-permute-start | bytes 442376 | tf_op jit(solution)/shard_map/ppermute | solution.py:782
  345.6 12.1 %collective-permute-start.52 = (bf16[160,384]{1,0:T(8,128)(2,1)S(1)}, bf16[160,384]{1,0:T(8,128)(2,1)S(1)}, u32[]{:S(2)}, u32[]{:S(2)}) collective-permute-start(bf16[160,384]{1,0:T(8,128)(2,1)S(1)} %get-tuple-element.289), channel_id=1, source_target_pairs={{0,8},{1,9},{2,10},{3,11},{4,12},{5,13},{6,14},{7,15},{8,0},{9,1},... | collective-permute-start | bytes 368648 | tf_op jit(solution)/shard_map/ppermute | solution.py:782
  347.0 10.7 %collective-permute-start.53 = (bf16[160,384]{1,0:T(8,128)(2,1)S(1)}, bf16[160,384]{1,0:T(8,128)(2,1)S(1)}, u32[]{:S(2)}, u32[]{:S(2)}) collective-permute-start(bf16[160,384]{1,0:T(8,128)(2,1)S(1)} %get-tuple-element.290), channel_id=1, source_target_pairs={{0,4},{1,5},{2,6},{3,7},{4,8},{5,9},{6,10},{7,11},{8,12},{9,13},{1... | collective-permute-start | bytes 368648 | tf_op jit(solution)/shard_map/ppermute | solution.py:782
  (42 other events, 397.6 us)

commit v4 on v3

--- a/solution.py
+++ b/solution.py
@@ -14,6 +14,7 @@
 F32 = jnp.float32
 BF16 = jnp.bfloat16
 VMEM_LIMIT = 60000 * 1024
+FF_ROWS = 2
 
 
 def product(left, right):
@@ -51,6 +52,17 @@
 def fold(values):
     rows, width = values.shape
     return jnp.sum(values.reshape(rows // 8, 8, width), axis=0)
+
+
+def interleave(work, first, second, third):
+    begun, done = {}, {}
+    for number in range(len(work) + 2):
+        if number < len(work):
+            begun[number] = first(*work[number])
+        if 0 <= number - 1 < len(work):
+            done[number - 1] = second(*work[number - 1], begun.pop(number - 1))
+        if number >= 2:
+            third(*work[number - 2], done.pop(number - 2))
 
 
 def lane_halves():
@@ -111,32 +123,36 @@
         cols = pl.ds(part * width, width)
         qkv_ref[:, cols] = (product(x, w_ref[:, cols]) + bias_ref[0:1, cols]).astype(BF16)
     low_half, high_half = lane_halves()
-    ones_low = jnp.broadcast_to(low_half, (length, PAIR))
-    ones_high = jnp.broadcast_to(high_half, (length, PAIR))
+    ones = jnp.concatenate(
+        [jnp.broadcast_to(low_half, (length, PAIR)), jnp.broadcast_to(high_half, (length, PAIR))], axis=0
+    )
     scale = HEAD**-0.5
+    masks = []
     for local in range(tokens // length):
+        along_lanes, along_rows = segment_grid(seg_ref, step * (tokens // length) + local, length)
+        masks.append(along_lanes == along_rows)
+
+    def score(local, pair):
         rows = pl.ds(local * length, length)
-        along_lanes, along_rows = segment_grid(seg_ref, step * (tokens // length) + local, length)
-        same = along_lanes == along_rows
-        for pair in range(width // PAIR):
-            q = qkv_ref[rows, pl.ds(pair * PAIR, PAIR)] * BF16(scale)
-            k = qkv_ref[rows, pl.ds(width + pair * PAIR, PAIR)]
-            v = qkv_ref[rows, pl.ds(2 * width + pair * PAIR, PAIR)]
-            scores = times_transpose(q, split_heads(k, low_half, high_half))
-            parts = []
-            for half in range(2):
-                masked = jnp.where(same, scores[:, half * length : (half + 1) * length], -1e30)
-                peak = jnp.max(masked, axis=-1, keepdims=True)
-                parts.append(jnp.exp(masked - peak).astype(BF16))
-            values = jnp.concatenate(
-                [
-                    split_heads(v, low_half, high_half),
-                    jnp.concatenate([ones_low, ones_high], axis=0),
-                ],
-                axis=1,
-            )
-            both = product(jnp.concatenate(parts, axis=1), values)
-            ctx_ref[rows, pl.ds(pair * PAIR, PAIR)] = (both[:, :PAIR] / both[:, PAIR:]).astype(BF16)
+        q = qkv_ref[rows, pl.ds(pair * PAIR, PAIR)] * BF16(scale)
+        k = qkv_ref[rows, pl.ds(width + pair * PAIR, PAIR)]
+        return times_transpose(q, split_heads(k, low_half, high_half))
+
+    def weigh(local, pair, scores):
+        parts = []
+        for half in range(2):
+            masked = jnp.where(masks[local], scores[:, half * length : (half + 1) * length], -1e30)
+            parts.append(jnp.exp(masked - jnp.max(masked, axis=-1, keepdims=True)).astype(BF16))
+        return jnp.concatenate(parts, axis=1)
+
+    def mix(local, pair, weights):
+        rows = pl.ds(local * length, length)
+        v = qkv_ref[rows, pl.ds(2 * width + pair * PAIR, PAIR)]
+        values = jnp.concatenate([split_heads(v, low_half, high_half), ones], axis=1)
+        both = product(weights, values)
+        ctx_ref[rows, pl.ds(pair * PAIR, PAIR)] = (both[:, :PAIR] / both[:, PAIR:]).astype(BF16)
+
+    interleave([(local, pair) for local in range(tokens // length) for pair in range(width // PAIR)], score, weigh, mix)
 
 
 def attention_gathered_kernel(length, width, place_ref, x_ref, seg_ref, *rest):
@@ -381,7 +397,7 @@
     )
 
 
-def feedforward(x, ctx, seg, pooled_grad, weights, hidden, place=None, rows_per_step=4, chunk=768):
+def feedforward(x, ctx, seg, pooled_grad, weights, hidden, place=None, rows_per_step=FF_ROWS, chunk=768):
     row_count, length = seg.shape
     tokens, width = x.shape
     segments = pooled_grad.shape[1]
@@ -481,6 +497,10 @@
     )(place, x, ctx, seg, pooled_grad, *weights)
 
 
+def resident(shape):
+    return pl.BlockSpec(shape, lambda i, *_: (0,) * len(shape), pipeline_mode=pl.Buffered(1))
+
+
 def attention_back_kernel(length, width, first, qkv_ref, grad_ref, seg_ref, *rest):
     out_ref, small_ref = rest[-2:]
     tokens = grad_ref.shape[0]
@@ -491,33 +511,47 @@
         small_ref[...] = rest[1][...] if first else jnp.zeros_like(small_ref)
 
     low_half, high_half = lane_halves()
-    scale = HEAD**-0.5
+    scale = BF16(HEAD**-0.5)
+    masks = []
     for local in range(tokens // length):
-        rows = pl.ds(local * length, length)
         along_lanes, along_rows = segment_grid(seg_ref, step * (tokens // length) + local, length)
         same = along_lanes == along_rows
-        same = jnp.concatenate([same, same], axis=1)
-        for pair in range(width // PAIR):
-            at = (pl.ds(pair * PAIR, PAIR), pl.ds(width + pair * PAIR, PAIR), pl.ds(2 * width + pair * PAIR, PAIR))
-            q = split_heads(qkv_ref[rows, at[0]] * BF16(scale), low_half, high_half)
-            k = qkv_ref[rows, at[1]]
-            v = qkv_ref[rows, at[2]]
-            ctx_grad = split_heads(grad_ref[rows, at[0]], low_half, high_half)
-            scores = jnp.where(same, times_transpose(k, q), -1e30)
-            weights = jnp.exp(scores - jnp.max(scores, axis=0, keepdims=True))
-            weights = weights * (1.0 / jnp.sum(weights, axis=0, keepdims=True))
-            probs_grad = times_transpose(v, ctx_grad)
-            inner = jnp.sum(weights * probs_grad, axis=0, keepdims=True)
-            scores_grad = (weights * (probs_grad - inner)).astype(BF16)
-            values_grad = product(weights.astype(BF16), ctx_grad).astype(BF16)
-            keys_grad = product(scores_grad, q).astype(BF16)
-            turned = jnp.concatenate([scores_grad[:, :length].T, scores_grad[:, length:].T], axis=1)
-            queries_grad = product(turned, split_heads(k * BF16(scale), low_half, high_half)).astype(BF16)
-            out_ref[rows, at[0]] = queries_grad
-            out_ref[rows, at[1]] = keys_grad
-            out_ref[rows, at[2]] = values_grad
-            small_ref[:, at[0]] += fold(queries_grad.astype(F32))
-            small_ref[:, at[1]] += fold(values_grad.astype(F32))
+        masks.append(jnp.concatenate([same, same], axis=1))
+
+    def load(ref, local, part, pair):
+        return ref[pl.ds(local * length, length), pl.ds(part * width + pair * PAIR, PAIR)]
+
+    def split(block):
+        return split_heads(block, low_half, high_half)
+
+    def score(local, pair):
+        q = split(load(qkv_ref, local, 0, pair) * scale)
+        ctx_grad = split(load(grad_ref, local, 0, pair))
+        k, v = load(qkv_ref, local, 1, pair), load(qkv_ref, local, 2, pair)
+        return times_transpose(k, q), times_transpose(v, ctx_grad)
+
+    def weigh(local, pair, products):
+        scores, probs_grad = products
+        scores = jnp.where(masks[local], scores, -1e30)
+        weights = jnp.exp(scores - jnp.max(scores, axis=0, keepdims=True))
+        weights = weights * (1.0 / jnp.sum(weights, axis=0, keepdims=True))
+        inner = jnp.sum(weights * probs_grad, axis=0, keepdims=True)
+        scores_grad = (weights * (probs_grad - inner)).astype(BF16)
+        turned = jnp.concatenate([scores_grad[:, :length].T, scores_grad[:, length:].T], axis=1)
+        return weights.astype(BF16), scores_grad, turned
+
+    def mix(local, pair, found):
+        weights, scores_grad, turned = found
+        values_grad = product(weights, split(load(grad_ref, local, 0, pair))).astype(BF16)
+        keys_grad = product(scores_grad, split(load(qkv_ref, local, 0, pair) * scale)).astype(BF16)
+        queries_grad = product(turned, split(load(qkv_ref, local, 1, pair) * scale)).astype(BF16)
+        rows = pl.ds(local * length, length)
+        for part, grad in enumerate((queries_grad, keys_grad, values_grad)):
+            out_ref[rows, pl.ds(part * width + pair * PAIR, PAIR)] = grad
+        small_ref[:, pl.ds(pair * PAIR, PAIR)] += fold(queries_grad.astype(F32))
+        small_ref[:, pl.ds(width + pair * PAIR, PAIR)] += fold(values_grad.astype(F32))
+
+    interleave([(local, pair) for local in range(tokens // length) for pair in range(width // PAIR)], score, weigh, mix)
 
 
 def attention_backward(qkv, ctx_grad, seg, part=(0, 1), earlier=(), rows_per_step=2):
@@ -733,15 +767,11 @@
     )(place, *arrays)
 
 
-def resident(shape):
-    return pl.BlockSpec(shape, lambda i, *_: (0,) * len(shape), pipeline_mode=pl.Buffered(1))
-
-
 def input_gradient_kernel(first_ref, grad_ref, w_ref, *outs):
     outs[-1][...] = first_ref[...] + times_transpose(grad_ref[...], w_ref[...])
 
 
-def input_gradient(first_grad, qkv_grad, matrix, part=(0, 1, 1), earlier=(), rows=512):
+def input_gradient(first_grad, qkv_grad, matrix, part=(0, 1, 1), earlier=(), rows=256):
     tokens, width = first_grad.shape
     first = tokens // rows * part[0] // part[2]
     steps = tokens // rows * part[1] // part[2] - first
@@ -769,6 +799,7 @@
 
 AXES = ("dp", "fsdp")
 DEVICES = 32
+CORE, X, Y = 1, 2, 16
 
 
 def across(value, mask):
@@ -780,9 +811,6 @@
         return i - i % 16 + (i % 16 + 4 * distance) % 16
 
     return lax.ppermute(value, AXES, [(i, target(i)) for i in range(DEVICES)])
-
-
-CORE, X, Y = 1, 2, 16
 
 
 def together(*values):
@@ -967,20 +995,15 @@
     )
     up_got, down_keep, down_send = together(up_got, down_keep, down_send)
     up = Reduction(up_keep, up_got)
-    *up_first, down_send, ctx_grad = together(*up.first(), down_send, ctx_grad)
-    up_first = up.send_first(up_first)
+    low_u, high_u, down_send, ctx_grad = together(*up.first(), down_send, ctx_grad)
+    up_first = up.send_first((low_u, high_u))
     down_got = across(down_send, CORE)
-    qkv_grad, qv_sums = attention_backward(qkv, ctx_grad, segment_ids, (0, 2))
-    *up_first, down_got, qkv_grad, qv_sums = together(*up_first, down_got, qkv_grad, qv_sums)
+    qkv_grad, qv_sums = attention_backward(qkv, ctx_grad, segment_ids)
+    low_u, high_u, down_got, qkv_grad, qv_sums = together(*up_first, down_got, qkv_grad, qv_sums)
     down = Reduction(down_keep, down_got)
-    *up_second, low_d, high_d, qv_sums = together(*up.second(up_first), *down.first(), qv_sums)
-    up_second = up.send_second(up_second)
+    low_u, high_u, low_d, high_d, qv_sums = together(*up.second((low_u, high_u)), *down.first(), qv_sums)
+    up_second = up.send_second((low_u, high_u))
     down_first = down.send_first((low_d, high_d))
-    qkv_grad, qv_sums = attention_backward(qkv, ctx_grad, segment_ids, (1, 2), (qkv_grad, qv_sums))
-    *up_second, low_d, high_d, qkv_grad, qv_sums = together(*up_second, *down_first, qkv_grad, qv_sums)
-    u1, u2, u3, low_d, high_d, qv_sums = together(*up.third(up_second), *down.second((low_d, high_d)), qv_sums)
-    up_third = up.send_third((u1, u2, u3))
-    down_second = down.send_second((low_d, high_d))
     qkv_keep, qkv_send = weight_gradient(
         qkv_gradient_kernel,
         "qkv_gradient",
@@ -996,39 +1019,41 @@
         6 * tokens * width * width,
         (width, tokens),
     )
-    *up_third, low_d, high_d, qkv_keep, qkv_send = together(*up_third, *down_second, qkv_keep, qkv_send)
+    low_u, high_u, qkv_keep, qkv_send = together(*up_second, qkv_keep, qkv_send)
+    u1, u2, u3, qkv_send, qkv_grad = together(*up.third((low_u, high_u)), qkv_send, qkv_grad)
+    up_third = up.send_third((u1, u2, u3))
+    qkv_got = across(qkv_send, CORE)
+    grad_input = input_gradient(first_grad, qkv_grad, qkv_matrix, (0, 1, 4))
+    low_d, high_d, qkv_got, grad_input = together(*down_first, qkv_got, grad_input)
+    qkv_sum = Reduction(qkv_keep, qkv_got)
+    low_d, high_d, low_q, high_q, grad_input = together(*down.second((low_d, high_d)), *qkv_sum.first(), grad_input)
+    down_second = down.send_second((low_d, high_d))
+    qkv_first = qkv_sum.send_first((low_q, high_q))
+    grad_input = input_gradient(first_grad, qkv_grad, qkv_matrix, (1, 3, 4), (grad_input,))
+    low_d, high_d, low_q, high_q, *up_third, grad_input = together(*down_second, *qkv_first, *up_third, grad_input)
+    d1, d2, d3, low_q, high_q, grad_input = together(
+        *down.third((low_d, high_d)), *qkv_sum.second((low_q, high_q)), grad_input
+    )
+    qkv_second = qkv_sum.send_second((low_q, high_q))
+    down_third = down.send_third((d1, d2, d3))
     up_total = up.finish(up_third)
     up_part, up_small = up_total[: (ratio + 1) * unit], up_total[(ratio + 1) * unit :]
-    up_half, qkv_send, qkv_grad = together(up_part.astype(BF16), qkv_send, qkv_grad)
-    qkv_got = across(qkv_send, CORE)
-    up_theirs = across(up_half, Y)
-    grad_input = input_gradient(first_grad, qkv_grad, qkv_matrix, (0, 1, 4))
-    qkv_got, up_theirs, grad_input = together(qkv_got, up_theirs, grad_input)
+    grad_input = input_gradient(first_grad, qkv_grad, qkv_matrix, (3, 4, 4), (grad_input,))
+    low_q, high_q, grad_input = together(*qkv_second, grad_input)
+    qkv_third = together(*qkv_sum.third((low_q, high_q)), up_part)
+    up_part = qkv_third[-1]
+    qkv_third = qkv_sum.send_third(qkv_third[:-1])
+    up_theirs = across(up_part.astype(BF16), Y)
     up_low, up_high = both_halves(up_part, up_theirs, y)
     grad_up = join_columns((up_low[: ratio * unit], up_high[: ratio * unit]), unit, ratio)
     grad_out = join_columns((up_low[ratio * unit :], up_high[ratio * unit :]), unit, 1)
-    qkv_sum = Reduction(qkv_keep, qkv_got)
-    low_q, high_q, d1, d2, d3, grad_up, grad_out, grad_input = together(
-        *qkv_sum.first(), *down.third((low_d, high_d)), grad_up, grad_out, grad_input
-    )
-    qkv_first = qkv_sum.send_first((low_q, high_q))
-    down_third = down.send_third((d1, d2, d3))
-    grad_input = input_gradient(first_grad, qkv_grad, qkv_matrix, (1, 3, 4), (grad_input,))
-    *qkv_first, grad_input = together(*qkv_first, grad_input)
-    *qkv_second, grad_input = together(*qkv_sum.second(qkv_first), grad_input)
-    qkv_second = qkv_sum.send_second(qkv_second)
-    grad_input = input_gradient(first_grad, qkv_grad, qkv_matrix, (3, 4, 4), (grad_input,))
-    low_q, high_q, *down_third, grad_input = together(*qkv_second, *down_third, grad_input)
-    qkv_second = low_q, high_q
-    qkv_third = together(*qkv_sum.third(qkv_second))
     down_total = down.finish(down_third)
-    qkv_third = qkv_sum.send_third(qkv_third)
-    down_theirs = across(down_total.astype(BF16), Y)
-    grad_down = jnp.concatenate(both_halves(down_total, down_theirs, y), axis=1)
-    *qkv_third, grad_down = together(*qkv_third, grad_down)
+    *qkv_third, down_total, grad_up, grad_out = together(*qkv_third, down_total, grad_up, grad_out)
     qkv_total = qkv_sum.finish(qkv_third)
     qkv_part, qkv_small = qkv_total[: 3 * unit], qkv_total[3 * unit :]
-    qkv_theirs = across(qkv_part.astype(BF16), Y)
+    theirs = across(jnp.concatenate([qkv_part, down_total], axis=0).astype(BF16), Y)
+    qkv_theirs, down_theirs = theirs[: 3 * unit], theirs[3 * unit :]
+    grad_down = jnp.concatenate(both_halves(down_total, down_theirs, y), axis=1)
     grad_qkv = join_columns(both_halves(qkv_part, qkv_theirs, y), unit, 3)
     return (
         pooled,

time: 371 us -> 351 us (0.946); the launches traced: 364 us -> 350 us
  Pallas kernels: 207 us -> 194 us
  waiting for transfers between devices: 64.9 us -> 68.7 us
    pallas_call x2 -> x1, Pallas kernels: 32.5 us -> 17.5 us  [attention_backward(): pl.pallas_call(functools.partial(attention_back_kernel, length, width, fi...]
    ppermute x41 -> x40, waiting for transfers between devices: 37.8 us -> 42.5 us  [across(): return lax.ppermute(value, AXES, [(i, i ^ mask) for i in range(DEVICES)])]
    pallas_call x1, Pallas kernels: 68.7 us -> 72.8 us  [feedforward(): pl.pallas_call(functools.partial(feedforward_gathered_kernel, length, chu...]
    ppermute x41 -> x40, starting transfers between devices: 27.5 us -> 28.4 us  [across(): return lax.ppermute(value, AXES, [(i, i ^ mask) for i in range(DEVICES)])]
  transfers between devices with their start and end apart: 56 -> 55, of which waited for: 19 -> 18; matrix products, arithmetic and copies ran while one was open for 4% -> 5% of each run, Pallas kernels for 31% -> 27%
where the time goes in v4:
time: 351 us; the launch traced here: 350 us
  Pallas kernels  194 us (55%)
  waiting for transfers between devices  68.7 us (20%)
  starting transfers between devices  47.5 us (14%)
  other arithmetic  26.9 us (8%)
  local copies, waits for them, and re-layouts  11.9 us (3%)
    pallas_call x1, Pallas kernels, feedforward(): pl.pallas_call(functools.partial(feedforward_gathered_kernel, length, chu...  72.8 us
    pallas_call x3, Pallas kernels, weight_gradient(): pl.pallas_call(kernel, grid_spec=spec, out_shape=[jax.ShapeDtypeStruct(sh...  54.4 us
    ppermute x40, waiting for transfers between devices, across(): return lax.ppermute(value, AXES, [(i, i ^ mask) for i in range(DEVICES)])  42.5 us
    ppermute x40, starting transfers between devices, across(): return lax.ppermute(value, AXES, [(i, i ^ mask) for i in range(DEVICES)])  28.4 us
    ppermute x15, waiting for transfers between devices, along_z(): return lax.ppermute(value, AXES, [(i, target(i)) for i in range(DEVICES)])  26.2 us
    pallas_call x3, Pallas kernels, input_gradient(): pl.pallas_call(input_gradient_kernel, grid=(steps,), in_specs=[pl.BlockSp...  20.4 us
    ppermute x15, starting transfers between devices, along_z(): return lax.ppermute(value, AXES, [(i, target(i)) for i in range(DEVICES)])  19.1 us
    pallas_call x1, Pallas kernels, attention_backward(): pl.pallas_call(functools.partial(attention_back_kernel, length, width, fi...  17.5 us
  transfers between devices with their start and end apart: 55, of which 18 were waited for; matrix products, arithmetic and copies ran while one was open for 5% of the time, Pallas kernels for 27%

profile of v4, /device:TPU:0, one launch (start us, length us, event | category | flops | bytes accessed | tf_op | source)
XLA Modules:
  0.0 349.8 jit_solution(12323937637442531930)
XLA Ops:
  2.5 2.3 pack_attention.1
  4.8 5.0 %collective-permute-start.2 = (bf16[160,384]{1,0:T(8,128)(2,1)}, bf16[160,384]{1,0:T(8,128)(2,1)S(1)}, u32[]{:S(2)}, u32[]{:S(2)}) collective-permute-start(bf16[160,384]{1,0:T(8,128)(2,1)} %pack_attention.1), channel_id=1, source_target_pairs={{0,12},{1,13},{2,14},{3,15},{4,0},{5,1},{6,2},{7,3},{8,4},{9,5},{1... | collective-permute-start | bytes 368648 | tf_op jit(solution)/shard_map/ppermute | solution.py:813
  16.8 2.5 pack_feedforward.1
  19.3 1.4 collective-permute-done.1
  21.6 1.6 collective-permute-start.4
  23.2 1.5 collective-permute-start.3
  25.9 9.6 %collective-permute-done.5 = bf16[448,384]{1,0:T(8,128)(2,1)S(1)} collective-permute-done((bf16[448,384]{1,0:T(8,128)(2,1)}, bf16[448,384]{1,0:T(8,128)(2,1)S(1)}, u32[]{:S(2)}, u32[]{:S(2)}) %collective-permute-start.5) | collective-permute-done | bytes 344096 | tf_op jit(solution)/shard_map/ppermute | solution.py:813
  35.6 1.5 collective-permute-start.7
  39.1 2.7 collective-permute-done.7.rest_4_
  41.8 1.4 collective-permute-done.6.rest_3_
  43.3 1.4 collective-permute-start.8
  46.6 4.0 %collective-permute-done.8 = bf16[448,384]{1,0:T(8,128)(2,1)S(1)} collective-permute-done((bf16[448,384]{1,0:T(8,128)(2,1)S(1)}, bf16[448,384]{1,0:T(8,128)(2,1)S(1)}, u32[]{:S(2)}, u32[]{:S(2)}) %collective-permute-start.8) | collective-permute-done | bytes 344096 | tf_op jit(solution)/shard_map/ppermute | solution.py:813
  51.6 2.6 collective-permute-start.16
  54.2 13.2 %attention_forward.2 = (bf16[2048,2304]{1,0:T(8,128)(2,1)}, bf16[2048,768]{1,0:T(8,128)(2,1)}, bf16[768,2304]{1,0:T(8,128)(2,1)}, f32[8,2304]{1,0:T(8,128)}) custom-call(s32[4]{0:T(128)} %pad_add_fusion.place_ref, bf16[2048,768]{1,0:T(8,128)(2,1)} %bitcast.145, s32[16,128]{1,0:T(8,128)} %seg_ref.7, bf16[4,160,384]{2,1,0:T(8,128)(2,1)} %copy-done.7, ...), custom_call_target="tpu_custom_call" | custom-call | flops 4429185024 | bytes 11403264 | tf_op jit(solution)/shard_map/attention_forward/pallas_call | solution.py:249
  67.6 1.9 collective-permute-start.18
  69.5 2.0 collective-permute-start.17
  72.1 10.4 %attention_forward.3 = (bf16[2048,2304]{1,0:T(8,128)(2,1)}, bf16[2048,768]{1,0:T(8,128)(2,1)}) custom-call(bf16[2048,768]{1,0:T(8,128)(2,1)} %bitcast.146, s32[16,128]{1,0:T(8,128)} %seg_ref.7, bf16[768,2304]{1,0:T(8,128)(2,1)} %get-tuple-element.187.w_ref, f32[8,2304]{1,0:T(8,128)} %get-tuple-element.188.bias_ref, ...), custom_call_target="tpu_custom_call", output_to_operand_aliasing={{0}: (4, {}), {1}: (5, {})} | custom-call | flops 4429185024 | bytes 11403264 | tf_op jit(solution)/shard_map/attention_forward/pallas_call | solution.py:226
  85.2 15.2 %collective-permute-done.19.rest_6_ = bf16[2,448,384]{2,1,0:T(8,128)(2,1)S(1)} collective-permute-done((bf16[2,448,384]{2,1,0:T(8,128)(2,1)S(1)}, bf16[2,448,384]{2,1,0:T(8,128)(2,1)S(1)}, u32[]{:S(2)}, u32[]{:S(2)}) %collective-permute-start.19) | collective-permute-done | bytes 688160 | tf_op jit(solution)/shard_map/ppermute | solution.py:806
  103.8 72.8 %feedforward.1 = (f32[16,4,768]{2,1,0:T(4,128)}, bf16[2048,3072]{1,0:T(8,128)(2,1)}, bf16[2048,3072]{1,0:T(8,128)(2,1)}, bf16[2048,768]{1,0:T(8,128)(2,1)}, bf16...) custom-call(s32[4]{0:T(128)} %pad_add_fusion.place_ref, ...), custom_call_target="tpu_custom_call" | custom-call | flops 43486543872 | bytes 62914560 | tf_op jit(solution)/shard_map/feedforward/pallas_call | solution.py:492
  176.6 23.0 %up_gradient.1 = (bf16[2,2,4,256,384]{4,3,2,1,0:T(8,128)(2,1)}, bf16[2,2,4,256,384]{4,3,2,1,0:T(8,128)(2,1)}) custom-call(s32[4]{0:T(128)} %pad_add_fusion.place_ref, bf16[2048,768]{1,0:T(8,128)(2,1)} %get-tuple-element.199.normed_ref, bf16[2048,3072]{1,0:T(8,128)(2,1)} %get-tuple-element.200.hidden_ref, bf16[2048,768]{1,0:T(8,128)(2,1)} %get-tuple-element.193.ctx_ref, ...), custom_call_target="tpu_custom_call" | custom-call | flops 12079595520 | bytes 22142976 | tf_op jit(solution)/shard_map/up_gradient/pallas_call | solution.py:758
  199.7 16.7 %down_gradient.1 = (bf16[2,2,4,192,384]{4,3,2,1,0:T(8,128)(2,1)}, bf16[2,2,4,192,384]{4,3,2,1,0:T(8,128)(2,1)}) custom-call(s32[4]{0:T(128)} %pad_add_fusion.place_ref, bf16[2048,3072]{1,0:T(8,128)(2,1)} %get-tuple-element.208.active_ref, bf16[2048,768]{1,0:T(8,128)(2,1)} %get-tuple-element.209.branch_ref), custom_call_target="tpu_custom_call" | custom-call | flops 9663676416 | bytes 15728640 | tf_op jit(solution)/shard_map/down_gradient/pallas_call | solution.py:758
  216.4 2.3 fusion.1
  218.7 2.2 fusion
  222.3 17.5 %attention_backward.1 = (bf16[2048,2304]{1,0:T(8,128)(2,1)}, f32[8,1536]{1,0:T(8,128)}) custom-call(bf16[2048,2304]{1,0:T(8,128)(2,1)} %get-tuple-element.220.qkv_ref, bf16[2048,768]{1,0:T(8,128)(2,1)} %get-tuple-element.221.grad_ref, s32[16,128]{1,0:T(8,128)} %seg_ref.7), custom_call_target="tpu_custom_call" | custom-call | flops 4026531840 | bytes 22020096 | tf_op jit(solution)/shard_map/attention_backward/pallas_call | solution.py:564
  239.8 1.3 collective-permute-done.30
  241.2 2.0 fusion.8
  243.2 2.0 fusion.7
  245.2 1.7 fusion.5
  247.7 1.7 collective-permute-start.36
  249.4 14.7 %qkv_gradient.1 = (bf16[2,2,4,160,384]{4,3,2,1,0:T(8,128)(2,1)}, bf16[2,2,4,160,384]{4,3,2,1,0:T(8,128)(2,1)}) custom-call(s32[4]{0:T(128)} %pad_add_fusion.place_ref, bf16[2048,768]{1,0:T(8,128)(2,1)} %bitcast.148, bf16[2048,2304]{1,0:T(8,128)(2,1)} %get-tuple-element.241.grad_ref, f32[8,1536]{1,0:T(8,128)} %get-tuple-element.233.sums_ref), custom_call_target="tpu_custom_call" | custom-call | flops 7247757312 | bytes 12607488 | tf_op jit(solution)/shard_map/qkv_gradient/pallas_call | solution.py:758
  264.2 1.7 fusion.3
  268.3 1.9 collective-permute-start.43
  270.2 5.9 %input_gradient.3.outs_0_ = f32[2048,768]{1,0:T(8,128)} custom-call(f32[2048,768]{1,0:T(8,128)} %get-tuple-element.240.first_ref, bf16[2048,2304]{1,0:T(8,128)(2,1)} %get-tuple-element.241.grad_ref, bf16[768,2304]{1,0:T(8,128)(2,1)} %get-tuple-element.187.w_ref), custom_call_target="tpu_custom_call" | custom-call | flops 1811939328 | bytes 5505024 | tf_op jit(solution)/shard_map/input_gradient/pallas_call | solution.py:778
  276.1 6.6 %collective-permute-done.33 = bf16[2,2,192,384]{3,2,1,0:T(8,128)(2,1)S(1)} collective-permute-done((bf16[2,2,192,384]{3,2,1,0:T(8,128)(2,1)}, bf16[2,2,192,384]{3,2,1,0:T(8,128)(2,1)S(1)}, u32[]{:S(2)}, u32[]{:S(2)}) %collective-permute-start.33) | collective-permute-done | bytes 589856 | tf_op jit(solution)/shard_map/ppermute | solution.py:806
  283.8 2.2 fusion.11
  287.2 1.8 collective-permute-start.40
  291.8 8.8 %input_gradient.4.outs_0_ = f32[2048,768]{1,0:T(8,128)} custom-call(f32[2048,768]{1,0:T(8,128)} %get-tuple-element.240.first_ref, bf16[2048,2304]{1,0:T(8,128)(2,1)} %get-tuple-element.241.grad_ref, bf16[768,2304]{1,0:T(8,128)(2,1)} %get-tuple-element.187.w_ref, f32[2048,768]{1,0:T(8,128)} %input_gradient.3.outs_0_), custom_call_target="tpu_custom_call", output_to_operand_aliasing={{}: (3, {})} | custom-call | flops 3623878656 | bytes 11010048 | tf_op jit(solution)/shard_map/input_gradient/pallas_call | solution.py:778
  300.6 7.0 %collective-permute-done.38 = bf16[2,192,384]{2,1,0:T(8,128)(2,1)S(1)} collective-permute-done((bf16[2,192,384]{2,1,0:T(8,128)(2,1)}, bf16[2,192,384]{2,1,0:T(8,128)(2,1)S(1)}, u32[]{:S(2)}, u32[]{:S(2)}) %collective-permute-start.38) | collective-permute-done | bytes 294944 | tf_op jit(solution)/shard_map/ppermute | solution.py:806
  307.7 1.6 fusion.10
  310.0 1.5 fusion.19
  311.5 1.3 collective-permute-start.45
  314.7 1.6 collective-permute-start.51
  316.8 5.7 %input_gradient.5 = f32[2048,768]{1,0:T(8,128)} custom-call(f32[2048,768]{1,0:T(8,128)} %get-tuple-element.240.first_ref, bf16[2048,2304]{1,0:T(8,128)(2,1)} %get-tuple-element.241.grad_ref, bf16[768,2304]{1,0:T(8,128)(2,1)} %get-tuple-element.187.w_ref, f32[2048,768]{1,0:T(8,128)} %input_gradient.4.outs_0_), custom_call_target="tpu_custom_call", output_to_operand_aliasing={{}: (3, {})} | custom-call | flops 1811939328 | bytes 5505024 | tf_op jit(solution)/shard_map/input_gradient/pallas_call | solution.py:778
  322.5 1.5 fusion.17
  325.0 2.8 collective-permute-done.51
  329.5 1.9 collective-permute-start.49
  333.2 7.6 %collective-permute-done.48 = bf16[160,384]{1,0:T(8,128)(2,1)S(1)} collective-permute-done((bf16[160,384]{1,0:T(8,128)(2,1)S(1)}, bf16[160,384]{1,0:T(8,128)(2,1)S(1)}, u32[]{:S(2)}, u32[]{:S(2)}) %collective-permute-start.48) | collective-permute-done | bytes 122912 | tf_op jit(solution)/shard_map/ppermute | solution.py:813
  343.5 5.2 %collective-permute-done.54 = bf16[336,384]{1,0:T(8,128)(2,1)S(1)} collective-permute-done((bf16[336,384]{1,0:T(8,128)(2,1)S(1)}, bf16[336,384]{1,0:T(8,128)(2,1)S(1)}, u32[]{:S(2)}, u32[]{:S(2)}) %collective-permute-start.54) | collective-permute-done | bytes 258080 | tf_op jit(solution)/shard_map/ppermute | solution.py:806
  (205 shorter events, 43.5 us)
Async XLA Ops:
  4.8 14.5 %collective-permute-start.2 = (bf16[160,384]{1,0:T(8,128)(2,1)}, bf16[160,384]{1,0:T(8,128)(2,1)S(1)}, u32[]{:S(2)}, u32[]{:S(2)}) collective-permute-start(bf16[160,384]{1,0:T(8,128)(2,1)} %pack_attention.1), channel_id=1, source_target_pairs={{0,12},{1,13},{2,14},{3,15},{4,0},{5,1},{6,2},{7,3},{8,4},{9,5},{1... | collective-permute-start | bytes 368648 | tf_op jit(solution)/shard_map/ppermute | solution.py:813
  9.8 10.8 %collective-permute-start.1 = (bf16[160,384]{1,0:T(8,128)(2,1)}, bf16[160,384]{1,0:T(8,128)(2,1)S(1)}, u32[]{:S(2)}, u32[]{:S(2)}) collective-permute-start(bf16[160,384]{1,0:T(8,128)(2,1)} %pack_attention.1), channel_id=1, source_target_pairs={{0,8},{1,9},{2,10},{3,11},{4,12},{5,13},{6,14},{7,15},{8,0},{9,1},... | collective-permute-start | bytes 368648 | tf_op jit(solution)/shard_map/ppermute | solution.py:813
  9.8 10.8 %collective-permute-start = (bf16[160,384]{1,0:T(8,128)(2,1)}, bf16[160,384]{1,0:T(8,128)(2,1)S(1)}, u32[]{:S(2)}, u32[]{:S(2)}) collective-permute-start(bf16[160,384]{1,0:T(8,128)(2,1)} %pack_attention.1), channel_id=1, source_target_pairs={{0,4},{1,5},{2,6},{3,7},{4,8},{5,9},{6,10},{7,11},{8,12},{9,13},{1... | collective-permute-start | bytes 368648 | tf_op jit(solution)/shard_map/ppermute | solution.py:813
  21.6 13.8 %collective-permute-start.4 = (bf16[4,160,384]{2,1,0:T(8,128)(2,1)S(1)}, bf16[4,160,384]{2,1,0:T(8,128)(2,1)S(1)}, u32[]{:S(2)}, u32[]{:S(2)}) collective-permute-start(bf16[4,160,384]{2,1,0:T(8,128)(2,1)S(1)} %pad_maximum_fusion.3.rest_0_), channel_id=1, source_target_pairs={{0,16},{1,17},{2,18},{3,19},{4,20},{5,21},{6,22},{7,23},{8,24},{9,... | collective-permute-start | bytes 1474568 | tf_op jit(solution)/shard_map/ppermute | solution.py:806
  23.2 12.3 %collective-permute-start.3 = (bf16[4,160,384]{2,1,0:T(8,128)(2,1)S(1)}, bf16[4,160,384]{2,1,0:T(8,128)(2,1)S(1)}, u32[]{:S(2)}, u32[]{:S(2)}) collective-permute-start(bf16[4,160,384]{2,1,0:T(8,128)(2,1)S(1)} %pad_maximum_fusion.3.rest_0_), channel_id=1, source_target_pairs={{0,2},{1,3},{2,0},{3,1},{4,6},{5,7},{6,4},{7,5},{8,10},{9,11},{10,... | collective-permute-start | bytes 1474568 | tf_op jit(solution)/shard_map/ppermute | solution.py:806
  24.7 10.8 %collective-permute-start.5 = (bf16[448,384]{1,0:T(8,128)(2,1)}, bf16[448,384]{1,0:T(8,128)(2,1)S(1)}, u32[]{:S(2)}, u32[]{:S(2)}) collective-permute-start(bf16[448,384]{1,0:T(8,128)(2,1)} %pack_feedforward.1), channel_id=1, source_target_pairs={{0,4},{1,5},{2,6},{3,7},{4,8},{5,9},{6,10},{7,11},{8,12},{9,13},{1... | collective-permute-start | bytes 1032200 | tf_op jit(solution)/shard_map/ppermute | solution.py:813
  25.9 18.8 %collective-permute-start.9 = (bf16[4,160,384]{2,1,0:T(8,128)(2,1)S(1)}, bf16[4,160,384]{2,1,0:T(8,128)(2,1)S(1)}, u32[]{:S(2)}, u32[]{:S(2)}) collective-permute-start(bf16[4,160,384]{2,1,0:T(8,128)(2,1)S(1)} %pad_maximum_fusion.3.rest_0_), channel_id=1, source_target_pairs={{0,1},{1,0},{2,3},{3,2},{4,5},{5,4},{6,7},{7,6},{8,9},{9,8},{10,11... | collective-permute-start | bytes 1474568 | tf_op jit(solution)/shard_map/ppermute | solution.py:806
  37.6 7.6 %collective-permute-start.10 = (bf16[4,160,384]{2,1,0:T(8,128)(2,1)S(1)}, bf16[4,160,384]{2,1,0:T(8,128)(2,1)S(1)}, u32[]{:S(2)}, u32[]{:S(2)}) collective-permute-start(bf16[4,160,384]{2,1,0:T(8,128)(2,1)S(1)} %collective-permute-done.3.rest_1_), channel_id=1, source_target_pairs={{0,1},{1,0},{2,3},{3,2},{4,5},{5,4},{6,7},{7,6},{8,9},{9,8},{10,11... | collective-permute-start | bytes 1474568 | tf_op jit(solution)/shard_map/ppermute | solution.py:806
  37.6 7.6 %collective-permute-start.11 = (bf16[4,160,384]{2,1,0:T(8,128)(2,1)S(1)}, bf16[4,160,384]{2,1,0:T(8,128)(2,1)S(1)}, u32[]{:S(2)}, u32[]{:S(2)}) collective-permute-start(bf16[4,160,384]{2,1,0:T(8,128)(2,1)S(1)} %collective-permute-done.4.rest_2_), channel_id=1, source_target_pairs={{0,1},{1,0},{2,3},{3,2},{4,5},{5,4},{6,7},{7,6},{8,9},{9,8},{10,11... | collective-permute-start | bytes 1474568 | tf_op jit(solution)/shard_map/ppermute | solution.py:806
  43.3 7.3 %collective-permute-start.8 = (bf16[448,384]{1,0:T(8,128)(2,1)S(1)}, bf16[448,384]{1,0:T(8,128)(2,1)S(1)}, u32[]{:S(2)}, u32[]{:S(2)}) collective-permute-start(bf16[448,384]{1,0:T(8,128)(2,1)S(1)} %copy-done.4), channel_id=1, source_target_pairs={{0,12},{1,13},{2,14},{3,15},{4,0},{5,1},{6,2},{7,3},{8,4},{9,5},{1... | collective-permute-start | bytes 1032200 | tf_op jit(solution)/shard_map/ppermute | solution.py:813
  50.5 16.9 %collective-permute-start.15 = (bf16[2,448,384]{2,1,0:T(8,128)(2,1)S(1)}, bf16[2,448,384]{2,1,0:T(8,128)(2,1)S(1)}, u32[]{:S(2)}, u32[]{:S(2)}) collective-permute-start(bf16[2,448,384]{2,1,0:T(8,128)(2,1)S(1)} %pad_maximum_fusion.rest_0_), channel_id=1, source_target_pairs={{0,16},{1,17},{2,18},{3,19},{4,20},{5,21},{6,22},{7,23},{8,24},{9,... | collective-permute-start | bytes 2064392 | tf_op jit(solution)/shard_map/ppermute | solution.py:806
  51.0 16.4 %collective-permute-start.14 = (bf16[2,448,384]{2,1,0:T(8,128)(2,1)S(1)}, bf16[2,448,384]{2,1,0:T(8,128)(2,1)S(1)}, u32[]{:S(2)}, u32[]{:S(2)}) collective-permute-start(bf16[2,448,384]{2,1,0:T(8,128)(2,1)S(1)} %pad_maximum_fusion.rest_0_), channel_id=1, source_target_pairs={{0,2},{1,3},{2,0},{3,1},{4,6},{5,7},{6,4},{7,5},{8,10},{9,11},{10,... | collective-permute-start | bytes 2064392 | tf_op jit(solution)/shard_map/ppermute | solution.py:806
  51.6 15.8 %collective-permute-start.16 = (bf16[448,384]{1,0:T(8,128)(2,1)S(1)}, bf16[448,384]{1,0:T(8,128)(2,1)S(1)}, u32[]{:S(2)}, u32[]{:S(2)}) collective-permute-start(bf16[448,384]{1,0:T(8,128)(2,1)S(1)} %copy-done.4), channel_id=1, source_target_pairs={{0,8},{1,9},{2,10},{3,11},{4,12},{5,13},{6,14},{7,15},{8,0},{9,1},... | collective-permute-start | bytes 1032200 | tf_op jit(solution)/shard_map/ppermute | solution.py:813
  67.6 14.9 %collective-permute-start.18 = (bf16[2,448,384]{2,1,0:T(8,128)(2,1)S(1)}, bf16[2,448,384]{2,1,0:T(8,128)(2,1)S(1)}, u32[]{:S(2)}, u32[]{:S(2)}) collective-permute-start(bf16[2,448,384]{2,1,0:T(8,128)(2,1)S(1)} %pad_maximum_fusion.1.rest_1_), channel_id=1, source_target_pairs={{0,16},{1,17},{2,18},{3,19},{4,20},{5,21},{6,22},{7,23},{8,24},{9,... | collective-permute-start | bytes 2064392 | tf_op jit(solution)/shard_map/ppermute | solution.py:806
  69.5 13.9 %collective-permute-start.17 = (bf16[2,448,384]{2,1,0:T(8,128)(2,1)S(1)}, bf16[2,448,384]{2,1,0:T(8,128)(2,1)S(1)}, u32[]{:S(2)}, u32[]{:S(2)}) collective-permute-start(bf16[2,448,384]{2,1,0:T(8,128)(2,1)S(1)} %pad_maximum_fusion.1.rest_1_), channel_id=1, source_target_pairs={{0,2},{1,3},{2,0},{3,1},{4,6},{5,7},{6,4},{7,5},{8,10},{9,11},{10,... | collective-permute-start | bytes 2064392 | tf_op jit(solution)/shard_map/ppermute | solution.py:806
  71.6 13.0 %collective-permute-start.21 = (bf16[2,448,384]{2,1,0:T(8,128)(2,1)S(1)}, bf16[2,448,384]{2,1,0:T(8,128)(2,1)S(1)}, u32[]{:S(2)}, u32[]{:S(2)}) collective-permute-start(bf16[2,448,384]{2,1,0:T(8,128)(2,1)S(1)} %pad_maximum_fusion.rest_0_), channel_id=1, source_target_pairs={{0,1},{1,0},{2,3},{3,2},{4,5},{5,4},{6,7},{7,6},{8,9},{9,8},{10,11... | collective-permute-start | bytes 2064392 | tf_op jit(solution)/shard_map/ppermute | solution.py:806
  71.6 13.1 %collective-permute-start.22 = (bf16[2,448,384]{2,1,0:T(8,128)(2,1)S(1)}, bf16[2,448,384]{2,1,0:T(8,128)(2,1)}, u32[]{:S(2)}, u32[]{:S(2)}) collective-permute-start(bf16[2,448,384]{2,1,0:T(8,128)(2,1)S(1)} %pad_maximum_fusion.1.rest_1_), channel_id=1, source_target_pairs={{0,1},{1,0},{2,3},{3,2},{4,5},{5,4},{6,7},{7,6},{8,9},{9,8},{10,11... | collective-permute-start | bytes 2064392 | tf_op jit(solution)/shard_map/ppermute | solution.py:806
  72.1 13.1 %collective-permute-start.25 = (bf16[2,448,384]{2,1,0:T(8,128)(2,1)S(1)}, bf16[2,448,384]{2,1,0:T(8,128)(2,1)}, u32[]{:S(2)}, u32[]{:S(2)}) collective-permute-start(bf16[2,448,384]{2,1,0:T(8,128)(2,1)S(1)} %collective-permute-done.15.rest_4_), channel_id=1, source_target_pairs={{0,1},{1,0},{2,3},{3,2},{4,5},{5,4},{6,7},{7,6},{8,9},{9,8},{10,11... | collective-permute-start | bytes 2064392 | tf_op jit(solution)/shard_map/ppermute | solution.py:806
  82.5 17.9 %collective-permute-start.19 = (bf16[2,448,384]{2,1,0:T(8,128)(2,1)S(1)}, bf16[2,448,384]{2,1,0:T(8,128)(2,1)S(1)}, u32[]{:S(2)}, u32[]{:S(2)}) collective-permute-start(bf16[2,448,384]{2,1,0:T(8,128)(2,1)S(1)} %collective-permute-done.14.rest_2_), channel_id=1, source_target_pairs={{0,16},{1,17},{2,18},{3,19},{4,20},{5,21},{6,22},{7,23},{8,24},{9,... | collective-permute-start | bytes 2064392 | tf_op jit(solution)/shard_map/ppermute | solution.py:806
  83.5 17.1 %collective-permute-start.20 = (bf16[2,448,384]{2,1,0:T(8,128)(2,1)S(1)}, bf16[2,448,384]{2,1,0:T(8,128)(2,1)S(1)}, u32[]{:S(2)}, u32[]{:S(2)}) collective-permute-start(bf16[2,448,384]{2,1,0:T(8,128)(2,1)S(1)} %collective-permute-done.18.rest_5_), channel_id=1, source_target_pairs={{0,2},{1,3},{2,0},{3,1},{4,6},{5,7},{6,4},{7,5},{8,10},{9,11},{10,... | collective-permute-start | bytes 2064392 | tf_op jit(solution)/shard_map/ppermute | solution.py:806
  84.6 16.4 %collective-permute-start.23 = (bf16[2,448,384]{2,1,0:T(8,128)(2,1)S(1)}, bf16[2,448,384]{2,1,0:T(8,128)(2,1)S(1)}, u32[]{:S(2)}, u32[]{:S(2)}) collective-permute-start(bf16[2,448,384]{2,1,0:T(8,128)(2,1)S(1)} %collective-permute-done.14.rest_2_), channel_id=1, source_target_pairs={{0,1},{1,0},{2,3},{3,2},{4,5},{5,4},{6,7},{7,6},{8,9},{9,8},{10,11... | collective-permute-start | bytes 2064392 | tf_op jit(solution)/shard_map/ppermute | solution.py:806
  84.7 16.3 %collective-permute-start.26 = (bf16[2,448,384]{2,1,0:T(8,128)(2,1)S(1)}, bf16[2,448,384]{2,1,0:T(8,128)(2,1)S(1)}, u32[]{:S(2)}, u32[]{:S(2)}) collective-permute-start(bf16[2,448,384]{2,1,0:T(8,128)(2,1)S(1)} %collective-permute-done.18.rest_5_), channel_id=1, source_target_pairs={{0,1},{1,0},{2,3},{3,2},{4,5},{5,4},{6,7},{7,6},{8,9},{9,8},{10,11... | collective-permute-start | bytes 2064392 | tf_op jit(solution)/shard_map/ppermute | solution.py:806
  85.2 15.8 %collective-permute-start.24 = (bf16[2,448,384]{2,1,0:T(8,128)(2,1)S(1)}, bf16[2,448,384]{2,1,0:T(8,128)(2,1)S(1)}, u32[]{:S(2)}, u32[]{:S(2)}) collective-permute-start(bf16[2,448,384]{2,1,0:T(8,128)(2,1)S(1)} %collective-permute-done.17.rest_3_), channel_id=1, source_target_pairs={{0,1},{1,0},{2,3},{3,2},{4,5},{5,4},{6,7},{7,6},{8,9},{9,8},{10,11... | collective-permute-start | bytes 2064392 | tf_op jit(solution)/shard_map/ppermute | solution.py:806
  199.6 16.9 %collective-permute-start.29 = (bf16[2,2,4,256,384]{4,3,2,1,0:T(8,128)(2,1)}, bf16[2,2,4,256,384]{4,3,2,1,0:T(8,128)(2,1)}, u32[]{:S(2)}, u32[]{:S(2)}) collective-permute-start(bf16[2,2,4,256,384]{4,3,2,1,0:T(8,128)(2,1)} %get-tuple-element.207), channel_id=1, source_target_pairs={{0,1},{1,0},{2,3},{3,2},{4,5},{5,4},{6,7},{7,6},{8,9},{9,8},{10,11... | collective-permute-start | bytes 9437192 | tf_op jit(solution)/shard_map/ppermute | solution.py:806
  220.9 20.3 %collective-permute-start.32 = (bf16[2,2,4,192,384]{4,3,2,1,0:T(8,128)(2,1)}, bf16[2,2,4,192,384]{4,3,2,1,0:T(8,128)(2,1)}, u32[]{:S(2)}, u32[]{:S(2)}) collective-permute-start(bf16[2,2,4,192,384]{4,3,2,1,0:T(8,128)(2,1)} %get-tuple-element.219), channel_id=1, source_target_pairs={{0,1},{1,0},{2,3},{3,2},{4,5},{5,4},{6,7},{7,6},{8,9},{9,8},{10,11... | collective-permute-start | bytes 7077896 | tf_op jit(solution)/shard_map/ppermute | solution.py:806
  221.3 19.9 %collective-permute-start.30 = (bf16[2,2,256,384]{3,2,1,0:T(8,128)(2,1)}, bf16[2,2,256,384]{3,2,1,0:T(8,128)(2,1)}, u32[]{:S(2)}, u32[]{:S(2)}) collective-permute-start(bf16[2,2,256,384]{3,2,1,0:T(8,128)(2,1)} %fusion), channel_id=1, source_target_pairs={{0,2},{1,3},{2,0},{3,1},{4,6},{5,7},{6,4},{7,5},{8,10},{9,11},{10,... | collective-permute-start | bytes 2359304 | tf_op jit(solution)/shard_map/ppermute | solution.py:806
  221.3 19.9 %collective-permute-start.31 = (bf16[2,2,256,384]{3,2,1,0:T(8,128)(2,1)}, bf16[2,2,256,384]{3,2,1,0:T(8,128)(2,1)}, u32[]{:S(2)}, u32[]{:S(2)}) collective-permute-start(bf16[2,2,256,384]{3,2,1,0:T(8,128)(2,1)} %fusion.1), channel_id=1, source_target_pairs={{0,16},{1,17},{2,18},{3,19},{4,20},{5,21},{6,22},{7,23},{8,24},{9,... | collective-permute-start | bytes 2359304 | tf_op jit(solution)/shard_map/ppermute | solution.py:806
  246.9 17.3 %collective-permute-start.35 = (bf16[2,256,384]{2,1,0:T(8,128)(2,1)S(1)}, bf16[2,256,384]{2,1,0:T(8,128)(2,1)S(1)}, u32[]{:S(2)}, u32[]{:S(2)}) collective-permute-start(bf16[2,256,384]{2,1,0:T(8,128)(2,1)S(1)} %get-tuple-element.230), channel_id=1, source_target_pairs={{0,16},{1,17},{2,18},{3,19},{4,20},{5,21},{6,22},{7,23},{8,24},{9,... | collective-permute-start | bytes 1179656 | tf_op jit(solution)/shard_map/ppermute | solution.py:806
  247.7 16.4 %collective-permute-start.36 = (bf16[2,256,384]{2,1,0:T(8,128)(2,1)S(1)}, bf16[2,256,384]{2,1,0:T(8,128)(2,1)S(1)}, u32[]{:S(2)}, u32[]{:S(2)}) collective-permute-start(bf16[2,256,384]{2,1,0:T(8,128)(2,1)S(1)} %get-tuple-element.231), channel_id=1, source_target_pairs={{0,2},{1,3},{2,0},{3,1},{4,6},{5,7},{6,4},{7,5},{8,10},{9,11},{10,... | collective-permute-start | bytes 1179656 | tf_op jit(solution)/shard_map/ppermute | solution.py:806
  266.7 16.0 %collective-permute-start.37 = (bf16[2,2,4,160,384]{4,3,2,1,0:T(8,128)(2,1)}, bf16[2,2,4,160,384]{4,3,2,1,0:T(8,128)(2,1)}, u32[]{:S(2)}, u32[]{:S(2)}) collective-permute-start(bf16[2,2,4,160,384]{4,3,2,1,0:T(8,128)(2,1)} %get-tuple-element.239), channel_id=1, source_target_pairs={{0,1},{1,0},{2,3},{3,2},{4,5},{5,4},{6,7},{7,6},{8,9},{9,8},{10,11... | collective-permute-start | bytes 5898248 | tf_op jit(solution)/shard_map/ppermute | solution.py:806
  266.7 16.0 %collective-permute-start.33 = (bf16[2,2,192,384]{3,2,1,0:T(8,128)(2,1)}, bf16[2,2,192,384]{3,2,1,0:T(8,128)(2,1)S(1)}, u32[]{:S(2)}, u32[]{:S(2)}) collective-permute-start(bf16[2,2,192,384]{3,2,1,0:T(8,128)(2,1)} %fusion.7), channel_id=1, source_target_pairs={{0,2},{1,3},{2,0},{3,1},{4,6},{5,7},{6,4},{7,5},{8,10},{9,11},{10,... | collective-permute-start | bytes 1769480 | tf_op jit(solution)/shard_map/ppermute | solution.py:806
  267.0 15.7 %collective-permute-start.34 = (bf16[2,2,192,384]{3,2,1,0:T(8,128)(2,1)}, bf16[2,2,192,384]{3,2,1,0:T(8,128)(2,1)S(1)}, u32[]{:S(2)}, u32[]{:S(2)}) collective-permute-start(bf16[2,2,192,384]{3,2,1,0:T(8,128)(2,1)} %fusion.8), channel_id=1, source_target_pairs={{0,16},{1,17},{2,18},{3,19},{4,20},{5,21},{6,22},{7,23},{8,24},{9,... | collective-permute-start | bytes 1769480 | tf_op jit(solution)/shard_map/ppermute | solution.py:806
  268.3 22.2 %collective-permute-start.42 = (bf16[256,384]{1,0:T(8,128)(2,1)}, bf16[256,384]{1,0:T(8,128)(2,1)}, u32[]{:S(2)}, u32[]{:S(2)}) collective-permute-start(bf16[256,384]{1,0:T(8,128)(2,1)} %get-tuple-element.251), channel_id=1, source_target_pairs={{0,12},{1,13},{2,14},{3,15},{4,0},{5,1},{6,2},{7,3},{8,4},{9,5},{1... | collective-permute-start | bytes 589832 | tf_op jit(solution)/shard_map/ppermute | solution.py:813
  268.3 23.0 %collective-permute-start.43 = (bf16[256,384]{1,0:T(8,128)(2,1)S(1)}, bf16[256,384]{1,0:T(8,128)(2,1)}, u32[]{:S(2)}, u32[]{:S(2)}) collective-permute-start(bf16[256,384]{1,0:T(8,128)(2,1)S(1)} %get-tuple-element.252), channel_id=1, source_target_pairs={{0,8},{1,9},{2,10},{3,11},{4,12},{5,13},{6,14},{7,15},{8,0},{9,1},... | collective-permute-start | bytes 589832 | tf_op jit(solution)/shard_map/ppermute | solution.py:813
  287.2 20.5 %collective-permute-start.40 = (bf16[2,2,160,384]{3,2,1,0:T(8,128)(2,1)S(1)}, bf16[2,2,160,384]{3,2,1,0:T(8,128)(2,1)}, u32[]{:S(2)}, u32[]{:S(2)}) collective-permute-start(bf16[2,2,160,384]{3,2,1,0:T(8,128)(2,1)S(1)} %fusion.14), channel_id=1, source_target_pairs={{0,2},{1,3},{2,0},{3,1},{4,6},{5,7},{6,4},{7,5},{8,10},{9,11},{10,... | collective-permute-start | bytes 1474568 | tf_op jit(solution)/shard_map/ppermute | solution.py:806
  289.0 18.7 %collective-permute-start.41 = (bf16[2,2,160,384]{3,2,1,0:T(8,128)(2,1)S(1)}, bf16[2,2,160,384]{3,2,1,0:T(8,128)(2,1)}, u32[]{:S(2)}, u32[]{:S(2)}) collective-permute-start(bf16[2,2,160,384]{3,2,1,0:T(8,128)(2,1)S(1)} %fusion.15), channel_id=1, source_target_pairs={{0,16},{1,17},{2,18},{3,19},{4,20},{5,21},{6,22},{7,23},{8,24},{9,... | collective-permute-start | bytes 1474568 | tf_op jit(solution)/shard_map/ppermute | solution.py:806
  290.2 10.4 %collective-permute-start.44 = (bf16[256,384]{1,0:T(8,128)(2,1)}, bf16[256,384]{1,0:T(8,128)(2,1)}, u32[]{:S(2)}, u32[]{:S(2)}) collective-permute-start(bf16[256,384]{1,0:T(8,128)(2,1)} %get-tuple-element.253), channel_id=1, source_target_pairs={{0,4},{1,5},{2,6},{3,7},{4,8},{5,9},{6,10},{7,11},{8,12},{9,13},{1... | collective-permute-start | bytes 589832 | tf_op jit(solution)/shard_map/ppermute | solution.py:813
  290.5 17.2 %collective-permute-start.38 = (bf16[2,192,384]{2,1,0:T(8,128)(2,1)}, bf16[2,192,384]{2,1,0:T(8,128)(2,1)S(1)}, u32[]{:S(2)}, u32[]{:S(2)}) collective-permute-start(bf16[2,192,384]{2,1,0:T(8,128)(2,1)} %get-tuple-element.247), channel_id=1, source_target_pairs={{0,16},{1,17},{2,18},{3,19},{4,20},{5,21},{6,22},{7,23},{8,24},{9,... | collective-permute-start | bytes 884744 | tf_op jit(solution)/shard_map/ppermute | solution.py:806
  291.3 16.4 %collective-permute-start.39 = (bf16[2,192,384]{2,1,0:T(8,128)(2,1)S(1)}, bf16[2,192,384]{2,1,0:T(8,128)(2,1)}, u32[]{:S(2)}, u32[]{:S(2)}) collective-permute-start(bf16[2,192,384]{2,1,0:T(8,128)(2,1)S(1)} %get-tuple-element.248), channel_id=1, source_target_pairs={{0,2},{1,3},{2,0},{3,1},{4,6},{5,7},{6,4},{7,5},{8,10},{9,11},{10,... | collective-permute-start | bytes 884744 | tf_op jit(solution)/shard_map/ppermute | solution.py:806
  311.5 11.0 %collective-permute-start.45 = (bf16[2,160,384]{2,1,0:T(8,128)(2,1)S(1)}, bf16[2,160,384]{2,1,0:T(8,128)(2,1)S(1)}, u32[]{:S(2)}, u32[]{:S(2)}) collective-permute-start(bf16[2,160,384]{2,1,0:T(8,128)(2,1)S(1)} %get-tuple-element.260), channel_id=1, source_target_pairs={{0,16},{1,17},{2,18},{3,19},{4,20},{5,21},{6,22},{7,23},{8,24},{9,... | collective-permute-start | bytes 737288 | tf_op jit(solution)/shard_map/ppermute | solution.py:806
  312.8 9.7 %collective-permute-start.46 = (bf16[2,160,384]{2,1,0:T(8,128)(2,1)S(1)}, bf16[2,160,384]{2,1,0:T(8,128)(2,1)S(1)}, u32[]{:S(2)}, u32[]{:S(2)}) collective-permute-start(bf16[2,160,384]{2,1,0:T(8,128)(2,1)S(1)} %get-tuple-element.261), channel_id=1, source_target_pairs={{0,2},{1,3},{2,0},{3,1},{4,6},{5,7},{6,4},{7,5},{8,10},{9,11},{10,... | collective-permute-start | bytes 737288 | tf_op jit(solution)/shard_map/ppermute | solution.py:806
  314.7 10.3 %collective-permute-start.50 = (bf16[192,384]{1,0:T(8,128)(2,1)S(1)}, bf16[192,384]{1,0:T(8,128)(2,1)S(1)}, u32[]{:S(2)}, u32[]{:S(2)}) collective-permute-start(bf16[192,384]{1,0:T(8,128)(2,1)S(1)} %fusion.31), channel_id=1, source_target_pairs={{0,12},{1,13},{2,14},{3,15},{4,0},{5,1},{6,2},{7,3},{8,4},{9,5},{1... | collective-permute-start | bytes 442376 | tf_op jit(solution)/shard_map/ppermute | solution.py:813
  314.7 13.1 %collective-permute-start.51 = (bf16[192,384]{1,0:T(8,128)(2,1)}, bf16[192,384]{1,0:T(8,128)(2,1)S(1)}, u32[]{:S(2)}, u32[]{:S(2)}) collective-permute-start(bf16[192,384]{1,0:T(8,128)(2,1)} %get-tuple-element.273), channel_id=1, source_target_pairs={{0,8},{1,9},{2,10},{3,11},{4,12},{5,13},{6,14},{7,15},{8,0},{9,1},... | collective-permute-start | bytes 442376 | tf_op jit(solution)/shard_map/ppermute | solution.py:813
  316.3 11.5 %collective-permute-start.52 = (bf16[192,384]{1,0:T(8,128)(2,1)S(1)}, bf16[192,384]{1,0:T(8,128)(2,1)S(1)}, u32[]{:S(2)}, u32[]{:S(2)}) collective-permute-start(bf16[192,384]{1,0:T(8,128)(2,1)S(1)} %get-tuple-element.274), channel_id=1, source_target_pairs={{0,4},{1,5},{2,6},{3,7},{4,8},{5,9},{6,10},{7,11},{8,12},{9,13},{1... | collective-permute-start | bytes 442376 | tf_op jit(solution)/shard_map/ppermute | solution.py:813
  324.1 7.3 %collective-permute-start.53 = (bf16[240,384]{1,0:T(8,128)(2,1)S(1)}, bf16[240,384]{1,0:T(8,128)(2,1)S(1)}, u32[]{:S(2)}, u32[]{:S(2)}) collective-permute-start(bf16[240,384]{1,0:T(8,128)(2,1)S(1)} %convert_element_type.474), channel_id=1, source_target_pairs={{0,16},{1,17},{2,18},{3,19},{4,20},{5,21},{6,22},{7,23},{8,24},{9,... | collective-permute-start | bytes 552968 | tf_op jit(solution)/shard_map/ppermute | solution.py:806
  328.5 12.4 %collective-permute-start.48 = (bf16[160,384]{1,0:T(8,128)(2,1)S(1)}, bf16[160,384]{1,0:T(8,128)(2,1)S(1)}, u32[]{:S(2)}, u32[]{:S(2)}) collective-permute-start(bf16[160,384]{1,0:T(8,128)(2,1)S(1)} %get-tuple-element.270), channel_id=1, source_target_pairs={{0,8},{1,9},{2,10},{3,11},{4,12},{5,13},{6,14},{7,15},{8,0},{9,1},... | collective-permute-start | bytes 368648 | tf_op jit(solution)/shard_map/ppermute | solution.py:813
  329.5 11.3 %collective-permute-start.49 = (bf16[160,384]{1,0:T(8,128)(2,1)S(1)}, bf16[160,384]{1,0:T(8,128)(2,1)S(1)}, u32[]{:S(2)}, u32[]{:S(2)}) collective-permute-start(bf16[160,384]{1,0:T(8,128)(2,1)S(1)} %get-tuple-element.271), channel_id=1, source_target_pairs={{0,4},{1,5},{2,6},{3,7},{4,8},{5,9},{6,10},{7,11},{8,12},{9,13},{1... | collective-permute-start | bytes 368648 | tf_op jit(solution)/shard_map/ppermute | solution.py:813
  341.0 7.7 %collective-permute-start.54 = (bf16[336,384]{1,0:T(8,128)(2,1)S(1)}, bf16[336,384]{1,0:T(8,128)(2,1)S(1)}, u32[]{:S(2)}, u32[]{:S(2)}) collective-permute-start(bf16[336,384]{1,0:T(8,128)(2,1)S(1)} %pad_maximum_fusion.4), channel_id=1, source_target_pairs={{0,16},{1,17},{2,18},{3,19},{4,20},{5,21},{6,22},{7,23},{8,24},{9,... | collective-permute-start | bytes 774152 | tf_op jit(solution)/shard_map/ppermute | solution.py:806
  (37 other events, 393.8 us)

commit v5 on v4

--- a/solution.py
+++ b/solution.py
@@ -497,6 +497,10 @@
     )(place, x, ctx, seg, pooled_grad, *weights)
 
 
+def tiled(block, columns):
+    return pl.BlockSpec((block, columns), lambda i, *_: (i, 0))
+
+
 def resident(shape):
     return pl.BlockSpec(shape, lambda i, *_: (0,) * len(shape), pipeline_mode=pl.Buffered(1))
 
@@ -597,10 +601,11 @@
                 out_ref[pl.ds(row_at + block * rows, rows), :] = shard[:, cols]
 
 
-def pack_attention_kernel(place_ref, qkv_ref, small_ref, out_ref):
+def pack_attention_kernel(place_ref, qkv_ref, bias_ref, out_ref):
     unit = qkv_ref.shape[0]
     cut_columns(place_ref[0], qkv_ref, out_ref, 0, 3)
-    out_ref[pl.ds(3 * unit, SMALL), :] = small_ref[...]
+    out_ref[pl.ds(3 * unit, SMALL), :] = jnp.zeros((SMALL, BLOCK), BF16)
+    out_ref[pl.ds(3 * unit, 1), pl.ds(0, 2 * unit)] = bias_ref[...]
 
 
 def pack_feedforward_kernel(place_ref, up_ref, down_ref, out_w_ref, small_ref, out_ref):
@@ -636,38 +641,70 @@
         send_ref[at] = jnp.where(first, odd, even)
 
 
-def down_gradient_kernel(place_ref, active_ref, branch_ref, keep_ref, send_ref):
+def write_back(regions, steps, pairs, sems):
+    step = pl.program_id(0)
+
+    def copies(at_step):
+        for number, region in enumerate(regions(at_step)):
+            for side, (stored, result) in enumerate(pairs):
+                sem = sems.at[at_step, number, side]
+                yield pltpu.make_async_copy(stored.at[region], result.at[region], sem)
+
+    for copy in copies(step):
+        copy.start()
+
+    @pl.when(step == steps - 1)
+    def _():
+        for at_step in range(steps):
+            for copy in copies(at_step):
+                copy.wait()
+
+
+def down_gradient_kernel(place_ref, active_ref, branch_ref, keep_out, send_out, keep_ref, send_ref, sems):
     grad = transpose_times(active_ref[...], branch_ref[...]).astype(BF16)
     rows = grad.shape[0] // 4
+    y, z, x, core = place_of(place_ref)
+    first = core == 0
+    turn = (z - pl.program_id(0)) & 3
     for half in range(2):
-
-        def values(s):
-            return grad[(s % 4) * rows : (s % 4 + 1) * rows, half * BLOCK : (half + 1) * BLOCK]
-
-        y, z, x, core = place_of(place_ref)
-        turn = (z - pl.program_id(0)) & 3
-        first = core == 0
+        cols = slice(half * BLOCK, (half + 1) * BLOCK)
         for plane_x in range(2):
-            even, odd = values(plane_x * 2), values(plane_x * 2 + 1)
+            even = grad[2 * plane_x * rows : (2 * plane_x + 1) * rows, cols]
+            odd = grad[(2 * plane_x + 1) * rows : (2 * plane_x + 2) * rows, cols]
             at = (half ^ y, plane_x ^ x, turn)
             keep_ref[at] = jnp.where(first, even, odd)
             send_ref[at] = jnp.where(first, odd, even)
+    every = slice(None)
+
+    def regions(step):
+        return [(every, every, (z - step) & 3)]
+
+    write_back(regions, 4, ((keep_ref, keep_out), (send_ref, send_out)), sems)
+
+
+def block_place(number, blocks, unit):
+    half = number // blocks
+    row = (number - half * blocks) * unit
+    return half, row if isinstance(row, int) else pl.multiple_of(row, unit)
 
 
 def store_columns(place_ref, keep_ref, send_ref, grad, first_block, blocks):
     unit = grad.shape[0] // 16
     for part in range(2):
-        number = first_block + part
-        half = number // blocks
-        row_at = (number - half * blocks) * unit
-        if not isinstance(row_at, int):
-            row_at = pl.multiple_of(row_at, unit)
+        half, row_at = block_place(first_block + part, blocks, unit)
 
         def values(s):
             return grad[s * unit : (s + 1) * unit, part * BLOCK : (part + 1) * BLOCK]
 
         for plane_z in range(4):
             store_shards(place_ref, keep_ref, send_ref, plane_z, half, row_at, unit, values)
+
+
+def column_regions(place_ref, first_block, blocks, unit):
+    every = slice(None)
+    for part in range(2):
+        half, row_at = block_place(first_block + part, blocks, unit)
+        yield half ^ place_ref[0], every, every, pl.ds(row_at, unit)
 
 
 def store_small(place_ref, keep_ref, send_ref, row_at, values):
@@ -677,31 +714,30 @@
 
 
 def up_gradient_kernel(
-    place_ref, normed_ref, hidden_ref, ctx_ref, attended_ref, sums_ref, up_sums_ref, keep_ref, send_ref, turned_ref
+    place_ref, normed_ref, hidden_ref, ctx_ref, attended_ref, sums_ref, up_sums_ref,
+    keep_out, send_out, keep_ref, send_ref, sems, turned_ref, total_ref,
 ):
     step = pl.program_id(0)
-    last = pl.num_programs(0) - 1
+    steps = up_sums_ref.shape[1] // normed_ref.shape[1]
     width = normed_ref.shape[1]
     unit = width // 16
-    blocks = last
 
     @pl.when(step == 0)
     def _():
         turned_ref[...] = normed_ref[...].T
-
-    @pl.when(step < last)
+        total_ref[...] = jnp.zeros_like(total_ref)
+
+    grad = product(turned_ref[...], hidden_ref[...]).astype(BF16)
+    store_columns(place_ref, keep_ref, send_ref, grad, 2 * step, steps)
+    total_ref[...] += transpose_times(ctx_ref[...], attended_ref[...])
+
+    @pl.when(step == steps - 1)
     def _():
-        grad = product(turned_ref[...], hidden_ref[...]).astype(BF16)
-        store_columns(place_ref, keep_ref, send_ref, grad, 2 * step, blocks)
-
-    @pl.when(step == last)
-    def _():
-        grad = transpose_times(ctx_ref[...], attended_ref[...]).astype(BF16)
-        steps = up_sums_ref.shape[1] // width
         for part in range(2):
 
             def values(s):
-                return grad[s * unit : (s + 1) * unit, part * BLOCK : (part + 1) * BLOCK]
+                cols = pl.ds(part * BLOCK, BLOCK)
+                return total_ref[pl.ds(s * unit, unit), cols].astype(BF16)
 
             for plane_z in range(4):
                 store_shards(place_ref, keep_ref, send_ref, plane_z, part, steps * unit, unit, values)
@@ -721,11 +757,30 @@
 
         store_small(place_ref, keep_ref, send_ref, (steps + 1) * unit, small)
 
-
-def qkv_gradient_kernel(place_ref, x_ref, grad_ref, sums_ref, keep_ref, send_ref, turned_ref):
+    every = slice(None)
+
+    def regions(at_step):
+        yield from column_regions(place_ref, 2 * at_step, steps, unit)
+        if isinstance(at_step, int) and at_step == steps - 1:
+            yield every, every, every, pl.ds(steps * unit, unit + SMALL)
+
+    @pl.when(step == steps - 1)
+    def _():
+        region = (every, every, every, pl.ds(steps * unit, unit + SMALL))
+        for side, (stored, result) in enumerate(((keep_ref, keep_out), (send_ref, send_out))):
+            pltpu.make_async_copy(stored.at[region], result.at[region], sems.at[steps - 1, 2, side]).start()
+
+    write_back(regions, steps, ((keep_ref, keep_out), (send_ref, send_out)), sems)
+
+
+def qkv_gradient_kernel(
+    place_ref, x_ref, grad_ref, sums_ref, keep_out, send_out, keep_ref, send_ref, sems, turned_ref
+):
     step = pl.program_id(0)
     width = x_ref.shape[1]
     unit = width // 16
+    every = slice(None)
+    pairs = ((keep_ref, keep_out), (send_ref, send_out))
 
     @pl.when(step == 0)
     def _():
@@ -740,20 +795,34 @@
             return part[:, :BLOCK].astype(BF16)
 
         store_small(place_ref, keep_ref, send_ref, 3 * unit, small)
+        region = (every, every, every, pl.ds(3 * unit, SMALL))
+        for side, (stored, result) in enumerate(pairs):
+            pltpu.make_async_copy(stored.at[region], result.at[region], sems.at[0, 2, side]).start()
 
     grad = product(turned_ref[...], grad_ref[...]).astype(BF16)
     store_columns(place_ref, keep_ref, send_ref, grad, 2 * step, 3)
 
-
-def weight_gradient(kernel, name, place, rows, steps, arrays, specs, flops, turned=None):
+    def regions(at_step):
+        yield from column_regions(place_ref, 2 * at_step, 3, unit)
+        if isinstance(at_step, int) and at_step == 0:
+            yield every, every, every, pl.ds(3 * unit, SMALL)
+
+    write_back(regions, 3, pairs, sems)
+
+
+def weight_gradient(kernel, name, place, rows, steps, arrays, specs, flops, scratch=()):
     shape = (2, 2, 4, rows, BLOCK)
-    whole = pl.BlockSpec(shape, lambda i, *_: (0,) * 5)
     spec = pltpu.PrefetchScalarGridSpec(
         num_scalar_prefetch=1,
         grid=(steps,),
         in_specs=specs,
-        out_specs=[whole, whole],
-        scratch_shapes=[] if turned is None else [pltpu.VMEM(turned, BF16)],
+        out_specs=[pl.BlockSpec(memory_space=pl.ANY)] * 2,
+        scratch_shapes=[
+            pltpu.VMEM(shape, BF16),
+            pltpu.VMEM(shape, BF16),
+            pltpu.SemaphoreType.DMA((steps, 3, 2)),
+            *scratch,
+        ],
     )
     return pl.pallas_call(
         kernel,
@@ -916,7 +985,7 @@
         place,
         3 * unit + SMALL,
         qkv_weight,
-        jnp.pad(qv_bias[None], ((0, SMALL - 1), (0, BLOCK - 2 * unit))),
+        qv_bias[None],
     )
     vectors = [out_bias, first_gain, first_shift, down_bias, second_gain, second_shift, up_bias]
     own_attention, *vectors = together(own_attention, *vectors)
@@ -968,18 +1037,18 @@
         "up_gradient",
         place,
         (ratio + 1) * unit + SMALL,
-        ratio + 1,
+        ratio,
         (normed, hidden_grad, ctx, attended, sums, up_sums),
         [
             resident((tokens, width)),
-            pl.BlockSpec((tokens, width), lambda i, *_: (0, jnp.minimum(i, ratio - 1))),
-            resident((tokens, width)),
-            resident((tokens, width)),
+            pl.BlockSpec((tokens, width), lambda i, *_: (0, i)),
+            tiled(tokens // ratio, width),
+            tiled(tokens // ratio, width),
             resident(sums.shape),
             resident(up_sums.shape),
         ],
         2 * tokens * width * (hidden + width),
-        (width, tokens),
+        (pltpu.VMEM((width, tokens), BF16), pltpu.VMEM((width, width), F32)),
     )
     up_keep, up_send, active = together(up_keep, up_send, active)
     up_got = across(up_send, CORE)
@@ -1017,26 +1086,28 @@
             resident(qv_sums.shape),
         ],
         6 * tokens * width * width,
-        (width, tokens),
-    )
-    low_u, high_u, qkv_keep, qkv_send = together(*up_second, qkv_keep, qkv_send)
-    u1, u2, u3, qkv_send, qkv_grad = together(*up.third((low_u, high_u)), qkv_send, qkv_grad)
+        (pltpu.VMEM((width, tokens), BF16),),
+    )
+    low_u, high_u, low_d, high_d, qkv_keep, qkv_send = together(*up_second, *down_first, qkv_keep, qkv_send)
+    u1, u2, u3, low_d, high_d, qkv_send, qkv_grad = together(
+        *up.third((low_u, high_u)), *down.second((low_d, high_d)), qkv_send, qkv_grad
+    )
     up_third = up.send_third((u1, u2, u3))
+    down_second = down.send_second((low_d, high_d))
     qkv_got = across(qkv_send, CORE)
     grad_input = input_gradient(first_grad, qkv_grad, qkv_matrix, (0, 1, 4))
-    low_d, high_d, qkv_got, grad_input = together(*down_first, qkv_got, grad_input)
+    low_d, high_d, u1, u3, qkv_got, grad_input = together(
+        *down_second, up_third[0], up_third[2], qkv_got, grad_input
+    )
     qkv_sum = Reduction(qkv_keep, qkv_got)
-    low_d, high_d, low_q, high_q, grad_input = together(*down.second((low_d, high_d)), *qkv_sum.first(), grad_input)
-    down_second = down.send_second((low_d, high_d))
+    d1, d2, d3, low_q, high_q, grad_input = together(*down.third((low_d, high_d)), *qkv_sum.first(), grad_input)
     qkv_first = qkv_sum.send_first((low_q, high_q))
     grad_input = input_gradient(first_grad, qkv_grad, qkv_matrix, (1, 3, 4), (grad_input,))
-    low_d, high_d, low_q, high_q, *up_third, grad_input = together(*down_second, *qkv_first, *up_third, grad_input)
-    d1, d2, d3, low_q, high_q, grad_input = together(
-        *down.third((low_d, high_d)), *qkv_sum.second((low_q, high_q)), grad_input
-    )
+    low_q, high_q, u2, grad_input = together(*qkv_first, up_third[1], grad_input)
+    low_q, high_q, d1, d2, d3, grad_input = together(*qkv_sum.second((low_q, high_q)), d1, d2, d3, grad_input)
     qkv_second = qkv_sum.send_second((low_q, high_q))
     down_third = down.send_third((d1, d2, d3))
-    up_total = up.finish(up_third)
+    up_total = up.finish((u1, u2, u3))
     up_part, up_small = up_total[: (ratio + 1) * unit], up_total[(ratio + 1) * unit :]
     grad_input = input_gradient(first_grad, qkv_grad, qkv_matrix, (3, 4, 4), (grad_input,))
     low_q, high_q, grad_input = together(*qkv_second, grad_input)

time: 351 us -> 342 us (0.974)
  waiting for transfers between devices: 68.7 us -> 60.3 us
  Pallas kernels: 194 us -> 189 us
  starting transfers between devices: 47.5 us -> 52 us
    ppermute x40, waiting for transfers between devices: 42.5 us -> 33.4 us  [across(): return lax.ppermute(value, AXES, [(i, i ^ mask) for i in range(DEVICES)])]
    pallas_call x3, Pallas kernels: 54.4 us -> 50.4 us  [weight_gradient(): pl.pallas_call(kernel, grid_spec=spec, out_shape=[jax.ShapeDtypeStruct(sh...]
  transfers between devices with their start and end apart: 55 -> 55, of which waited for: 18 -> 20; matrix products, arithmetic and copies ran while one was open for 5% -> 4% of each run, Pallas kernels for 27% -> 27%
where the time goes in v5:
time: 342 us; the launch traced here: 341 us
  Pallas kernels  189 us (55%)
  waiting for transfers between devices  60.3 us (18%)
  starting transfers between devices  52 us (15%)
  other arithmetic  27 us (8%)
  local copies, waits for them, and re-layouts  11.3 us (3%)
    pallas_call x1, Pallas kernels, feedforward(): pl.pallas_call(functools.partial(feedforward_gathered_kernel, length, chu...  72.8 us
    pallas_call x3, Pallas kernels, weight_gradient(): pl.pallas_call(kernel, grid_spec=spec, out_shape=[jax.ShapeDtypeStruct(sh...  50.4 us
    ppermute x40, waiting for transfers between devices, across(): return lax.ppermute(value, AXES, [(i, i ^ mask) for i in range(DEVICES)])  33.4 us
    ppermute x40, starting transfers between devices, across(): return lax.ppermute(value, AXES, [(i, i ^ mask) for i in range(DEVICES)])  29.6 us
    ppermute x15, waiting for transfers between devices, along_z(): return lax.ppermute(value, AXES, [(i, target(i)) for i in range(DEVICES)])  26.9 us
    ppermute x15, starting transfers between devices, along_z(): return lax.ppermute(value, AXES, [(i, target(i)) for i in range(DEVICES)])  22.4 us
    pallas_call x3, Pallas kernels, input_gradient(): pl.pallas_call(input_gradient_kernel, grid=(steps,), in_specs=[pl.BlockSp...  20.4 us
    pallas_call x1, Pallas kernels, attention_backward(): pl.pallas_call(functools.partial(attention_back_kernel, length, width, fi...  17.5 us
  transfers between devices with their start and end apart: 55, of which 20 were waited for; matrix products, arithmetic and copies ran while one was open for 4% of the time, Pallas kernels for 27%

profile of v5, /device:TPU:0, one launch (start us, length us, event | category | flops | bytes accessed | tf_op | source)
XLA Modules:
  0.0 341.4 jit_solution(14137250699896115667)
XLA Ops:
  1.3 2.3 pack_attention.1
  3.5 5.0 %collective-permute-start.2 = (bf16[160,384]{1,0:T(8,128)(2,1)}, bf16[160,384]{1,0:T(8,128)(2,1)S(1)}, u32[]{:S(2)}, u32[]{:S(2)}) collective-permute-start(bf16[160,384]{1,0:T(8,128)(2,1)} %pack_attention.1), channel_id=1, source_target_pairs={{0,12},{1,13},{2,14},{3,15},{4,0},{5,1},{6,2},{7,3},{8,4},{9,5},{1... | collective-permute-start | bytes 368648 | tf_op jit(solution)/shard_map/ppermute | solution.py:882
  15.5 2.5 pack_feedforward.1
  18.0 1.4 collective-permute-done.1
  20.4 1.6 collective-permute-start.4
  22.0 1.5 collective-permute-start.3
  24.6 9.6 %collective-permute-done.5 = bf16[448,384]{1,0:T(8,128)(2,1)S(1)} collective-permute-done((bf16[448,384]{1,0:T(8,128)(2,1)}, bf16[448,384]{1,0:T(8,128)(2,1)S(1)}, u32[]{:S(2)}, u32[]{:S(2)}) %collective-permute-start.5) | collective-permute-done | bytes 344096 | tf_op jit(solution)/shard_map/ppermute | solution.py:882
  34.3 1.5 collective-permute-start.7
  37.9 2.7 collective-permute-done.7.rest_4_
  40.6 1.4 collective-permute-done.6.rest_3_
  42.0 1.4 collective-permute-start.8
  45.3 4.0 %collective-permute-done.8 = bf16[448,384]{1,0:T(8,128)(2,1)S(1)} collective-permute-done((bf16[448,384]{1,0:T(8,128)(2,1)S(1)}, bf16[448,384]{1,0:T(8,128)(2,1)S(1)}, u32[]{:S(2)}, u32[]{:S(2)}) %collective-permute-start.8) | collective-permute-done | bytes 344096 | tf_op jit(solution)/shard_map/ppermute | solution.py:882
  50.4 2.6 collective-permute-start.16
  53.0 13.2 %attention_forward.2 = (bf16[2048,2304]{1,0:T(8,128)(2,1)}, bf16[2048,768]{1,0:T(8,128)(2,1)}, bf16[768,2304]{1,0:T(8,128)(2,1)}, f32[8,2304]{1,0:T(8,128)}) custom-call(s32[4]{0:T(128)} %pad_add_fusion.place_ref, bf16[2048,768]{1,0:T(8,128)(2,1)} %bitcast.145, s32[16,128]{1,0:T(8,128)} %seg_ref.7, bf16[4,160,384]{2,1,0:T(8,128)(2,1)} %copy-done.7, ...), custom_call_target="tpu_custom_call" | custom-call | flops 4429185024 | bytes 11403264 | tf_op jit(solution)/shard_map/attention_forward/pallas_call | solution.py:249
  66.3 1.9 collective-permute-start.18
  68.3 2.0 collective-permute-start.17
  70.8 10.4 %attention_forward.3 = (bf16[2048,2304]{1,0:T(8,128)(2,1)}, bf16[2048,768]{1,0:T(8,128)(2,1)}) custom-call(bf16[2048,768]{1,0:T(8,128)(2,1)} %bitcast.146, s32[16,128]{1,0:T(8,128)} %seg_ref.7, bf16[768,2304]{1,0:T(8,128)(2,1)} %get-tuple-element.190.w_ref, f32[8,2304]{1,0:T(8,128)} %get-tuple-element.191.bias_ref, ...), custom_call_target="tpu_custom_call", output_to_operand_aliasing={{0}: (4, {}), {1}: (5, {})} | custom-call | flops 4429185024 | bytes 11403264 | tf_op jit(solution)/shard_map/attention_forward/pallas_call | solution.py:226
  84.0 15.2 %collective-permute-done.19.rest_6_ = bf16[2,448,384]{2,1,0:T(8,128)(2,1)S(1)} collective-permute-done((bf16[2,448,384]{2,1,0:T(8,128)(2,1)S(1)}, bf16[2,448,384]{2,1,0:T(8,128)(2,1)S(1)}, u32[]{:S(2)}, u32[]{:S(2)}) %collective-permute-start.19) | collective-permute-done | bytes 688160 | tf_op jit(solution)/shard_map/ppermute | solution.py:875
  102.5 72.8 %feedforward.1 = (f32[16,4,768]{2,1,0:T(4,128)}, bf16[2048,3072]{1,0:T(8,128)(2,1)}, bf16[2048,3072]{1,0:T(8,128)(2,1)}, bf16[2048,768]{1,0:T(8,128)(2,1)}, bf16...) custom-call(s32[4]{0:T(128)} %pad_add_fusion.place_ref, ...), custom_call_target="tpu_custom_call" | custom-call | flops 43486543872 | bytes 62914560 | tf_op jit(solution)/shard_map/feedforward/pallas_call | solution.py:492
  175.3 20.8 %up_gradient.1 = (bf16[2,2,4,256,384]{4,3,2,1,0:T(8,128)(2,1)}, bf16[2,2,4,256,384]{4,3,2,1,0:T(8,128)(2,1)}) custom-call(s32[4]{0:T(128)} %pad_add_fusion.place_ref, bf16[2048,768]{1,0:T(8,128)(2,1)} %get-tuple-element.202.normed_ref, bf16[2048,3072]{1,0:T(8,128)(2,1)} %get-tuple-element.203.hidden_ref, bf16[2048,768]{1,0:T(8,128)(2,1)} %get-tuple-element.196.ctx_ref, ...), custom_call_target="tpu_custom_call" | custom-call | flops 12079595520 | bytes 22142976 | tf_op jit(solution)/shard_map/up_gradient/pallas_call | solution.py:827
  196.3 15.8 %down_gradient.1 = (bf16[2,2,4,192,384]{4,3,2,1,0:T(8,128)(2,1)}, bf16[2,2,4,192,384]{4,3,2,1,0:T(8,128)(2,1)}) custom-call(s32[4]{0:T(128)} %pad_add_fusion.place_ref, bf16[2048,3072]{1,0:T(8,128)(2,1)} %get-tuple-element.212.active_ref, bf16[2048,768]{1,0:T(8,128)(2,1)} %get-tuple-element.213.branch_ref), custom_call_target="tpu_custom_call" | custom-call | flops 9663676416 | bytes 15728640 | tf_op jit(solution)/shard_map/down_gradient/pallas_call | solution.py:827
  212.1 2.3 fusion.1
  214.4 2.2 fusion
  218.0 17.5 %attention_backward.1 = (bf16[2048,2304]{1,0:T(8,128)(2,1)}, f32[8,1536]{1,0:T(8,128)}) custom-call(bf16[2048,2304]{1,0:T(8,128)(2,1)} %get-tuple-element.222.qkv_ref, bf16[2048,768]{1,0:T(8,128)(2,1)} %get-tuple-element.223.grad_ref, s32[16,128]{1,0:T(8,128)} %seg_ref.7), custom_call_target="tpu_custom_call" | custom-call | flops 4026531840 | bytes 22020096 | tf_op jit(solution)/shard_map/attention_backward/pallas_call | solution.py:568
  235.5 1.4 collective-permute-done.30
  236.9 2.0 fusion.8
  238.9 2.0 fusion.7
  241.0 1.7 fusion.5
  243.4 1.7 collective-permute-start.34
  246.7 13.8 %qkv_gradient.1 = (bf16[2,2,4,160,384]{4,3,2,1,0:T(8,128)(2,1)}, bf16[2,2,4,160,384]{4,3,2,1,0:T(8,128)(2,1)}) custom-call(s32[4]{0:T(128)} %pad_add_fusion.place_ref, bf16[2048,768]{1,0:T(8,128)(2,1)} %bitcast.148, bf16[2048,2304]{1,0:T(8,128)(2,1)} %get-tuple-element.251.grad_ref, f32[8,1536]{1,0:T(8,128)} %get-tuple-element.236.sums_ref), custom_call_target="tpu_custom_call" | custom-call | flops 7247757312 | bytes 12607488 | tf_op jit(solution)/shard_map/qkv_gradient/pallas_call | solution.py:827
  260.6 5.5 %collective-permute-done.35 = bf16[2,2,192,384]{3,2,1,0:T(8,128)(2,1)S(1)} collective-permute-done((bf16[2,2,192,384]{3,2,1,0:T(8,128)(2,1)}, bf16[2,2,192,384]{3,2,1,0:T(8,128)(2,1)S(1)}, u32[]{:S(2)}, u32[]{:S(2)}) %collective-permute-start.35) | collective-permute-done | bytes 589856 | tf_op jit(solution)/shard_map/ppermute | solution.py:875
  266.1 1.8 fusion.3
  268.7 1.5 fusion.12
  271.6 1.4 collective-permute-start.38
  273.0 2.0 collective-permute-start.40
  275.0 5.9 %input_gradient.3.outs_0_ = f32[2048,768]{1,0:T(8,128)} custom-call(f32[2048,768]{1,0:T(8,128)} %get-tuple-element.250.first_ref, bf16[2048,2304]{1,0:T(8,128)(2,1)} %get-tuple-element.251.grad_ref, bf16[768,2304]{1,0:T(8,128)(2,1)} %get-tuple-element.190.w_ref), custom_call_target="tpu_custom_call" | custom-call | flops 1811939328 | bytes 5505024 | tf_op jit(solution)/shard_map/input_gradient/pallas_call | solution.py:847
  280.9 3.1 collective-permute-done.39
  285.3 1.9 fusion.14
  287.3 1.6 fusion.10
  292.9 8.8 %input_gradient.4.outs_0_ = f32[2048,768]{1,0:T(8,128)} custom-call(f32[2048,768]{1,0:T(8,128)} %get-tuple-element.250.first_ref, bf16[2048,2304]{1,0:T(8,128)(2,1)} %get-tuple-element.251.grad_ref, bf16[768,2304]{1,0:T(8,128)(2,1)} %get-tuple-element.190.w_ref, f32[2048,768]{1,0:T(8,128)} %input_gradient.3.outs_0_), custom_call_target="tpu_custom_call", output_to_operand_aliasing={{}: (3, {})} | custom-call | flops 3623878656 | bytes 11010048 | tf_op jit(solution)/shard_map/input_gradient/pallas_call | solution.py:847
  304.6 1.4 collective-permute-start.46
  307.1 1.8 collective-permute-start.50
  309.9 1.9 collective-permute-start.52
  311.9 5.7 %input_gradient.5 = f32[2048,768]{1,0:T(8,128)} custom-call(f32[2048,768]{1,0:T(8,128)} %get-tuple-element.250.first_ref, bf16[2048,2304]{1,0:T(8,128)(2,1)} %get-tuple-element.251.grad_ref, bf16[768,2304]{1,0:T(8,128)(2,1)} %get-tuple-element.190.w_ref, f32[2048,768]{1,0:T(8,128)} %input_gradient.4.outs_0_), custom_call_target="tpu_custom_call", output_to_operand_aliasing={{}: (3, {})} | custom-call | flops 1811939328 | bytes 5505024 | tf_op jit(solution)/shard_map/input_gradient/pallas_call | solution.py:847
  317.6 1.5 fusion.17
  323.2 1.9 collective-permute-start.49
  327.2 6.5 %collective-permute-done.48 = bf16[160,384]{1,0:T(8,128)(2,1)S(1)} collective-permute-done((bf16[160,384]{1,0:T(8,128)(2,1)S(1)}, bf16[160,384]{1,0:T(8,128)(2,1)S(1)}, u32[]{:S(2)}, u32[]{:S(2)}) %collective-permute-start.48) | collective-permute-done | bytes 122912 | tf_op jit(solution)/shard_map/ppermute | solution.py:882
  336.8 3.4 %collective-permute-done.54 = bf16[336,384]{1,0:T(8,128)(2,1)S(1)} collective-permute-done((bf16[336,384]{1,0:T(8,128)(2,1)S(1)}, bf16[336,384]{1,0:T(8,128)(2,1)S(1)}, u32[]{:S(2)}, u32[]{:S(2)}) %collective-permute-start.54) | collective-permute-done | bytes 258080 | tf_op jit(solution)/shard_map/ppermute | solution.py:875
  (208 shorter events, 47.8 us)
Async XLA Ops:
  3.5 14.5 %collective-permute-start.2 = (bf16[160,384]{1,0:T(8,128)(2,1)}, bf16[160,384]{1,0:T(8,128)(2,1)S(1)}, u32[]{:S(2)}, u32[]{:S(2)}) collective-permute-start(bf16[160,384]{1,0:T(8,128)(2,1)} %pack_attention.1), channel_id=1, source_target_pairs={{0,12},{1,13},{2,14},{3,15},{4,0},{5,1},{6,2},{7,3},{8,4},{9,5},{1... | collective-permute-start | bytes 368648 | tf_op jit(solution)/shard_map/ppermute | solution.py:882
  8.6 10.8 %collective-permute-start.1 = (bf16[160,384]{1,0:T(8,128)(2,1)}, bf16[160,384]{1,0:T(8,128)(2,1)S(1)}, u32[]{:S(2)}, u32[]{:S(2)}) collective-permute-start(bf16[160,384]{1,0:T(8,128)(2,1)} %pack_attention.1), channel_id=1, source_target_pairs={{0,8},{1,9},{2,10},{3,11},{4,12},{5,13},{6,14},{7,15},{8,0},{9,1},... | collective-permute-start | bytes 368648 | tf_op jit(solution)/shard_map/ppermute | solution.py:882
  8.6 10.8 %collective-permute-start = (bf16[160,384]{1,0:T(8,128)(2,1)}, bf16[160,384]{1,0:T(8,128)(2,1)S(1)}, u32[]{:S(2)}, u32[]{:S(2)}) collective-permute-start(bf16[160,384]{1,0:T(8,128)(2,1)} %pack_attention.1), channel_id=1, source_target_pairs={{0,4},{1,5},{2,6},{3,7},{4,8},{5,9},{6,10},{7,11},{8,12},{9,13},{1... | collective-permute-start | bytes 368648 | tf_op jit(solution)/shard_map/ppermute | solution.py:882
  20.4 13.8 %collective-permute-start.4 = (bf16[4,160,384]{2,1,0:T(8,128)(2,1)S(1)}, bf16[4,160,384]{2,1,0:T(8,128)(2,1)S(1)}, u32[]{:S(2)}, u32[]{:S(2)}) collective-permute-start(bf16[4,160,384]{2,1,0:T(8,128)(2,1)S(1)} %pad_maximum_fusion.3.rest_0_), channel_id=1, source_target_pairs={{0,16},{1,17},{2,18},{3,19},{4,20},{5,21},{6,22},{7,23},{8,24},{9,... | collective-permute-start | bytes 1474568 | tf_op jit(solution)/shard_map/ppermute | solution.py:875
  22.0 12.3 %collective-permute-start.3 = (bf16[4,160,384]{2,1,0:T(8,128)(2,1)S(1)}, bf16[4,160,384]{2,1,0:T(8,128)(2,1)S(1)}, u32[]{:S(2)}, u32[]{:S(2)}) collective-permute-start(bf16[4,160,384]{2,1,0:T(8,128)(2,1)S(1)} %pad_maximum_fusion.3.rest_0_), channel_id=1, source_target_pairs={{0,2},{1,3},{2,0},{3,1},{4,6},{5,7},{6,4},{7,5},{8,10},{9,11},{10,... | collective-permute-start | bytes 1474568 | tf_op jit(solution)/shard_map/ppermute | solution.py:875
  23.5 10.8 %collective-permute-start.5 = (bf16[448,384]{1,0:T(8,128)(2,1)}, bf16[448,384]{1,0:T(8,128)(2,1)S(1)}, u32[]{:S(2)}, u32[]{:S(2)}) collective-permute-start(bf16[448,384]{1,0:T(8,128)(2,1)} %pack_feedforward.1), channel_id=1, source_target_pairs={{0,4},{1,5},{2,6},{3,7},{4,8},{5,9},{6,10},{7,11},{8,12},{9,13},{1... | collective-permute-start | bytes 1032200 | tf_op jit(solution)/shard_map/ppermute | solution.py:882
  24.6 18.8 %collective-permute-start.9 = (bf16[4,160,384]{2,1,0:T(8,128)(2,1)S(1)}, bf16[4,160,384]{2,1,0:T(8,128)(2,1)S(1)}, u32[]{:S(2)}, u32[]{:S(2)}) collective-permute-start(bf16[4,160,384]{2,1,0:T(8,128)(2,1)S(1)} %pad_maximum_fusion.3.rest_0_), channel_id=1, source_target_pairs={{0,1},{1,0},{2,3},{3,2},{4,5},{5,4},{6,7},{7,6},{8,9},{9,8},{10,11... | collective-permute-start | bytes 1474568 | tf_op jit(solution)/shard_map/ppermute | solution.py:875
  34.3 6.3 %collective-permute-start.7 = (bf16[2,160,384]{2,1,0:T(8,128)(2,1)S(1)}, bf16[2,160,384]{2,1,0:T(8,128)(2,1)S(1)}, u32[]{:S(2)}, u32[]{:S(2)}) collective-permute-start(bf16[2,160,384]{2,1,0:T(8,128)(2,1)S(1)} %slice.314), channel_id=1, source_target_pairs={{0,2},{1,3},{2,0},{3,1},{4,6},{5,7},{6,4},{7,5},{8,10},{9,11},{10,... | collective-permute-start | bytes 737288 | tf_op jit(solution)/shard_map/ppermute | solution.py:875
  36.3 7.6 %collective-permute-start.10 = (bf16[4,160,384]{2,1,0:T(8,128)(2,1)S(1)}, bf16[4,160,384]{2,1,0:T(8,128)(2,1)S(1)}, u32[]{:S(2)}, u32[]{:S(2)}) collective-permute-start(bf16[4,160,384]{2,1,0:T(8,128)(2,1)S(1)} %collective-permute-done.3.rest_1_), channel_id=1, source_target_pairs={{0,1},{1,0},{2,3},{3,2},{4,5},{5,4},{6,7},{7,6},{8,9},{9,8},{10,11... | collective-permute-start | bytes 1474568 | tf_op jit(solution)/shard_map/ppermute | solution.py:875
  36.3 7.6 %collective-permute-start.11 = (bf16[4,160,384]{2,1,0:T(8,128)(2,1)S(1)}, bf16[4,160,384]{2,1,0:T(8,128)(2,1)S(1)}, u32[]{:S(2)}, u32[]{:S(2)}) collective-permute-start(bf16[4,160,384]{2,1,0:T(8,128)(2,1)S(1)} %collective-permute-done.4.rest_2_), channel_id=1, source_target_pairs={{0,1},{1,0},{2,3},{3,2},{4,5},{5,4},{6,7},{7,6},{8,9},{9,8},{10,11... | collective-permute-start | bytes 1474568 | tf_op jit(solution)/shard_map/ppermute | solution.py:875
  42.0 7.3 %collective-permute-start.8 = (bf16[448,384]{1,0:T(8,128)(2,1)S(1)}, bf16[448,384]{1,0:T(8,128)(2,1)S(1)}, u32[]{:S(2)}, u32[]{:S(2)}) collective-permute-start(bf16[448,384]{1,0:T(8,128)(2,1)S(1)} %copy-done.4), channel_id=1, source_target_pairs={{0,12},{1,13},{2,14},{3,15},{4,0},{5,1},{6,2},{7,3},{8,4},{9,5},{1... | collective-permute-start | bytes 1032200 | tf_op jit(solution)/shard_map/ppermute | solution.py:882
  49.3 16.9 %collective-permute-start.15 = (bf16[2,448,384]{2,1,0:T(8,128)(2,1)S(1)}, bf16[2,448,384]{2,1,0:T(8,128)(2,1)S(1)}, u32[]{:S(2)}, u32[]{:S(2)}) collective-permute-start(bf16[2,448,384]{2,1,0:T(8,128)(2,1)S(1)} %pad_maximum_fusion.rest_0_), channel_id=1, source_target_pairs={{0,16},{1,17},{2,18},{3,19},{4,20},{5,21},{6,22},{7,23},{8,24},{9,... | collective-permute-start | bytes 2064392 | tf_op jit(solution)/shard_map/ppermute | solution.py:875
  49.8 16.5 %collective-permute-start.14 = (bf16[2,448,384]{2,1,0:T(8,128)(2,1)S(1)}, bf16[2,448,384]{2,1,0:T(8,128)(2,1)S(1)}, u32[]{:S(2)}, u32[]{:S(2)}) collective-permute-start(bf16[2,448,384]{2,1,0:T(8,128)(2,1)S(1)} %pad_maximum_fusion.rest_0_), channel_id=1, source_target_pairs={{0,2},{1,3},{2,0},{3,1},{4,6},{5,7},{6,4},{7,5},{8,10},{9,11},{10,... | collective-permute-start | bytes 2064392 | tf_op jit(solution)/shard_map/ppermute | solution.py:875
  50.4 15.8 %collective-permute-start.16 = (bf16[448,384]{1,0:T(8,128)(2,1)S(1)}, bf16[448,384]{1,0:T(8,128)(2,1)S(1)}, u32[]{:S(2)}, u32[]{:S(2)}) collective-permute-start(bf16[448,384]{1,0:T(8,128)(2,1)S(1)} %copy-done.4), channel_id=1, source_target_pairs={{0,8},{1,9},{2,10},{3,11},{4,12},{5,13},{6,14},{7,15},{8,0},{9,1},... | collective-permute-start | bytes 1032200 | tf_op jit(solution)/shard_map/ppermute | solution.py:882
  66.3 14.9 %collective-permute-start.18 = (bf16[2,448,384]{2,1,0:T(8,128)(2,1)S(1)}, bf16[2,448,384]{2,1,0:T(8,128)(2,1)S(1)}, u32[]{:S(2)}, u32[]{:S(2)}) collective-permute-start(bf16[2,448,384]{2,1,0:T(8,128)(2,1)S(1)} %pad_maximum_fusion.1.rest_1_), channel_id=1, source_target_pairs={{0,16},{1,17},{2,18},{3,19},{4,20},{5,21},{6,22},{7,23},{8,24},{9,... | collective-permute-start | bytes 2064392 | tf_op jit(solution)/shard_map/ppermute | solution.py:875
  68.3 13.9 %collective-permute-start.17 = (bf16[2,448,384]{2,1,0:T(8,128)(2,1)S(1)}, bf16[2,448,384]{2,1,0:T(8,128)(2,1)S(1)}, u32[]{:S(2)}, u32[]{:S(2)}) collective-permute-start(bf16[2,448,384]{2,1,0:T(8,128)(2,1)S(1)} %pad_maximum_fusion.1.rest_1_), channel_id=1, source_target_pairs={{0,2},{1,3},{2,0},{3,1},{4,6},{5,7},{6,4},{7,5},{8,10},{9,11},{10,... | collective-permute-start | bytes 2064392 | tf_op jit(solution)/shard_map/ppermute | solution.py:875
  70.3 13.0 %collective-permute-start.21 = (bf16[2,448,384]{2,1,0:T(8,128)(2,1)S(1)}, bf16[2,448,384]{2,1,0:T(8,128)(2,1)S(1)}, u32[]{:S(2)}, u32[]{:S(2)}) collective-permute-start(bf16[2,448,384]{2,1,0:T(8,128)(2,1)S(1)} %pad_maximum_fusion.rest_0_), channel_id=1, source_target_pairs={{0,1},{1,0},{2,3},{3,2},{4,5},{5,4},{6,7},{7,6},{8,9},{9,8},{10,11... | collective-permute-start | bytes 2064392 | tf_op jit(solution)/shard_map/ppermute | solution.py:875
  70.3 13.1 %collective-permute-start.22 = (bf16[2,448,384]{2,1,0:T(8,128)(2,1)S(1)}, bf16[2,448,384]{2,1,0:T(8,128)(2,1)}, u32[]{:S(2)}, u32[]{:S(2)}) collective-permute-start(bf16[2,448,384]{2,1,0:T(8,128)(2,1)S(1)} %pad_maximum_fusion.1.rest_1_), channel_id=1, source_target_pairs={{0,1},{1,0},{2,3},{3,2},{4,5},{5,4},{6,7},{7,6},{8,9},{9,8},{10,11... | collective-permute-start | bytes 2064392 | tf_op jit(solution)/shard_map/ppermute | solution.py:875
  70.8 13.1 %collective-permute-start.25 = (bf16[2,448,384]{2,1,0:T(8,128)(2,1)S(1)}, bf16[2,448,384]{2,1,0:T(8,128)(2,1)}, u32[]{:S(2)}, u32[]{:S(2)}) collective-permute-start(bf16[2,448,384]{2,1,0:T(8,128)(2,1)S(1)} %collective-permute-done.15.rest_4_), channel_id=1, source_target_pairs={{0,1},{1,0},{2,3},{3,2},{4,5},{5,4},{6,7},{7,6},{8,9},{9,8},{10,11... | collective-permute-start | bytes 2064392 | tf_op jit(solution)/shard_map/ppermute | solution.py:875
  81.3 17.9 %collective-permute-start.19 = (bf16[2,448,384]{2,1,0:T(8,128)(2,1)S(1)}, bf16[2,448,384]{2,1,0:T(8,128)(2,1)S(1)}, u32[]{:S(2)}, u32[]{:S(2)}) collective-permute-start(bf16[2,448,384]{2,1,0:T(8,128)(2,1)S(1)} %collective-permute-done.14.rest_2_), channel_id=1, source_target_pairs={{0,16},{1,17},{2,18},{3,19},{4,20},{5,21},{6,22},{7,23},{8,24},{9,... | collective-permute-start | bytes 2064392 | tf_op jit(solution)/shard_map/ppermute | solution.py:875
  82.2 17.1 %collective-permute-start.20 = (bf16[2,448,384]{2,1,0:T(8,128)(2,1)S(1)}, bf16[2,448,384]{2,1,0:T(8,128)(2,1)S(1)}, u32[]{:S(2)}, u32[]{:S(2)}) collective-permute-start(bf16[2,448,384]{2,1,0:T(8,128)(2,1)S(1)} %collective-permute-done.18.rest_5_), channel_id=1, source_target_pairs={{0,2},{1,3},{2,0},{3,1},{4,6},{5,7},{6,4},{7,5},{8,10},{9,11},{10,... | collective-permute-start | bytes 2064392 | tf_op jit(solution)/shard_map/ppermute | solution.py:875
  83.3 16.4 %collective-permute-start.23 = (bf16[2,448,384]{2,1,0:T(8,128)(2,1)S(1)}, bf16[2,448,384]{2,1,0:T(8,128)(2,1)S(1)}, u32[]{:S(2)}, u32[]{:S(2)}) collective-permute-start(bf16[2,448,384]{2,1,0:T(8,128)(2,1)S(1)} %collective-permute-done.14.rest_2_), channel_id=1, source_target_pairs={{0,1},{1,0},{2,3},{3,2},{4,5},{5,4},{6,7},{7,6},{8,9},{9,8},{10,11... | collective-permute-start | bytes 2064392 | tf_op jit(solution)/shard_map/ppermute | solution.py:875
  83.4 16.4 %collective-permute-start.26 = (bf16[2,448,384]{2,1,0:T(8,128)(2,1)S(1)}, bf16[2,448,384]{2,1,0:T(8,128)(2,1)S(1)}, u32[]{:S(2)}, u32[]{:S(2)}) collective-permute-start(bf16[2,448,384]{2,1,0:T(8,128)(2,1)S(1)} %collective-permute-done.18.rest_5_), channel_id=1, source_target_pairs={{0,1},{1,0},{2,3},{3,2},{4,5},{5,4},{6,7},{7,6},{8,9},{9,8},{10,11... | collective-permute-start | bytes 2064392 | tf_op jit(solution)/shard_map/ppermute | solution.py:875
  83.9 15.9 %collective-permute-start.24 = (bf16[2,448,384]{2,1,0:T(8,128)(2,1)S(1)}, bf16[2,448,384]{2,1,0:T(8,128)(2,1)S(1)}, u32[]{:S(2)}, u32[]{:S(2)}) collective-permute-start(bf16[2,448,384]{2,1,0:T(8,128)(2,1)S(1)} %collective-permute-done.17.rest_3_), channel_id=1, source_target_pairs={{0,1},{1,0},{2,3},{3,2},{4,5},{5,4},{6,7},{7,6},{8,9},{9,8},{10,11... | collective-permute-start | bytes 2064392 | tf_op jit(solution)/shard_map/ppermute | solution.py:875
  196.1 16.0 %collective-permute-start.29 = (bf16[2,2,4,256,384]{4,3,2,1,0:T(8,128)(2,1)}, bf16[2,2,4,256,384]{4,3,2,1,0:T(8,128)(2,1)}, u32[]{:S(2)}, u32[]{:S(2)}) collective-permute-start(bf16[2,2,4,256,384]{4,3,2,1,0:T(8,128)(2,1)} %get-tuple-element.211), channel_id=1, source_target_pairs={{0,1},{1,0},{2,3},{3,2},{4,5},{5,4},{6,7},{7,6},{8,9},{9,8},{10,11... | collective-permute-start | bytes 9437192 | tf_op jit(solution)/shard_map/ppermute | solution.py:875
  216.6 20.3 %collective-permute-start.32 = (bf16[2,2,4,192,384]{4,3,2,1,0:T(8,128)(2,1)}, bf16[2,2,4,192,384]{4,3,2,1,0:T(8,128)(2,1)}, u32[]{:S(2)}, u32[]{:S(2)}) collective-permute-start(bf16[2,2,4,192,384]{4,3,2,1,0:T(8,128)(2,1)} %get-tuple-element.221), channel_id=1, source_target_pairs={{0,1},{1,0},{2,3},{3,2},{4,5},{5,4},{6,7},{7,6},{8,9},{9,8},{10,11... | collective-permute-start | bytes 7077896 | tf_op jit(solution)/shard_map/ppermute | solution.py:875
  217.0 19.9 %collective-permute-start.30 = (bf16[2,2,256,384]{3,2,1,0:T(8,128)(2,1)}, bf16[2,2,256,384]{3,2,1,0:T(8,128)(2,1)}, u32[]{:S(2)}, u32[]{:S(2)}) collective-permute-start(bf16[2,2,256,384]{3,2,1,0:T(8,128)(2,1)} %fusion), channel_id=1, source_target_pairs={{0,2},{1,3},{2,0},{3,1},{4,6},{5,7},{6,4},{7,5},{8,10},{9,11},{10,... | collective-permute-start | bytes 2359304 | tf_op jit(solution)/shard_map/ppermute | solution.py:875
  217.0 19.9 %collective-permute-start.31 = (bf16[2,2,256,384]{3,2,1,0:T(8,128)(2,1)}, bf16[2,2,256,384]{3,2,1,0:T(8,128)(2,1)}, u32[]{:S(2)}, u32[]{:S(2)}) collective-permute-start(bf16[2,2,256,384]{3,2,1,0:T(8,128)(2,1)} %fusion.1), channel_id=1, source_target_pairs={{0,16},{1,17},{2,18},{3,19},{4,20},{5,21},{6,22},{7,23},{8,24},{9,... | collective-permute-start | bytes 2359304 | tf_op jit(solution)/shard_map/ppermute | solution.py:875
  242.6 17.9 %collective-permute-start.33 = (bf16[2,256,384]{2,1,0:T(8,128)(2,1)S(1)}, bf16[2,256,384]{2,1,0:T(8,128)(2,1)S(1)}, u32[]{:S(2)}, u32[]{:S(2)}) collective-permute-start(bf16[2,256,384]{2,1,0:T(8,128)(2,1)S(1)} %get-tuple-element.231), channel_id=1, source_target_pairs={{0,16},{1,17},{2,18},{3,19},{4,20},{5,21},{6,22},{7,23},{8,24},{9,... | collective-permute-start | bytes 1179656 | tf_op jit(solution)/shard_map/ppermute | solution.py:875
  243.4 17.1 %collective-permute-start.34 = (bf16[2,256,384]{2,1,0:T(8,128)(2,1)S(1)}, bf16[2,256,384]{2,1,0:T(8,128)(2,1)}, u32[]{:S(2)}, u32[]{:S(2)}) collective-permute-start(bf16[2,256,384]{2,1,0:T(8,128)(2,1)S(1)} %get-tuple-element.232), channel_id=1, source_target_pairs={{0,2},{1,3},{2,0},{3,1},{4,6},{5,7},{6,4},{7,5},{8,10},{9,11},{10,... | collective-permute-start | bytes 1179656 | tf_op jit(solution)/shard_map/ppermute | solution.py:875
  245.1 20.9 %collective-permute-start.35 = (bf16[2,2,192,384]{3,2,1,0:T(8,128)(2,1)}, bf16[2,2,192,384]{3,2,1,0:T(8,128)(2,1)S(1)}, u32[]{:S(2)}, u32[]{:S(2)}) collective-permute-start(bf16[2,2,192,384]{3,2,1,0:T(8,128)(2,1)} %fusion.7), channel_id=1, source_target_pairs={{0,2},{1,3},{2,0},{3,1},{4,6},{5,7},{6,4},{7,5},{8,10},{9,11},{10,... | collective-permute-start | bytes 1769480 | tf_op jit(solution)/shard_map/ppermute | solution.py:875
  245.4 20.7 %collective-permute-start.36 = (bf16[2,2,192,384]{3,2,1,0:T(8,128)(2,1)}, bf16[2,2,192,384]{3,2,1,0:T(8,128)(2,1)S(1)}, u32[]{:S(2)}, u32[]{:S(2)}) collective-permute-start(bf16[2,2,192,384]{3,2,1,0:T(8,128)(2,1)} %fusion.8), channel_id=1, source_target_pairs={{0,16},{1,17},{2,18},{3,19},{4,20},{5,21},{6,22},{7,23},{8,24},{9,... | collective-permute-start | bytes 1769480 | tf_op jit(solution)/shard_map/ppermute | solution.py:875
  270.2 13.9 %collective-permute-start.41 = (bf16[2,2,4,160,384]{4,3,2,1,0:T(8,128)(2,1)}, bf16[2,2,4,160,384]{4,3,2,1,0:T(8,128)(2,1)}, u32[]{:S(2)}, u32[]{:S(2)}) collective-permute-start(bf16[2,2,4,160,384]{4,3,2,1,0:T(8,128)(2,1)} %get-tuple-element.249), channel_id=1, source_target_pairs={{0,1},{1,0},{2,3},{3,2},{4,5},{5,4},{6,7},{7,6},{8,9},{9,8},{10,11... | collective-permute-start | bytes 5898248 | tf_op jit(solution)/shard_map/ppermute | solution.py:875
  270.2 13.8 %collective-permute-start.37 = (bf16[2,192,384]{2,1,0:T(8,128)(2,1)S(1)}, bf16[2,192,384]{2,1,0:T(8,128)(2,1)S(1)}, u32[]{:S(2)}, u32[]{:S(2)}) collective-permute-start(bf16[2,192,384]{2,1,0:T(8,128)(2,1)S(1)} %get-tuple-element.245), channel_id=1, source_target_pairs={{0,16},{1,17},{2,18},{3,19},{4,20},{5,21},{6,22},{7,23},{8,24},{9,... | collective-permute-start | bytes 884744 | tf_op jit(solution)/shard_map/ppermute | solution.py:875
  271.6 12.4 %collective-permute-start.38 = (bf16[2,192,384]{2,1,0:T(8,128)(2,1)S(1)}, bf16[2,192,384]{2,1,0:T(8,128)(2,1)S(1)}, u32[]{:S(2)}, u32[]{:S(2)}) collective-permute-start(bf16[2,192,384]{2,1,0:T(8,128)(2,1)S(1)} %get-tuple-element.246), channel_id=1, source_target_pairs={{0,2},{1,3},{2,0},{3,1},{4,6},{5,7},{6,4},{7,5},{8,10},{9,11},{10,... | collective-permute-start | bytes 884744 | tf_op jit(solution)/shard_map/ppermute | solution.py:875
  273.0 11.0 %collective-permute-start.39 = (bf16[256,384]{1,0:T(8,128)(2,1)S(1)}, bf16[256,384]{1,0:T(8,128)(2,1)}, u32[]{:S(2)}, u32[]{:S(2)}) collective-permute-start(bf16[256,384]{1,0:T(8,128)(2,1)S(1)} %get-tuple-element.247), channel_id=1, source_target_pairs={{0,12},{1,13},{2,14},{3,15},{4,0},{5,1},{6,2},{7,3},{8,4},{9,5},{1... | collective-permute-start | bytes 589832 | tf_op jit(solution)/shard_map/ppermute | solution.py:882
  273.0 11.0 %collective-permute-start.40 = (bf16[256,384]{1,0:T(8,128)(2,1)S(1)}, bf16[256,384]{1,0:T(8,128)(2,1)}, u32[]{:S(2)}, u32[]{:S(2)}) collective-permute-start(bf16[256,384]{1,0:T(8,128)(2,1)S(1)} %get-tuple-element.248), channel_id=1, source_target_pairs={{0,4},{1,5},{2,6},{3,7},{4,8},{5,9},{6,10},{7,11},{8,12},{9,13},{1... | collective-permute-start | bytes 589832 | tf_op jit(solution)/shard_map/ppermute | solution.py:882
  290.3 11.8 %collective-permute-start.42 = (bf16[2,2,160,384]{3,2,1,0:T(8,128)(2,1)}, bf16[2,2,160,384]{3,2,1,0:T(8,128)(2,1)S(1)}, u32[]{:S(2)}, u32[]{:S(2)}) collective-permute-start(bf16[2,2,160,384]{3,2,1,0:T(8,128)(2,1)} %fusion.14), channel_id=1, source_target_pairs={{0,2},{1,3},{2,0},{3,1},{4,6},{5,7},{6,4},{7,5},{8,10},{9,11},{10,... | collective-permute-start | bytes 1474568 | tf_op jit(solution)/shard_map/ppermute | solution.py:875
  290.9 11.5 %collective-permute-start.43 = (bf16[2,2,160,384]{3,2,1,0:T(8,128)(2,1)S(1)}, bf16[2,2,160,384]{3,2,1,0:T(8,128)(2,1)}, u32[]{:S(2)}, u32[]{:S(2)}) collective-permute-start(bf16[2,2,160,384]{3,2,1,0:T(8,128)(2,1)S(1)} %fusion.15), channel_id=1, source_target_pairs={{0,16},{1,17},{2,18},{3,19},{4,20},{5,21},{6,22},{7,23},{8,24},{9,... | collective-permute-start | bytes 1474568 | tf_op jit(solution)/shard_map/ppermute | solution.py:875
  291.7 10.0 %collective-permute-start.44 = (bf16[256,384]{1,0:T(8,128)(2,1)S(1)}, bf16[256,384]{1,0:T(8,128)(2,1)S(1)}, u32[]{:S(2)}, u32[]{:S(2)}) collective-permute-start(bf16[256,384]{1,0:T(8,128)(2,1)S(1)} %copy-done.9), channel_id=1, source_target_pairs={{0,8},{1,9},{2,10},{3,11},{4,12},{5,13},{6,14},{7,15},{8,0},{9,1},... | collective-permute-start | bytes 589832 | tf_op jit(solution)/shard_map/ppermute | solution.py:882
  303.8 13.9 %collective-permute-start.45 = (bf16[2,160,384]{2,1,0:T(8,128)(2,1)S(1)}, bf16[2,160,384]{2,1,0:T(8,128)(2,1)S(1)}, u32[]{:S(2)}, u32[]{:S(2)}) collective-permute-start(bf16[2,160,384]{2,1,0:T(8,128)(2,1)S(1)} %get-tuple-element.266), channel_id=1, source_target_pairs={{0,16},{1,17},{2,18},{3,19},{4,20},{5,21},{6,22},{7,23},{8,24},{9,... | collective-permute-start | bytes 737288 | tf_op jit(solution)/shard_map/ppermute | solution.py:875
  304.6 13.1 %collective-permute-start.46 = (bf16[2,160,384]{2,1,0:T(8,128)(2,1)S(1)}, bf16[2,160,384]{2,1,0:T(8,128)(2,1)}, u32[]{:S(2)}, u32[]{:S(2)}) collective-permute-start(bf16[2,160,384]{2,1,0:T(8,128)(2,1)S(1)} %get-tuple-element.267), channel_id=1, source_target_pairs={{0,2},{1,3},{2,0},{3,1},{4,6},{5,7},{6,4},{7,5},{8,10},{9,11},{10,... | collective-permute-start | bytes 737288 | tf_op jit(solution)/shard_map/ppermute | solution.py:875
  307.1 13.5 %collective-permute-start.50 = (bf16[192,384]{1,0:T(8,128)(2,1)}, bf16[192,384]{1,0:T(8,128)(2,1)S(1)}, u32[]{:S(2)}, u32[]{:S(2)}) collective-permute-start(bf16[192,384]{1,0:T(8,128)(2,1)} %fusion.31), channel_id=1, source_target_pairs={{0,12},{1,13},{2,14},{3,15},{4,0},{5,1},{6,2},{7,3},{8,4},{9,5},{1... | collective-permute-start | bytes 442376 | tf_op jit(solution)/shard_map/ppermute | solution.py:882
  308.9 13.0 %collective-permute-start.51 = (bf16[192,384]{1,0:T(8,128)(2,1)}, bf16[192,384]{1,0:T(8,128)(2,1)S(1)}, u32[]{:S(2)}, u32[]{:S(2)}) collective-permute-start(bf16[192,384]{1,0:T(8,128)(2,1)} %get-tuple-element.279), channel_id=1, source_target_pairs={{0,8},{1,9},{2,10},{3,11},{4,12},{5,13},{6,14},{7,15},{8,0},{9,1},... | collective-permute-start | bytes 442376 | tf_op jit(solution)/shard_map/ppermute | solution.py:882
  309.9 12.0 %collective-permute-start.52 = (bf16[192,384]{1,0:T(8,128)(2,1)}, bf16[192,384]{1,0:T(8,128)(2,1)S(1)}, u32[]{:S(2)}, u32[]{:S(2)}) collective-permute-start(bf16[192,384]{1,0:T(8,128)(2,1)} %get-tuple-element.280), channel_id=1, source_target_pairs={{0,4},{1,5},{2,6},{3,7},{4,8},{5,9},{6,10},{7,11},{8,12},{9,13},{1... | collective-permute-start | bytes 442376 | tf_op jit(solution)/shard_map/ppermute | solution.py:882
  322.6 11.1 %collective-permute-start.48 = (bf16[160,384]{1,0:T(8,128)(2,1)S(1)}, bf16[160,384]{1,0:T(8,128)(2,1)S(1)}, u32[]{:S(2)}, u32[]{:S(2)}) collective-permute-start(bf16[160,384]{1,0:T(8,128)(2,1)S(1)} %get-tuple-element.276), channel_id=1, source_target_pairs={{0,8},{1,9},{2,10},{3,11},{4,12},{5,13},{6,14},{7,15},{8,0},{9,1},... | collective-permute-start | bytes 368648 | tf_op jit(solution)/shard_map/ppermute | solution.py:882
  323.2 10.5 %collective-permute-start.49 = (bf16[160,384]{1,0:T(8,128)(2,1)S(1)}, bf16[160,384]{1,0:T(8,128)(2,1)S(1)}, u32[]{:S(2)}, u32[]{:S(2)}) collective-permute-start(bf16[160,384]{1,0:T(8,128)(2,1)S(1)} %get-tuple-element.277), channel_id=1, source_target_pairs={{0,4},{1,5},{2,6},{3,7},{4,8},{5,9},{6,10},{7,11},{8,12},{9,13},{1... | collective-permute-start | bytes 368648 | tf_op jit(solution)/shard_map/ppermute | solution.py:882
  333.9 6.4 %collective-permute-start.54 = (bf16[336,384]{1,0:T(8,128)(2,1)S(1)}, bf16[336,384]{1,0:T(8,128)(2,1)S(1)}, u32[]{:S(2)}, u32[]{:S(2)}) collective-permute-start(bf16[336,384]{1,0:T(8,128)(2,1)S(1)} %pad_maximum_fusion.4), channel_id=1, source_target_pairs={{0,16},{1,17},{2,18},{3,19},{4,20},{5,21},{6,22},{7,23},{8,24},{9,... | collective-permute-start | bytes 774152 | tf_op jit(solution)/shard_map/ppermute | solution.py:875
  (39 other events, 394.0 us)
